TPU v7x, 128 devices: a whole 4x4x4 slice. The times are simulated.
128 devices in a mesh: lat: 8 (over y_lo, x), lon: 16 (over z, y_hi, core).
Axes of the slice: x: 4, y: 4 (y_hi: 2, y_lo: 2; y = y_hi * 2 + y_lo), z: 4, core: 2. Of those that a mesh axis runs over, the one named last changes fastest.
Arguments:
- grad_out: bfloat16 [1, 720, 128, 1440], P(None, 'lat', None, 'lon'), may hold values from -6 to 6
- spectrum: bfloat16 [640, 720, 1, 2, 128], P('lon', 'lat'), may hold values from -0.8984375 to 0.8984375
- weights: bfloat16 [720, 128, 128], P('lat'), may hold values from -0.5 to 0.5
Outputs:
- grad_in: bfloat16 [1, 720, 128, 1440], P(None, 'lat', None, 'lon')
- weight_grad: float32 [720, 128, 128], P('lat', 'lon')
All inputs are finite; a program needn't handle non-finite values.
Results may differ from a plain program's by a relative error of at most 0.015.
Values may be sent and summed in bfloat16 or wider, within the bound.
No kernel may reach another device: no remote copies, remote signals or barrier semaphores. Data moves between devices by JAX's collectives and lax.ppermute only.
A program may use at most 128 MiB of HBM per device.

v0:
```python
import math

import jax
import jax.numpy as jnp
from jax import lax
from jax.sharding import PartitionSpec as P

LAT = 720
LON = 1440
L = 720
M = 640


def fourier_table(point_count, mode_count):
    positions = jnp.arange(point_count, dtype=jnp.int32)[:, None]
    mode_index = jnp.arange(mode_count, dtype=jnp.int32)[None, :]
    phase_index = positions * mode_index % point_count
    angles = phase_index.astype(jnp.float32) * (2.0 * math.pi / point_count)
    factor = 1.0 / math.sqrt(point_count)
    stacked = jnp.stack([jnp.cos(angles) * factor, -jnp.sin(angles) * factor], axis=-1)
    return stacked.reshape(point_count, 2 * mode_count).astype(jnp.bfloat16)


def block_steps(degrees):
    step_count = -(-degrees // 30)
    while degrees % step_count != 0:
        step_count = step_count + 1
    return step_count


def legendre_table(orders, degrees, lat_count):
    colatitude = (jnp.arange(lat_count, dtype=jnp.float32) + 0.5) * (math.pi / lat_count)
    cosine = jnp.cos(colatitude)[None, :]
    sines = jnp.sin(colatitude)[None, :]
    root_weight = jnp.sqrt(sines * (math.pi / lat_count))
    order_val = orders.astype(jnp.float32)[:, None]
    order_col = orders[:, None]
    log_seed = (
        0.5 * jnp.log(order_val + 0.5)
        + 0.5 * lax.lgamma(2.0 * order_val + 1.0)
        - lax.lgamma(order_val + 1.0)
        - order_val * math.log(2.0)
        + order_val * jnp.log(sines)
    )
    step_count = block_steps(degrees)

    def advance(carried, start_deg):
        current, previous, log_scale = carried
        outputs = []
        for offset in range(step_count):
            degree = start_deg + offset
            degree_val = degree.astype(jnp.float32)
            past_start = degree > order_col
            at_start = degree == order_col
            divisor = jnp.where(past_start, degree_val * degree_val - order_val * order_val, 1.0)
            coeff_up = jnp.sqrt(jnp.maximum((4.0 * degree_val * degree_val - 1.0) / divisor, 0.0))
            lower_term = (degree_val - 1.0) * (degree_val - 1.0) - order_val * order_val
            coeff_back = jnp.sqrt(
                jnp.maximum(
                    lower_term * (2.0 * degree_val + 1.0) / ((2.0 * degree_val - 3.0) * divisor),
                    0.0,
                )
            )
            advanced = coeff_up * cosine * current - coeff_back * previous
            magnitude = jnp.where(past_start, jnp.maximum(jnp.abs(advanced), jnp.abs(current)), 1.0)
            previous = jnp.where(past_start, current / magnitude, 0.0)
            log_scale = jnp.where(
                at_start, log_seed, jnp.where(past_start, log_scale + jnp.log(magnitude), 0.0)
            )
            current = jnp.where(at_start, 1.0, jnp.where(past_start, advanced / magnitude, 0.0))
            outputs.append(current * jnp.exp(log_scale) * root_weight)
        return ((current, previous, log_scale), jnp.stack(outputs))

    initial = jnp.zeros((orders.shape[0], lat_count), jnp.float32)
    starts = jnp.arange(degrees // step_count, dtype=jnp.int32) * step_count
    _, blocks = lax.scan(advance, (initial, initial, initial), starts)
    return blocks.reshape(degrees, orders.shape[0], lat_count)


def on_device(grad_out, spectrum, weights):
    batch_size, lat_rows, channels, lon_cols = grad_out.shape
    lon_count = lax.axis_size("lon")
    lat_count = lax.axis_size("lat")
    per_device = spectrum.shape[0] // lat_count
    fourier = fourier_table(LON, M)
    spectra = jnp.einsum(
        "bicn,nq->bicq",
        lax.all_to_all(grad_out, "lon", split_axis=2, concat_axis=3, tiled=True),
        fourier,
        preferred_element_type=jnp.float32,
    ).astype(jnp.bfloat16)
    spectra = spectra.reshape(
        batch_size, lat_rows, channels // lon_count, lon_count, lat_count, 2 * per_device
    )
    columns = lax.all_to_all(
        lax.all_to_all(spectra, "lat", split_axis=4, concat_axis=1, tiled=True),
        "lon",
        split_axis=3,
        concat_axis=2,
        tiled=True,
    )
    columns = columns.reshape(batch_size, LAT, channels, per_device, 2)
    first_order = (lax.axis_index("lon") * lat_count + lax.axis_index("lat")) * per_device
    orders = first_order + jnp.arange(per_device, dtype=jnp.int32)
    legendre = legendre_table(orders, L, LAT).astype(jnp.bfloat16)
    analysed = jnp.einsum(
        "lst,btcsp->slbpc", legendre, columns, preferred_element_type=jnp.float32
    ).astype(jnp.bfloat16)
    gathered = lax.all_to_all(analysed, "lat", split_axis=1, concat_axis=0, tiled=True)
    partial_value = jnp.einsum(
        "slbpc,slbpd->lcd", spectrum, gathered, preferred_element_type=jnp.float32
    )
    summed = lax.psum(partial_value.astype(jnp.bfloat16), "lon").astype(jnp.float32)
    col_share = channels // lon_count
    weight_grad = lax.dynamic_slice_in_dim(summed, lax.axis_index("lon") * col_share, col_share, 1)
    spec_local = jnp.einsum(
        "lcd,slbpd->slbpc", weights, gathered, preferred_element_type=jnp.float32
    ).astype(jnp.bfloat16)
    spec_grad = lax.all_to_all(spec_local, "lat", split_axis=0, concat_axis=1, tiled=True)
    col_grad = jnp.einsum(
        "lst,slbpc->btcsp", legendre, spec_grad, preferred_element_type=jnp.float32
    ).astype(jnp.bfloat16)
    col_grad = col_grad.reshape(batch_size, LAT, channels, 1, 1, 2 * per_device)
    row_block = lax.all_to_all(
        lax.all_to_all(col_grad, "lat", split_axis=1, concat_axis=4, tiled=True),
        "lon",
        split_axis=2,
        concat_axis=3,
        tiled=True,
    )
    row_block = row_block.reshape(batch_size, lat_rows, channels // lon_count, 2 * M)
    grid_part = jnp.einsum(
        "bicq,nq->bicn", row_block, fourier, preferred_element_type=jnp.float32
    ).astype(jnp.bfloat16)
    grad_in = lax.all_to_all(grid_part, "lon", split_axis=3, concat_axis=2, tiled=True)
    return (grad_in, weight_grad)


def solution(mesh):
    in_specs = (
        P(None, "lat", None, "lon"),
        P("lon", "lat", None, None, None),
        P("lat", None, None),
    )
    out_specs = (P(None, "lat", None, "lon"), P("lat", "lon", None))
    return jax.shard_map(
        on_device, mesh=mesh, in_specs=in_specs, out_specs=out_specs, check_vma=False
    )
```

profile of v0, /device:TPU:0, one launch (start us, length us, event | category | flops | bytes accessed | tf_op | source)
XLA Modules:
  0.0 1223.8 jit_solution(18351164770912650509)
XLA Ops:
  7.2 4.9 copy.103
  12.1 8.2 all-to-all-start
  20.3 16.0 %multiply_convert_fusion = (bf16[1440,640,1]{1,0,2:T(8,128)(2,1)S(1)}, bf16[1440,640,1]{1,0,2:T(8,128)(2,1)S(1)}) fusion(), kind=kLoop, calls=%fused_computation.289 | loop fusion | flops 12902400 | bytes 3686400 | tf_op jit(solution)/shard_map/convert.1
  36.3 2.3 pad_maximum_fusion
  38.6 10.7 copy.102
  49.3 9.0 convert_element_type.272
  58.3 2.6 all-to-all-done
  60.9 3.0 copy.165
  63.9 1.9 copy.143
  65.9 5.7 reshape.1946
  71.6 7.4 fusion.51
  79.0 4.6 copy.108
  83.5 3.4 copy.109
  86.9 4.9 all-to-all-start.1
  92.1 32.3 %all-to-all-done.1 = bf16[1,90,8,16,8,10]{1,2,5,3,0,4:T(8,128)(2,1)} async-done(((bf16[1,90,8,16,8,10]{1,2,5,3,0,4:T(8,128)(2,1)}), bf16[1,90,8,16,8,10]{1,2,5,3,0,4:T(8,128)(2,1)}, u32[]{:S(2)}, u32[]{:S(2)}) %all-to-all-start.1) | async-done | bytes 1843232 | tf_op jit(solution)/shard_map/all_to_all | solution.py:96
  124.3 6.3 copy.144
  130.6 5.3 reshape.1947
  135.9 5.7 all-to-all-start.2
  141.5 743.1 %while.23 = (s32[]{:T(128)}, f32[5,720]{1,0:T(8,128)S(1)}, f32[5,720]{1,0:T(8,128)S(1)}, f32[5,720]{1,0:T(8,128)S(1)}, bf16[30,24,5,720]{3,2,1,0:T(8,128)(2,1)},...) while((s32[]{:T(128)}, f32[5,720]{1,0:T(8,128)S(1)}, ...), condition=%wide.region_1.2_spmd.clone.clone.clone.clone, body=%wide.region_0.1_spmd.clone.clone.clone.clone.sunk | while | flops 2781690 | bytes 4729721 | solution.py:76
  165.6 0.7 bitcast_dynamic-update-slice_fusion.2
  215.1 0.8 bitcast_dynamic-update-slice_fusion.2
  264.6 0.7 bitcast_dynamic-update-slice_fusion.2
  289.4 0.8 bitcast_dynamic-update-slice_fusion.2
  462.7 0.8 bitcast_dynamic-update-slice_fusion.2
  487.5 0.8 bitcast_dynamic-update-slice_fusion.2
  512.3 0.8 bitcast_dynamic-update-slice_fusion.2
  611.4 0.7 bitcast_dynamic-update-slice_fusion.2
  636.1 0.7 bitcast_dynamic-update-slice_fusion.2
  660.9 0.8 bitcast_dynamic-update-slice_fusion.2
  710.4 0.7 bitcast_dynamic-update-slice_fusion.2
  735.2 0.8 bitcast_dynamic-update-slice_fusion.2
  760.0 0.8 bitcast_dynamic-update-slice_fusion.2
  809.6 0.8 bitcast_dynamic-update-slice_fusion.2
  834.4 0.8 bitcast_dynamic-update-slice_fusion.2
  883.9 0.7 bitcast_dynamic-update-slice_fusion.2
  884.7 11.4 copy.139
  896.0 1.7 copy.112
  897.7 4.6 convert_bitcast_fusion.1
  902.3 1.4 copy.115
  903.8 34.5 %all_to_all.129 = bf16[5,720,1,2,128]{4,3,0,2,1:T(2,128)(2,1)S(1)} all-to-all(bf16[5,720,1,2,128]{4,3,0,2,1:T(2,128)(2,1)S(1)} %copy.115), channel_id=1, replica_groups=mesh['lat'=8,'lon'=16] {'lat'}, dimensions={1} | all-to-all | bytes 3686400 | tf_op jit(solution)/shard_map/all_to_all | solution.py:109
  938.3 1.3 copy.116
  939.6 1.3 copy.117
  940.9 1.2 copy-done.2
  942.1 2.2 convert_bitcast_fusion
  944.3 1.4 copy.119
  945.7 27.1 %all_to_all.130 = bf16[40,90,1,2,128]{4,3,1,2,0:T(2,128)(2,1)S(1)} all-to-all(bf16[40,90,1,2,128]{4,3,1,2,0:T(2,128)(2,1)S(1)} %copy.119), channel_id=1, replica_groups=mesh['lat'=8,'lon'=16] {'lat'}, dimensions={0} | all-to-all | bytes 3686400 | tf_op jit(solution)/shard_map/all_to_all | solution.py:119
  972.8 1.3 copy.120
  974.1 1.6 fusion.63
  976.4 37.7 %all_to_all.131 = bf16[1,720,128,1,1,10]{2,5,4,3,0,1:T(8,128)(2,1)S(1)} all-to-all(bf16[1,720,128,1,1,10]{2,5,4,3,0,1:T(8,128)(2,1)S(1)} %copy.123), channel_id=1, replica_groups=mesh['lat'=8,'lon'=16] {'lat'}, dimensions={1} | all-to-all | bytes 3686400 | tf_op jit(solution)/shard_map/all_to_all | solution.py:125
  1014.1 1.8 copy.166
  1015.9 4.5 copy.125
  1020.3 7.5 all-to-all-start.6
  1028.1 4.1 fusion.54
  1032.2 42.8 %all-to-all-done.6 = bf16[1,90,128,1,8,10]{1,4,5,3,0,2:T(8,128)(2,1)} async-done(((bf16[1,90,128,1,8,10]{1,4,5,3,0,2:T(8,128)(2,1)}), bf16[1,90,128,1,8,10]{1,4,5,3,0,2:T(8,128)(2,1)}, u32[]{:S(2)}, u32[]{:S(2)}) %all-to-all-start.6) | async-done | bytes 1843232 | tf_op jit(solution)/shard_map/all_to_all | solution.py:124
  1075.1 2.4 copy.126
  1077.5 3.8 copy.127
  1081.3 5.7 fusion.57
  1087.1 3.7 copy.129
  1090.8 5.3 all-to-all-start.7
  1096.1 99.0 %all-reduce.2.cloned.1.call-done = bf16[90,128,128]{1,2,0:T(8,128)(2,1)} async-done(((bf16[90,128,128]{1,2,0:T(8,128)(2,1)}), bf16[90,128,128]{1,2,0:T(8,128)(2,1)}) %all-reduce.2.cloned.1.call-update) | async-done | bytes 2949136 | tf_op jit(solution)/shard_map/psum | solution.py:113
  1195.2 5.4 dynamic-slice_convert_fusion
  1200.5 4.2 copy.134
  1204.8 7.5 copy.130
  1212.2 4.5 copy.133
  (2349 shorter events, 220.7 us)
Async XLA Ops:
  7.2 934.9 %copy-start = (bf16[90,128,128]{2,1,0:T(8,128)(2,1)S(1)}, bf16[90,128,128]{2,1,0:T(8,128)(2,1)}, u32[]{:S(2)}) copy-start(bf16[90,128,128]{2,1,0:T(8,128)(2,1)} %param.7) | copy-start | bytes 8847364
  12.1 48.8 %all-to-all-start = ((bf16[1,90,128,90]{3,1,0,2:T(8,128)(2,1)}), bf16[1,90,128,90]{3,1,0,2:T(8,128)(2,1)}, u32[]{:S(2)}, u32[]{:S(2)}) async-start(bf16[1,90,128,90]{3,1,0,2:T(8,128)(2,1)} %copy.103), calls=%async_computation | async-start | bytes 6291456 | tf_op jit(solution)/shard_map/all_to_all | solution.py:88
  86.9 37.4 %all-to-all-start.1 = ((bf16[1,90,8,16,8,10]{1,2,5,3,0,4:T(8,128)(2,1)}), bf16[1,90,8,16,8,10]{1,2,5,3,0,4:T(8,128)(2,1)}, u32[]{:S(2)}, u32[]{:S(2)}) async-start(bf16[1,90,8,16,8,10]{1,2,5,3,0,4:T(8,128)(2,1)} %copy.109), calls=%async_computation.1 | async-start | bytes 5242880 | tf_op jit(solution)/shard_map/all_to_all | solution.py:96
  135.9 760.2 %all-to-all-start.2 = ((bf16[1,720,8,16,1,10]{1,2,5,4,0,3:T(8,128)(2,1)}), bf16[1,720,8,16,1,10]{1,2,5,4,0,3:T(8,128)(2,1)}, u32[]{:S(2)}, u32[]{:S(2)}) async-start(bf16[1,720,8,16,1,10]{1,2,5,4,0,3:T(8,128)(2,1)} %reshape.1947), calls=%async_computation.2 | async-start | bytes 3932160 | tf_op jit(solution)/shard_map/all_to_all | solution.py:95
  940.9 1.2 copy-start.2
  942.1 31.9 %slice-start = ((s8[5529600]{0:T(1024)(128)(4,1)}), s8[4194304]{0:T(1024)(128)(4,1)S(1)}, s32[]{:S(2)}) async-start(s8[5529600]{0:T(1024)(128)(4,1)} %bitcast.730), calls=%async_computation.9 | async-start | bytes 8388608
  944.2 29.8 %slice-start.1 = ((s8[5529600]{0:T(1024)(128)(4,1)}), s8[1335296]{0:T(1024)(128)(4,1)S(1)}, s32[]{:S(2)}) async-start(s8[5529600]{0:T(1024)(128)(4,1)} %bitcast.730), calls=%async_computation.10 | async-start | bytes 2670592
  1020.3 7.8 copy-start.3
  1020.3 54.7 %all-to-all-start.6 = ((bf16[1,90,128,1,8,10]{1,4,5,3,0,2:T(8,128)(2,1)}), bf16[1,90,128,1,8,10]{1,4,5,3,0,2:T(8,128)(2,1)}, u32[]{:S(2)}, u32[]{:S(2)}) async-start(bf16[1,90,128,1,8,10]{1,4,5,3,0,2:T(8,128)(2,1)} %copy.125), calls=%async_computation.6 | async-start | bytes 5242880 | tf_op jit(solution)/shard_map/all_to_all | solution.py:124
  1027.9 167.3 %all-reduce.2.cloned.1.call-start = ((), (), s32[]{:S(2)}) async-start(), calls=%async_computation.8 | async-start | bytes 5898240 | tf_op jit(solution)/shard_map/psum | solution.py:113
  1090.8 114.0 %all-to-all-start.7 = ((bf16[1,90,8,1440]{1,2,0,3:T(8,128)(2,1)}), bf16[1,90,8,1440]{1,2,0,3:T(8,128)(2,1)}, u32[]{:S(2)}, u32[]{:S(2)}) async-start(bf16[1,90,8,1440]{1,2,0,3:T(8,128)(2,1)} %copy.129), calls=%async_computation.7 | async-start | bytes 5898240 | tf_op jit(solution)/shard_map/all_to_all | solution.py:135
  1204.8 12.0 copy-start.1
Sparse Core Ops, SparseCore 0:
  1032.4 162.7 all-reduce.1
where the time goes:
time: 1240 us; the launch traced here: 1220 us
  loops' own time  511 us (41%)
  other arithmetic  213 us (17%)
  waiting for transfers between devices  177 us (14%)
  local copies, waits for them, and re-layouts  151 us (12%)
  blocking collectives  99.3 us (8%)
  starting transfers between devices  31.9 us (3%)
  matrix products  25.6 us (2%)
  between operations  14.5 us (1%)
    another operation x1, loops' own time, legendre_table(): _, blocks = lax.scan(advance, (initial, initial, initial), starts)  511 us
    psum x1, waiting for transfers between devices, on_device(): lax.psum(partial_value.astype(jnp.bfloat16), 'lon').astype(jnp.float32)  99 us
    while x690, other arithmetic  94.7 us
    all_to_all x1, waiting for transfers between devices, on_device(): lax.all_to_all(lax.all_to_all(col_grad, 'lat', split_axis=1, concat_axis=...  42.8 us
    all_to_all x1, blocking collectives, on_device(): lax.all_to_all(col_grad, 'lat', split_axis=1, concat_axis=4, tiled=True)  37.7 us
    all_to_all x1, blocking collectives, on_device(): lax.all_to_all(analysed, 'lat', split_axis=1, concat_axis=0, tiled=True)  34.5 us
    all_to_all x1, waiting for transfers between devices, on_device(): lax.all_to_all(spectra, 'lat', split_axis=4, concat_axis=1, tiled=True)  32.3 us
    sqrt x570, other arithmetic, advance(): jnp.sqrt(jnp.maximum((4.0 * degree_val * degree_val - 1.0) / divisor, 0.0))  29.4 us
  transfers between devices with their start and end apart: 6, of which 4 were waited for; matrix products, arithmetic and copies ran while one was open for 25% of the time, Pallas kernels for 0%

commit v1 on v0

v1 whole, which is shorter than its diff:
```python
import math

import jax
import jax.numpy as jnp
import numpy as np
from jax import lax
from jax.experimental import pallas as pl
from jax.experimental.pallas import tpu as pltpu
from jax.sharding import PartitionSpec as P

LAT = 720
LON = 1440
L = 720
M = 640
C = 128
LATS = 8
LONS = 16
ROWS = LAT // LATS
COLS = LON // LONS
SLOT = 6
USED = ROWS // SLOT
PAD = 96
ORDERS = M // (LATS * LONS)
Q = 2 * ORDERS
DEGREES = L // LATS
BLOCK = 16
SHIFT = 40

F32 = jnp.float32
BF16 = jnp.bfloat16


def cosine_values(position, order, part):
    step = position * order + part * (LON // 4)
    turn = step - LON * jnp.floor(step * (1.0 / LON))
    fold = (LON // 4) - jnp.abs(turn - LON // 2)
    angle = fold * (2.0 * math.pi / LON)
    square = angle * angle
    series = -1.0 / 39916800.0
    for term in (1.0 / 362880.0, -1.0 / 5040.0, 1.0 / 120.0, -1.0 / 6.0, 1.0):
        series = series * square + term
    return -(angle * series) * (1.0 / math.sqrt(LON))


def fourier_tables():
    def line(shape, axis):
        at = lax.broadcasted_iota(jnp.int32, shape, axis)
        inner = at % PAD
        return (at // PAD * COLS + inner).astype(F32), (inner < COLS).astype(F32)

    def modes(shape, axis):
        at = lax.broadcasted_iota(jnp.int32, shape, axis)
        return (at // 2).astype(F32), (at % 2).astype(F32)

    wide = LONS * PAD
    position, live = line((1, wide), 1)
    order, part = modes((2 * M, 1), 0)
    forward = (cosine_values(position, order, part) * live).astype(BF16)
    position, live = line((wide, 1), 0)
    order, part = modes((1, 2 * M), 1)
    backward = (cosine_values(position, order, part) * live).astype(BF16)
    return forward, backward


def seed_constants():
    out = []
    for m in range(M):
        out.append(
            0.5 * math.log(m + 0.5)
            + 0.5 * math.lgamma(2.0 * m + 1.0)
            - math.lgamma(m + 1.0)
            - m * math.log(2.0)
        )
    return np.asarray(out, np.float32)


def legendre_kernel(up, back, start, seed, order, x_ref, root_ref, sine_ref, out, buf):
    x = x_ref[...]
    root = root_ref[...]
    base = [seed[k] + order[k] * sine_ref[...] for k in range(ORDERS)]
    zero = jnp.zeros_like(x)
    small = 2.0**-SHIFT
    unit = SHIFT * math.log(2.0)

    def block(step, carry):
        current, previous, count = (list(part) for part in carry)
        first = step * BLOCK
        factor = [None] * ORDERS
        for offset in range(BLOCK):
            if offset % 8 == 0:
                for k in range(ORDERS):
                    big = jnp.maximum(jnp.abs(current[k]), jnp.abs(previous[k])) > 1.0
                    scale = jnp.where(big, small, 1.0)
                    current[k] = current[k] * scale
                    previous[k] = previous[k] * scale
                    count[k] = count[k] + jnp.where(big, 1.0, 0.0)
                    factor[k] = jnp.exp(base[k] + unit * count[k]) * root
            for k in range(ORDERS):
                at = k * L + first + offset
                advanced = (up[at] * x) * current[k] - back[at] * previous[k] + start[at]
                previous[k] = current[k]
                current[k] = advanced
                buf[k, offset * 8 : offset * 8 + 8, :] = advanced * factor[k]
        for k in range(ORDERS):
            for row in range(6):
                low = buf[k, pl.ds(row, 8, stride=8), :]
                high = buf[k, pl.ds(64 + row, 8, stride=8), :]
                both = jnp.concatenate([low, high], axis=0).astype(BF16)
                width = min(128, LAT - row * 128)
                rows = pl.ds(pl.multiple_of(first, BLOCK), BLOCK)
                out[k, rows, row * 128 : row * 128 + width] = both[:, :width]
        return tuple(current), tuple(previous), tuple(count)

    none = (zero,) * ORDERS
    lax.fori_loop(0, L // BLOCK, block, (none, none, none))


def legendre_table(first_order):
    orders = first_order + jnp.arange(ORDERS, dtype=jnp.int32)
    order = orders.astype(F32)
    seed = lax.dynamic_slice(jnp.asarray(seed_constants()), (first_order,), (ORDERS,))
    slot = jnp.arange(1024, dtype=jnp.int32)
    live = slot < LAT
    slot = jnp.minimum(slot, LAT - 1)
    row = ROWS * (slot % (LATS * SLOT) // SLOT) + SLOT * (slot // (LATS * SLOT)) + slot % SLOT
    angle = (row.astype(F32) + 0.5) * (math.pi / LAT)
    sine = jnp.sin(angle)
    x = jnp.where(live, jnp.cos(angle), 0.0).reshape(8, 128)
    root = jnp.where(live, jnp.sqrt(sine * (math.pi / LAT)), 0.0).reshape(8, 128)
    log_sine = jnp.log(sine).reshape(8, 128)
    degree = jnp.arange(L, dtype=jnp.int32)[None, :]
    past = degree > orders[:, None]
    val, ord_val = degree.astype(F32), order[:, None]
    divisor = jnp.where(past, val * val - ord_val * ord_val, 1.0)
    up = jnp.where(past, jnp.sqrt(jnp.maximum((4.0 * val * val - 1.0) / divisor, 0.0)), 0.0)
    lower = (val - 1.0) * (val - 1.0) - ord_val * ord_val
    back = jnp.sqrt(
        jnp.maximum(lower * (2.0 * val + 1.0) / ((2.0 * val - 3.0) * divisor), 0.0)
    )
    back = jnp.where(past, back, 0.0)
    start = (degree == orders[:, None]).astype(F32)
    smem = pl.BlockSpec(memory_space=pltpu.SMEM)
    vmem = pl.BlockSpec(memory_space=pltpu.VMEM)
    return pl.pallas_call(
        legendre_kernel,
        out_shape=jax.ShapeDtypeStruct((ORDERS, L, LAT), BF16),
        in_specs=[smem] * 5 + [vmem] * 3,
        out_specs=vmem,
        scratch_shapes=[pltpu.VMEM((ORDERS, 8 * BLOCK, 128), F32)],
        name="legendre",
    )(up.reshape(-1), back.reshape(-1), start.reshape(-1), seed, order, x, root, log_sine)


def eye(rows, cols):
    same = lax.broadcasted_iota(jnp.int32, (rows, cols), 0) == lax.broadcasted_iota(
        jnp.int32, (rows, cols), 1
    )
    return same.astype(F32).astype(BF16)


def spread_kernel(x_ref, out_ref):
    @pl.when(pl.program_id(0) < USED)
    def _():
        unit = eye(PAD, COLS)
        for t in range(SLOT):
            out_ref[0, t] = lax.dot_general(
                unit, x_ref[t], (((1,), (1,)), ((), ())), preferred_element_type=F32
            ).astype(BF16)

    @pl.when(pl.program_id(0) >= USED)
    def _():
        out_ref[...] = jnp.zeros_like(out_ref)


def spread(x):
    return pl.pallas_call(
        spread_kernel,
        grid=(LONS,),
        out_shape=jax.ShapeDtypeStruct((LONS, SLOT, PAD, C), BF16),
        in_specs=[pl.BlockSpec((SLOT, C, COLS), lambda g: (jnp.minimum(g, USED - 1), 0, 0))],
        out_specs=pl.BlockSpec((1, SLOT, PAD, C), lambda g: (g, 0, 0, 0)),
        name="spread",
    )(x)


def collect_kernel(x_ref, out_ref):
    unit = eye(PAD, COLS)
    for t in range(SLOT):
        out_ref[t] = lax.dot_general(
            x_ref[0, t], unit, (((0,), (0,)), ((), ())), preferred_element_type=F32
        ).astype(BF16)


def collect(x):
    return pl.pallas_call(
        collect_kernel,
        grid=(USED,),
        out_shape=jax.ShapeDtypeStruct((ROWS, C, COLS), BF16),
        in_specs=[pl.BlockSpec((1, SLOT, PAD, C), lambda g: (g, 0, 0, 0))],
        out_specs=pl.BlockSpec((SLOT, C, COLS), lambda g: (g, 0, 0)),
        name="collect",
    )(x)


def forward_kernel(table, x_ref, out_ref, buf):
    rows = table.shape[0]
    for pair in range(SLOT // 2):
        right = jnp.concatenate(
            [x_ref[:, 2 * pair + half].reshape(LONS * PAD, C) for half in range(2)], axis=1
        )
        done = jnp.dot(table[...], right, preferred_element_type=F32)
        for half in range(2):
            buf[pl.ds(2 * pair + half, rows, stride=SLOT), :] = done[:, half * C : half * C + C]
    out_ref[...] = buf[...].astype(BF16)


def fourier_forward(table, x):
    steps = 2
    rows = 2 * M // steps
    return pl.pallas_call(
        forward_kernel,
        grid=(steps,),
        out_shape=jax.ShapeDtypeStruct((2 * M * SLOT, C), BF16),
        in_specs=[
            pl.BlockSpec((rows, LONS * PAD), lambda g: (g, 0)),
            pl.BlockSpec((LONS, SLOT, PAD, C), lambda g: (0, 0, 0, 0)),
        ],
        out_specs=pl.BlockSpec((rows * SLOT, C), lambda g: (g, 0)),
        scratch_shapes=[pltpu.VMEM((rows * SLOT, C), F32)],
        name="fourier_forward",
    )(table, x)


def backward_kernel(table, x_ref, out_ref):
    for pair in range(SLOT // 2):
        right = jnp.concatenate([x_ref[2 * pair], x_ref[2 * pair + 1]], axis=1)
        done = jnp.dot(table[...], right, preferred_element_type=F32).astype(BF16)
        for half in range(2):
            for j in range(out_ref.shape[0]):
                out_ref[j, 2 * pair + half] = done[
                    j * PAD : j * PAD + PAD, half * C : half * C + C
                ]


def fourier_backward(table, x):
    steps = 4
    each = LONS // steps
    return pl.pallas_call(
        backward_kernel,
        grid=(steps,),
        out_shape=jax.ShapeDtypeStruct((LONS, SLOT, PAD, C), BF16),
        in_specs=[
            pl.BlockSpec((each * PAD, 2 * M), lambda g: (g, 0)),
            pl.BlockSpec((SLOT, 2 * M, C), lambda g: (0, 0, 0)),
        ],
        out_specs=pl.BlockSpec((each, SLOT, PAD, C), lambda g: (g, 0, 0, 0)),
        name="fourier_backward",
    )(table, x)


def transform_kernel(table, x_ref, out_ref, buf):
    g = pl.program_id(0)
    rows = table.shape[1]
    right = jnp.concatenate([x_ref[0], x_ref[1]], axis=1)
    done = jnp.dot(table[0], right, preferred_element_type=F32)
    for half in range(2):
        buf[pl.ds(2 * g + half, rows, stride=Q), :] = done[:, half * C : half * C + C]

    @pl.when(g == ORDERS - 1)
    def _():
        out_ref[: rows * Q, :] = buf[...].astype(BF16)
        if out_ref.shape[0] > rows * Q:
            out_ref[rows * Q :, :] = jnp.zeros((out_ref.shape[0] - rows * Q, C), BF16)


def transform(table, x, out_rows, name):
    _, rows, inner = table.shape
    return pl.pallas_call(
        transform_kernel,
        grid=(ORDERS,),
        out_shape=jax.ShapeDtypeStruct((out_rows, C), BF16),
        in_specs=[
            pl.BlockSpec((1, rows, inner), lambda g: (g, 0, 0)),
            pl.BlockSpec((2, inner, C), lambda g: (g, 0, 0)),
        ],
        out_specs=pl.BlockSpec((out_rows, C), lambda g: (0, 0)),
        scratch_shapes=[pltpu.VMEM((rows * Q, C), F32)],
        name=name,
    )(table, x)


def exchange(x, axis):
    return lax.all_to_all(x, axis, split_axis=0, concat_axis=0, tiled=True)


def share_sum(partial):
    me = lax.axis_index("lon")
    held = partial.reshape(DEGREES, 2, 2, 2, 2, C // LONS, C)
    for bit in range(4):
        axis = 4 - bit
        mine = (me >> bit) & 1
        keep = lax.dynamic_index_in_dim(held, mine, axis, keepdims=False)
        give = lax.dynamic_index_in_dim(held, 1 - mine, axis, keepdims=False)
        got = lax.ppermute(
            give.astype(BF16), "lon", [(k, k ^ (1 << bit)) for k in range(LONS)]
        )
        held = keep + got.astype(F32)
    return held


def on_device(grad_out, spectrum, weights):
    both = ("lon", "lat")
    first_order = (lax.axis_index("lon") * LATS + lax.axis_index("lat")) * ORDERS
    rows = exchange(spread(grad_out[0]), "lon")
    forward, backward = fourier_tables()
    legendre = legendre_table(first_order)
    turned = jnp.swapaxes(legendre, 1, 2)
    stored = spectrum.reshape(LATS * ORDERS, DEGREES, 2, C).transpose(1, 0, 2, 3)
    stored = stored.reshape(DEGREES, LATS * Q, C)

    spectra = fourier_forward(forward, rows).reshape(LATS * LONS, Q, SLOT // 2, 2, C)
    columns = exchange(spectra, both)[: USED * LATS]
    columns = columns.transpose(1, 0, 2, 3, 4).reshape(Q, LAT, C)
    analysed = transform(legendre, columns, L * Q, "legendre_forward")
    gathered = exchange(analysed.reshape(LATS, DEGREES, ORDERS, 2, C), "lat")
    gathered = gathered.transpose(1, 0, 2, 3, 4).reshape(DEGREES, LATS * Q, C)
    spec_local = jnp.einsum("lrd,lcd->lrc", gathered, weights, preferred_element_type=F32)
    spec_local = spec_local.astype(BF16).reshape(DEGREES, LATS, Q, C).transpose(1, 2, 0, 3)
    spec_local = spec_local.reshape(LATS, Q, DEGREES // 2, 2, C)
    partial_sum = jnp.einsum("lrc,lrd->lcd", stored, gathered, preferred_element_type=F32)
    weight_grad = share_sum(partial_sum)

    spec_grad = exchange(spec_local, "lat").transpose(1, 0, 2, 3, 4).reshape(Q, L, C)
    col_grad = transform(turned, spec_grad, LATS * LONS * SLOT * Q, "legendre_backward")
    row_block = exchange(col_grad.reshape(LATS * LONS, SLOT, ORDERS, 2, C), both)
    row_block = row_block.transpose(1, 0, 2, 3, 4).reshape(SLOT, 2 * M, C)
    grid_part = fourier_backward(backward, row_block)
    grad_in = collect(exchange(grid_part, "lon"))
    return grad_in[None], weight_grad


def solution(mesh):
    in_specs = (
        P(None, "lat", None, "lon"),
        P("lon", "lat", None, None, None),
        P("lat", None, None),
    )
    out_specs = (P(None, "lat", None, "lon"), P("lat", "lon", None))
    return jax.shard_map(
        on_device, mesh=mesh, in_specs=in_specs, out_specs=out_specs, check_vma=False
    )
```

time: 1240 us -> 314 us (0.25); the launches traced: 1220 us -> 312 us
  loops' own time: 511 us -> 0 us
  other arithmetic: 213 us -> 26 us
  local copies, waits for them, and re-layouts: 151 us -> 49.6 us
  blocking collectives: 99.3 us -> 0 us
  Pallas kernels: 0 us -> 60.5 us
  waiting for transfers between devices: 177 us -> 125 us
  matrix products: 25.6 us -> 4.7 us
  between operations: 14.5 us -> 0.89 us
  starting transfers between devices: 31.9 us -> 45.2 us
    another operation x1 -> x0, loops' own time: 511 us -> none  [legendre_table(): _, blocks = lax.scan(advance, (initial, initial, initial), starts)]
    all_to_all x3 -> x0, blocking collectives: 99.3 us -> none  [the longest x1 37.7 us: on_device(): lax.all_to_all(col_grad, 'lat', split_axis=1, concat_axis=4, tiled=True)]
    psum x1 -> x0, waiting for transfers between devices: 99 us -> none  [on_device(): lax.psum(partial_value.astype(jnp.bfloat16), 'lon').astype(jnp.float32)]
    while x690 -> x0, other arithmetic: 94.7 us -> none
    sqrt x960 -> x0, other arithmetic: 60.5 us -> none  [the longest x570 29.4 us: advance(): jnp.sqrt(jnp.maximum((4.0 * degree_val * degree_val - 1.0) / divisor, 0.0))]
    pallas_call x0 -> x7, Pallas kernels: none -> 60.5 us  [the longest x2 13.7 us: transform(): pl.pallas_call(transform_kernel, grid=(ORDERS,), out_shape=jax.ShapeDtype...]
    ppermute x0 -> x4, waiting for transfers between devices: none -> 36.8 us  [share_sum(): lax.ppermute(give.astype(BF16), 'lon', [(k, k ^ 1 << bit) for k in range(...]
    all_to_all x11 -> x0, local copies, waits for them, and re-layouts: 36.2 us -> none  [the longest x2 11.5 us: on_device(): lax.all_to_all(spectra, 'lat', split_axis=4, concat_axis=1, tiled=True)]
  transfers between devices with their start and end apart: 6 -> 10, of which waited for: 4 -> 7; matrix products, arithmetic and copies ran while one was open for 25% -> 18% of each run, Pallas kernels for 0% -> 8%
where the time goes in v1:
time: 314 us; the launch traced here: 312 us
  waiting for transfers between devices  125 us (40%)
  Pallas kernels  60.5 us (19%)
  local copies, waits for them, and re-layouts  49.6 us (16%)
  starting transfers between devices  45.2 us (14%)
  other arithmetic  26 us (8%)
  matrix products  4.7 us (1%)
    all_to_all x6, waiting for transfers between devices, exchange(): return lax.all_to_all(x, axis, split_axis=0, concat_axis=0, tiled=True)  88 us
    all_to_all x6, starting transfers between devices, exchange(): return lax.all_to_all(x, axis, split_axis=0, concat_axis=0, tiled=True)  39.7 us
    ppermute x4, waiting for transfers between devices, share_sum(): lax.ppermute(give.astype(BF16), 'lon', [(k, k ^ 1 << bit) for k in range(...  36.8 us
    pallas_call x2, Pallas kernels, transform(): pl.pallas_call(transform_kernel, grid=(ORDERS,), out_shape=jax.ShapeDtype...  13.7 us
    pallas_call x1, Pallas kernels, legendre_table(): pl.pallas_call(legendre_kernel, out_shape=jax.ShapeDtypeStruct((ORDERS, L...  11.7 us
    unnamed x12, local copies, waits for them, and re-layouts  11.2 us
    pallas_call x1, Pallas kernels, spread(): pl.pallas_call(spread_kernel, grid=(LONS,), out_shape=jax.ShapeDtypeStruc...  10.8 us
    pallas_call x1, Pallas kernels, collect(): pl.pallas_call(collect_kernel, grid=(USED,), out_shape=jax.ShapeDtypeStru...  10.6 us
  transfers between devices with their start and end apart: 10, of which 7 were waited for; matrix products, arithmetic and copies ran while one was open for 18% of the time, Pallas kernels for 8%

profile of v1, /device:TPU:0, one launch (start us, length us, event | category | flops | bytes accessed | tf_op | source)
XLA Modules:
  0.0 311.6 jit_solution(5955164991517255546)
XLA Ops:
  0.6 0.0 copy-start
  0.6 4.7 %copy.28 = bf16[1,90,128,90]{3,2,1,0:T(8,128)(2,1)} copy(bf16[1,90,128,90]{2,3,1,0:T(8,128)(2,1)} %param.4) | data formatting | bytes 4147200 | tf_op args[0]
  5.3 10.8 %spread.1 = bf16[16,6,96,128]{3,2,1,0:T(8,128)(2,1)} custom-call(bf16[90,128,90]{2,1,0:T(8,128)(2,1)} %bitcast.52), custom_call_target="tpu_custom_call" | custom-call | tf_op jit(solution)/shard_map/spread/pallas_call | solution.py:176
  16.1 8.2 %all-to-all-start = ((bf16[16,6,96,128]{3,2,1,0:T(8,128)(2,1)}), bf16[16,6,96,128]{3,2,1,0:T(8,128)(2,1)}, u32[]{:S(2)}, u32[]{:S(2)}) async-start(bf16[16,6,96,128]{3,2,1,0:T(8,128)(2,1)} %spread.1), calls=%async_computation | async-start | bytes 4718592 | tf_op jit(solution)/shard_map/all_to_all | solution.py:293
  24.3 8.1 %multiply_convert_fusion.table = bf16[1280,1536]{1,0:T(8,128)(2,1)} fusion(f32[1536]{0:T(1024)S(1)} %fusion.32, f32[1280]{0:T(1024)S(1)} %fusion.30, f32[1280]{0:T(1024)S(1)} %fusion.26, f32[1536]{0:T(1024)S(1)} %fusion.25), kind=kLoop, calls=%fused_computation | loop fusion | flops 49152000 | bytes 3954688 | tf_op jit(solution)/shard_map/convert_element_type | solution.py:58
  32.5 23.9 %all-to-all-done.x_ref = bf16[16,6,96,128]{3,2,1,0:T(8,128)(2,1)} async-done(((bf16[16,6,96,128]{3,2,1,0:T(8,128)(2,1)}), bf16[16,6,96,128]{3,2,1,0:T(8,128)(2,1)}, u32[]{:S(2)}, u32[]{:S(2)}) %all-to-all-start) | async-done | bytes 2359328 | tf_op jit(solution)/shard_map/all_to_all | solution.py:293
  56.4 6.8 %fourier_forward.1 = bf16[7680,128]{1,0:T(8,128)(2,1)} custom-call(bf16[1280,1536]{1,0:T(8,128)(2,1)} %multiply_convert_fusion.table, bf16[16,6,96,128]{3,2,1,0:T(8,128)(2,1)} %all-to-all-done.x_ref), custom_call_target="tpu_custom_call" | custom-call | tf_op jit(solution)/shard_map/fourier_forward/pallas_call | solution.py:220
  63.2 6.7 %all-to-all-start.1 = ((bf16[128,10,3,2,128]{4,3,2,1,0:T(2,128)(2,1)}), bf16[128,10,3,2,128]{4,3,2,1,0:T(2,128)(2,1)}, u32[]{:S(2)}, u32[]{:S(2)}) async-start(bf16[128,10,3,2,128]{4,3,2,1,0:T(2,128)(2,1)} %bitcast.54), calls=%async_computation.1 | async-start | bytes 3932160 | tf_op jit(solution)/shard_map/all_to_all | solution.py:293
  69.9 0.1 subtract_multiply_fusion
  70.0 0.1 mul.332
  70.1 0.1 sub.132
  70.1 0.1 fusion.10
  70.2 0.1 gt.23
  70.3 0.1 div.76
  70.4 0.1 mul.334
  70.5 0.7 reshape.331.start
  71.2 1.3 dynamic_slice.31.seed
  72.5 0.6 fusion.57.order
  73.0 0.7 fusion.56.sine_ref
  73.7 0.7 sqrt_select_fusion.2
  74.4 0.6 sqrt_select_fusion
  75.0 11.7 %legendre.1.table = bf16[5,720,720]{2,1,0:T(8,128)(2,1)} custom-call(f32[3600]{0:T(1024)} %get-tuple-element.9.up, f32[3600]{0:T(1024)} %get-tuple-element.8.back, f32[3600]{0:T(1024)} %reshape.331.start, f32[5]{0:T(128)} %dynamic_slice.31.seed, f32[5]{0:T(128)} %fusion.57.order, f32[8,128]{1,0:T(8,128)} %get-tuple-element.17.x_ref, ...), custom_call_target="tpu_custom_call" | custom-call | tf_op jit(solution)/shard_map/legendre/pallas_call | solution.py:144
  86.7 11.8 %all-to-all-done.1 = bf16[128,10,3,2,128]{4,3,2,1,0:T(2,128)(2,1)} async-done(((bf16[128,10,3,2,128]{4,3,2,1,0:T(2,128)(2,1)}), bf16[128,10,3,2,128]{4,3,2,1,0:T(2,128)(2,1)}, u32[]{:S(2)}, u32[]{:S(2)}) %all-to-all-start.1) | async-done | bytes 1966112 | tf_op jit(solution)/shard_map/all_to_all | solution.py:293
  98.6 2.8 slice_bitcast_fusion
  101.3 2.5 copy.29
  103.8 6.8 %legendre_forward.1 = bf16[7200,128]{1,0:T(8,128)(2,1)} custom-call(bf16[5,720,720]{2,1,0:T(8,128)(2,1)} %legendre.1.table, bf16[10,720,128]{2,1,0:T(8,128)(2,1)} %bitcast.61), custom_call_target="tpu_custom_call" | custom-call | tf_op jit(solution)/shard_map/legendre_forward/pallas_call | solution.py:278
  110.6 4.5 %all-to-all-start.2 = ((bf16[8,90,5,2,128]{4,3,2,1,0:T(2,128)(2,1)}), bf16[8,90,5,2,128]{4,3,2,1,0:T(2,128)(2,1)}, u32[]{:S(2)}, u32[]{:S(2)}) async-start(bf16[8,90,5,2,128]{4,3,2,1,0:T(2,128)(2,1)} %bitcast.60), calls=%async_computation.2 | async-start | bytes 3686400 | tf_op jit(solution)/shard_map/all_to_all | solution.py:293
  115.1 4.0 %copy.36 = bf16[90,40,2,128]{3,2,1,0:T(2,128)(2,1)} copy(bf16[90,40,2,128]{3,2,0,1:T(2,128)(2,1)} %bitcast.62) | data formatting | bytes 3686400 | tf_op jit(solution)/shard_map/transpose | solution.py:318
  119.1 19.8 %all-to-all-done.2 = bf16[8,90,5,2,128]{4,3,2,1,0:T(2,128)(2,1)} async-done(((bf16[8,90,5,2,128]{4,3,2,1,0:T(2,128)(2,1)}), bf16[8,90,5,2,128]{4,3,2,1,0:T(2,128)(2,1)}, u32[]{:S(2)}, u32[]{:S(2)}) %all-to-all-start.2) | async-done | bytes 1843232 | tf_op jit(solution)/shard_map/all_to_all | solution.py:293
  138.9 2.8 copy.30
  141.7 2.5 fusion.58
  144.2 1.5 fusion.6
  145.7 2.2 convolution_convert_fusion
  147.9 0.5 copy.31
  148.4 1.2 copy.32
  149.6 2.7 copy.33
  152.2 4.3 %all-to-all-start.3 = ((bf16[8,10,45,2,128]{4,3,2,1,0:T(2,128)(2,1)}), bf16[8,10,45,2,128]{4,3,2,1,0:T(2,128)(2,1)}, u32[]{:S(2)}, u32[]{:S(2)}) async-start(bf16[8,10,45,2,128]{4,3,2,1,0:T(2,128)(2,1)} %copy.33), calls=%async_computation.3 | async-start | bytes 3686400 | tf_op jit(solution)/shard_map/all_to_all | solution.py:293
  156.6 8.8 %copy.27 = bf16[5,720,720]{1,2,0:T(8,128)(2,1)} copy(bf16[5,720,720]{2,1,0:T(8,128)(2,1)} %legendre.1.table) | data formatting | bytes 10368000 | tf_op jit(solution)/shard_map/legendre/pallas_call | solution.py:144
  165.4 2.5 bitcast_add_fusion
  167.9 1.1 fusion.7
  169.0 0.8 collective-permute-start.1
  169.9 12.0 %all-to-all-done.3 = bf16[8,10,45,2,128]{4,3,2,1,0:T(2,128)(2,1)} async-done(((bf16[8,10,45,2,128]{4,3,2,1,0:T(2,128)(2,1)}), bf16[8,10,45,2,128]{4,3,2,1,0:T(2,128)(2,1)}, u32[]{:S(2)}, u32[]{:S(2)}) %all-to-all-start.3) | async-done | bytes 1843232 | tf_op jit(solution)/shard_map/all_to_all | solution.py:293
  181.8 4.0 %copy.34 = bf16[10,8,45,2,128]{4,3,2,1,0:T(2,128)(2,1)} copy(bf16[10,8,45,2,128]{4,3,2,0,1:T(2,128)(2,1)} %bitcast.11) | data formatting | bytes 3686400 | tf_op jit(solution)/shard_map/transpose | solution.py:333
  185.9 6.9 %legendre_backward.1 = bf16[7680,128]{1,0:T(8,128)(2,1)} custom-call(bf16[5,720,720]{2,1,0:T(8,128)(2,1)} %bitcast.46, bf16[10,720,128]{2,1,0:T(8,128)(2,1)} %bitcast.58), custom_call_target="tpu_custom_call" | custom-call | tf_op jit(solution)/shard_map/legendre_backward/pallas_call | solution.py:278
  192.7 11.6 %all-to-all-start.4 = ((bf16[128,6,5,2,128]{4,3,2,1,0:T(2,128)(2,1)}), bf16[128,6,5,2,128]{4,3,2,1,0:T(2,128)(2,1)}, u32[]{:S(2)}, u32[]{:S(2)}) async-start(bf16[128,6,5,2,128]{4,3,2,1,0:T(2,128)(2,1)} %bitcast.53), calls=%async_computation.4 | async-start | bytes 3932160 | tf_op jit(solution)/shard_map/all_to_all | solution.py:293
  204.3 8.2 %multiply_convert_fusion.1.table = bf16[1536,1280]{1,0:T(8,128)(2,1)} fusion(f32[1536]{0:T(1024)S(1)} %fusion.32, f32[1280]{0:T(1024)S(1)} %fusion.30, f32[1280]{0:T(1024)S(1)} %fusion.26, f32[1536]{0:T(1024)S(1)} %fusion.25), kind=kLoop, calls=%fused_computation.7 | loop fusion | flops 49152000 | bytes 3954688 | tf_op jit(solution)/shard_map/convert_element_type | solution.py:61
  212.6 20.5 %all-to-all-done.4 = bf16[128,6,5,2,128]{4,3,2,1,0:T(2,128)(2,1)} async-done(((bf16[128,6,5,2,128]{4,3,2,1,0:T(2,128)(2,1)}), bf16[128,6,5,2,128]{4,3,2,1,0:T(2,128)(2,1)}, u32[]{:S(2)}, u32[]{:S(2)}) %all-to-all-start.4) | async-done | bytes 1966112 | tf_op jit(solution)/shard_map/all_to_all | solution.py:293
  233.1 4.2 %copy.35 = bf16[6,128,5,2,128]{4,3,2,1,0:T(2,128)(2,1)} copy(bf16[6,128,5,2,128]{4,3,2,0,1:T(2,128)(2,1)} %bitcast.14) | data formatting | bytes 3932160 | tf_op jit(solution)/shard_map/transpose | solution.py:336
  237.2 7.0 %fourier_backward.1 = bf16[16,6,96,128]{3,2,1,0:T(8,128)(2,1)} custom-call(bf16[1536,1280]{1,0:T(8,128)(2,1)} %multiply_convert_fusion.1.table, bf16[6,1280,128]{2,1,0:T(8,128)(2,1)} %bitcast.55), custom_call_target="tpu_custom_call" | custom-call | tf_op jit(solution)/shard_map/fourier_backward/pallas_call | solution.py:248
  244.2 4.5 %all-to-all-start.5 = ((bf16[16,6,96,128]{3,2,1,0:T(8,128)(2,1)}), bf16[16,6,96,128]{3,2,1,0:T(8,128)(2,1)}, u32[]{:S(2)}, u32[]{:S(2)}) async-start(bf16[16,6,96,128]{3,2,1,0:T(8,128)(2,1)} %fourier_backward.1), calls=%async_computation.5 | async-start | bytes 4718592 | tf_op jit(solution)/shard_map/all_to_all | solution.py:293
  248.7 1.2 bitcast_add_fusion.1
  249.9 0.0 copy-start.3
  249.9 1.1 copy-done.3
  251.0 0.1 fusion.8
  251.1 1.8 collective-permute-start.2
  252.9 31.9 %collective-permute-done.2 = bf16[90,2,8,128]{3,2,0,1:T(8,128)(2,1)S(1)} collective-permute-done((bf16[90,2,8,128]{3,2,0,1:T(8,128)(2,1)S(1)}, bf16[90,2,8,128]{3,2,0,1:T(8,128)(2,1)S(1)}, u32[]{:S(2)}, u32[]{:S(2)}) %collective-permute-start.2) | collective-permute-done | bytes 368672 | tf_op jit(solution)/shard_map/ppermute | solution.py:304
  284.9 1.3 bitcast_add_fusion.2
  286.2 0.0 copy-start.4
  286.2 0.9 copy-done.4
  287.1 2.8 collective-permute-start.3
  289.9 4.9 %collective-permute-done.3 = bf16[90,8,128]{2,1,0:T(8,128)(2,1)S(1)} collective-permute-done((bf16[90,8,128]{2,1,0:T(8,128)(2,1)S(1)}, bf16[90,8,128]{2,1,0:T(8,128)(2,1)S(1)}, u32[]{:S(2)}, u32[]{:S(2)}) %collective-permute-start.3) | collective-permute-done | bytes 184352 | tf_op jit(solution)/shard_map/ppermute | solution.py:304
  294.8 1.8 bitcast_add_fusion.3
  296.5 10.6 %collect.1 = bf16[90,128,90]{2,1,0:T(8,128)(2,1)} custom-call(bf16[16,6,96,128]{3,2,1,0:T(8,128)(2,1)} %all-to-all-done.5.x_ref), custom_call_target="tpu_custom_call" | custom-call | tf_op jit(solution)/shard_map/collect/pallas_call | solution.py:195
  307.1 4.5 %copy.39 = bf16[1,90,128,90]{2,3,1,0:T(8,128)(2,1)} copy(bf16[1,90,128,90]{3,2,1,0:T(8,128)(2,1)} %bitcast.51) | data formatting | bytes 4147200
  (22 shorter events, 0.1 us)
Async XLA Ops:
  0.6 145.0 %copy-start = (bf16[90,128,128]{2,1,0:T(8,128)(2,1)S(1)}, bf16[90,128,128]{2,1,0:T(8,128)(2,1)}, u32[]{:S(2)}) copy-start(bf16[90,128,128]{2,1,0:T(8,128)(2,1)} %param.6) | copy-start | bytes 8847364
  16.1 40.4 %all-to-all-start = ((bf16[16,6,96,128]{3,2,1,0:T(8,128)(2,1)}), bf16[16,6,96,128]{3,2,1,0:T(8,128)(2,1)}, u32[]{:S(2)}, u32[]{:S(2)}) async-start(bf16[16,6,96,128]{3,2,1,0:T(8,128)(2,1)} %spread.1), calls=%async_computation | async-start | bytes 4718592 | tf_op jit(solution)/shard_map/all_to_all | solution.py:293
  63.2 35.4 %all-to-all-start.1 = ((bf16[128,10,3,2,128]{4,3,2,1,0:T(2,128)(2,1)}), bf16[128,10,3,2,128]{4,3,2,1,0:T(2,128)(2,1)}, u32[]{:S(2)}, u32[]{:S(2)}) async-start(bf16[128,10,3,2,128]{4,3,2,1,0:T(2,128)(2,1)} %bitcast.54), calls=%async_computation.1 | async-start | bytes 3932160 | tf_op jit(solution)/shard_map/all_to_all | solution.py:293
  110.6 28.3 %all-to-all-start.2 = ((bf16[8,90,5,2,128]{4,3,2,1,0:T(2,128)(2,1)}), bf16[8,90,5,2,128]{4,3,2,1,0:T(2,128)(2,1)}, u32[]{:S(2)}, u32[]{:S(2)}) async-start(bf16[8,90,5,2,128]{4,3,2,1,0:T(2,128)(2,1)} %bitcast.60), calls=%async_computation.2 | async-start | bytes 3686400 | tf_op jit(solution)/shard_map/all_to_all | solution.py:293
  144.2 4.2 %copy-start.2 = (f32[90,128,128]{1,2,0:T(8,128)}, f32[90,128,128]{1,2,0:T(8,128)S(1)}, u32[]{:S(2)}) copy-start(f32[90,128,128]{1,2,0:T(8,128)S(1)} %fusion.58) | copy-start | bytes 17694724
  145.7 19.8 %collective-permute-start = (bf16[90,2,2,2,8,128]{5,4,0,1,2,3:T(8,128)(2,1)}, bf16[90,2,2,2,8,128]{5,4,0,1,2,3:T(8,128)(2,1)}, u32[]{:S(2)}, u32[]{:S(2)}) collective-permute-start(bf16[90,2,2,2,8,128]{5,4,0,1,2,3:T(8,128)(2,1)} %fusion.6), channel_id=1, source_target_pairs={{0,1},{1,0},{2,3},{3,2},{4,5},{5,4},{6,7},{7,6},{8,9},{9,8},{10,11... | collective-permute-start | bytes 4423688 | tf_op jit(solution)/shard_map/ppermute | solution.py:304
  152.2 29.6 %all-to-all-start.3 = ((bf16[8,10,45,2,128]{4,3,2,1,0:T(2,128)(2,1)}), bf16[8,10,45,2,128]{4,3,2,1,0:T(2,128)(2,1)}, u32[]{:S(2)}, u32[]{:S(2)}) async-start(bf16[8,10,45,2,128]{4,3,2,1,0:T(2,128)(2,1)} %copy.33), calls=%async_computation.3 | async-start | bytes 3686400 | tf_op jit(solution)/shard_map/all_to_all | solution.py:293
  169.0 79.7 %collective-permute-start.1 = (bf16[90,2,2,8,128]{4,3,0,1,2:T(8,128)(2,1)}, bf16[90,2,2,8,128]{4,3,0,1,2:T(8,128)(2,1)}, u32[]{:S(2)}, u32[]{:S(2)}) collective-permute-start(bf16[90,2,2,8,128]{4,3,0,1,2:T(8,128)(2,1)} %fusion.7), channel_id=1, source_target_pairs={{0,2},{1,3},{2,0},{3,1},{4,6},{5,7},{6,4},{7,5},{8,10},{9,11},{10,... | collective-permute-start | bytes 2211848 | tf_op jit(solution)/shard_map/ppermute | solution.py:304
  192.7 40.3 %all-to-all-start.4 = ((bf16[128,6,5,2,128]{4,3,2,1,0:T(2,128)(2,1)}), bf16[128,6,5,2,128]{4,3,2,1,0:T(2,128)(2,1)}, u32[]{:S(2)}, u32[]{:S(2)}) async-start(bf16[128,6,5,2,128]{4,3,2,1,0:T(2,128)(2,1)} %bitcast.53), calls=%async_computation.4 | async-start | bytes 3932160 | tf_op jit(solution)/shard_map/all_to_all | solution.py:293
  244.2 52.3 %all-to-all-start.5 = ((bf16[16,6,96,128]{3,2,1,0:T(8,128)(2,1)}), bf16[16,6,96,128]{3,2,1,0:T(8,128)(2,1)}, u32[]{:S(2)}, u32[]{:S(2)}) async-start(bf16[16,6,96,128]{3,2,1,0:T(8,128)(2,1)} %fourier_backward.1), calls=%async_computation.5 | async-start | bytes 4718592 | tf_op jit(solution)/shard_map/all_to_all | solution.py:293
  249.9 1.1 copy-start.3
  251.1 33.8 %collective-permute-start.2 = (bf16[90,2,8,128]{3,2,0,1:T(8,128)(2,1)S(1)}, bf16[90,2,8,128]{3,2,0,1:T(8,128)(2,1)S(1)}, u32[]{:S(2)}, u32[]{:S(2)}) collective-permute-start(bf16[90,2,8,128]{3,2,0,1:T(8,128)(2,1)S(1)} %fusion.8), channel_id=1, source_target_pairs={{0,4},{1,5},{2,6},{3,7},{4,0},{5,1},{6,2},{7,3},{8,12},{9,13},{10,... | collective-permute-start | bytes 1105928 | tf_op jit(solution)/shard_map/ppermute | solution.py:304
  284.9 26.8 %copy-start.1 = (bf16[90,128,128]{2,1,0:T(8,128)(2,1)S(1)}, bf16[90,128,128]{2,1,0:T(8,128)(2,1)}, u32[]{:S(2)}) copy-start(bf16[90,128,128]{2,1,0:T(8,128)(2,1)} %param.6) | copy-start | bytes 8847364
  286.2 0.9 copy-start.4
  287.1 7.7 %collective-permute-start.3 = (bf16[90,8,128]{2,1,0:T(8,128)(2,1)S(1)}, bf16[90,8,128]{2,1,0:T(8,128)(2,1)S(1)}, u32[]{:S(2)}, u32[]{:S(2)}) collective-permute-start(bf16[90,8,128]{2,1,0:T(8,128)(2,1)S(1)} %fusion.9), channel_id=1, source_target_pairs={{0,8},{1,9},{2,10},{3,11},{4,12},{5,13},{6,14},{7,15},{8,0},{9,1},... | collective-permute-start | bytes 552968 | tf_op jit(solution)/shard_map/ppermute | solution.py:304

commit v2 on v1

v2 whole, which is shorter than its diff:
```python
import math

import jax
import jax.numpy as jnp
import numpy as np
from jax import lax
from jax.experimental import pallas as pl
from jax.experimental.pallas import tpu as pltpu
from jax.sharding import PartitionSpec as P

LAT = 720
LON = 1440
L = 720
M = 640
C = 128
LATS = 8
LONS = 16
DEVICES = LATS * LONS
ROWS = LAT // LATS
COLS = LON // LONS
SLOT = 6
USED = ROWS // SLOT
PAD = 96
ORDERS = M // (LATS * LONS)
Q = 2 * ORDERS
CHUNK = Q * SLOT
DEGREES = L // LATS
BLOCK = 16
SHIFT = 40

F32 = jnp.float32
BF16 = jnp.bfloat16


def cosine_values(position, order, part):
    step = position * order + part * (LON // 4)
    turn = step - LON * jnp.floor(step * (1.0 / LON))
    fold = (LON // 4) - jnp.abs(turn - LON // 2)
    angle = fold * (2.0 * math.pi / LON)
    square = angle * angle
    series = -1.0 / 39916800.0
    for term in (1.0 / 362880.0, -1.0 / 5040.0, 1.0 / 120.0, -1.0 / 6.0, 1.0):
        series = series * square + term
    return -(angle * series) * (1.0 / math.sqrt(LON))


def fourier_tables():
    def line(shape, axis):
        at = lax.broadcasted_iota(jnp.int32, shape, axis)
        inner = at % PAD
        return (at // PAD * COLS + inner).astype(F32), (inner < COLS).astype(F32)

    def modes(shape, axis):
        at = lax.broadcasted_iota(jnp.int32, shape, axis)
        return (at // 2).astype(F32), (at % 2).astype(F32)

    wide = LONS * PAD
    position, live = line((1, wide), 1)
    order, part = modes((2 * M, 1), 0)
    forward = (cosine_values(position, order, part) * live).astype(BF16)
    position, live = line((wide, 1), 0)
    order, part = modes((1, 2 * M), 1)
    backward = (cosine_values(position, order, part) * live).astype(BF16)
    return forward, backward


def seed_constants():
    out = []
    for m in range(M):
        out.append(
            0.5 * math.log(m + 0.5)
            + 0.5 * math.lgamma(2.0 * m + 1.0)
            - math.lgamma(m + 1.0)
            - m * math.log(2.0)
        )
    return np.asarray(out, np.float32)


def legendre_kernel(up, back, start, seed, order, x_ref, root_ref, sine_ref, out, buf):
    x = x_ref[...]
    root = root_ref[...]
    base = [seed[k] + order[k] * sine_ref[...] for k in range(ORDERS)]
    zero = jnp.zeros_like(x)
    small = 2.0**-SHIFT
    unit = SHIFT * math.log(2.0)

    def block(first, row, steps, carry):
        current, previous, count = (list(part) for part in carry)
        factor = [None] * ORDERS
        for offset in range(steps):
            if offset % 8 == 0:
                for k in range(ORDERS):
                    big = jnp.maximum(jnp.abs(current[k]), jnp.abs(previous[k])) > 1.0
                    scale = jnp.where(big, small, 1.0)
                    current[k] = current[k] * scale
                    previous[k] = previous[k] * scale
                    count[k] = count[k] + jnp.where(big, 1.0, 0.0)
                    factor[k] = jnp.exp(base[k] + unit * count[k]) * root
            for k in range(ORDERS):
                at = k * L + first + offset
                advanced = (up[at] * x) * current[k] - back[at] * previous[k] + start[at]
                previous[k] = current[k]
                current[k] = advanced
                buf[k, offset * 8 : offset * 8 + 8, :] = advanced * factor[k]
        for k in range(ORDERS):
            for offset in range(steps, BLOCK):
                buf[k, offset * 8 : offset * 8 + 8, :] = zero
            for tt in range(SLOT):
                low = buf[k, pl.ds(tt, 8, stride=8), :]
                high = buf[k, pl.ds(64 + tt, 8, stride=8), :]
                both = jnp.concatenate([low, high], axis=0).astype(BF16)
                out[k, pl.ds(pl.multiple_of(row, BLOCK), BLOCK), tt * 128 : tt * 128 + 128] = both
        return tuple(current), tuple(previous), tuple(count)

    def band(k, carry):
        first, row = k * DEGREES, k * PAD
        whole = DEGREES // BLOCK

        def inner(step, carry):
            return block(first + step * BLOCK, row + step * BLOCK, BLOCK, carry)

        carry = lax.fori_loop(0, whole, inner, carry)
        done = whole * BLOCK
        return block(first + done, row + done, DEGREES - done, carry)

    none = (zero,) * ORDERS
    lax.fori_loop(0, LATS, band, (none, none, none))


def legendre_table(first_order):
    orders = first_order + jnp.arange(ORDERS, dtype=jnp.int32)
    order = orders.astype(F32)
    seed = lax.dynamic_slice(jnp.asarray(seed_constants()), (first_order,), (ORDERS,))
    slot = jnp.arange(1024, dtype=jnp.int32)
    tt, device = slot // DEVICES, slot % DEVICES
    lon, lat = device // LATS, device % LATS
    live = (tt < SLOT) & (lon < USED)
    row = jnp.where(live, ROWS * lat + SLOT * lon + tt, 0)
    angle = (row.astype(F32) + 0.5) * (math.pi / LAT)
    sine = jnp.sin(angle)
    x = jnp.where(live, jnp.cos(angle), 0.0).reshape(8, 128)
    root = jnp.where(live, jnp.sqrt(sine * (math.pi / LAT)), 0.0).reshape(8, 128)
    log_sine = jnp.log(sine).reshape(8, 128)
    degree = jnp.arange(L, dtype=jnp.int32)[None, :]
    past = degree > orders[:, None]
    val, ord_val = degree.astype(F32), order[:, None]
    divisor = jnp.where(past, val * val - ord_val * ord_val, 1.0)
    up = jnp.where(past, jnp.sqrt(jnp.maximum((4.0 * val * val - 1.0) / divisor, 0.0)), 0.0)
    lower = (val - 1.0) * (val - 1.0) - ord_val * ord_val
    back = jnp.sqrt(
        jnp.maximum(lower * (2.0 * val + 1.0) / ((2.0 * val - 3.0) * divisor), 0.0)
    )
    back = jnp.where(past, back, 0.0)
    start = (degree == orders[:, None]).astype(F32)
    smem = pl.BlockSpec(memory_space=pltpu.SMEM)
    vmem = pl.BlockSpec(memory_space=pltpu.VMEM)
    return pl.pallas_call(
        legendre_kernel,
        out_shape=jax.ShapeDtypeStruct((ORDERS, LATS * PAD, DEVICES * SLOT), BF16),
        in_specs=[smem] * 5 + [vmem] * 3,
        out_specs=vmem,
        scratch_shapes=[pltpu.VMEM((ORDERS, 8 * BLOCK, 128), F32)],
        name="legendre",
    )(up.reshape(-1), back.reshape(-1), start.reshape(-1), seed, order, x, root, log_sine)


def forward_kernel(table, x_ref, out_ref, buf):
    rows = table.shape[0]
    for pair in range(SLOT // 2):
        right = jnp.concatenate(
            [x_ref[:, 2 * pair + half].reshape(LONS * PAD, C) for half in range(2)], axis=1
        )
        done = jnp.dot(table[...], right, preferred_element_type=F32)
        for half in range(2):
            buf[pl.ds(2 * pair + half, rows, stride=SLOT), :] = done[:, half * C : half * C + C]
    out_ref[...] = buf[...].astype(BF16)


def fourier_forward(table, x):
    steps = 2
    rows = 2 * M // steps
    return pl.pallas_call(
        forward_kernel,
        grid=(steps,),
        out_shape=jax.ShapeDtypeStruct((2 * M * SLOT, C), BF16),
        in_specs=[
            pl.BlockSpec((rows, LONS * PAD), lambda g: (g, 0)),
            pl.BlockSpec((LONS, SLOT, PAD, C), lambda g: (0, 0, 0, 0)),
        ],
        out_specs=pl.BlockSpec((rows * SLOT, C), lambda g: (g, 0)),
        scratch_shapes=[pltpu.VMEM((rows * SLOT, C), F32)],
        name="fourier_forward",
    )(table, x)


def analyse_kernel(table, x_ref, out_ref, wide):
    g = pl.program_id(0)

    @pl.when(g == 0)
    def _():
        wide[...] = x_ref[...].astype(F32)

    def column(q):
        parts = [wide[pl.ds(q * SLOT + tt, DEVICES, stride=CHUNK), :] for tt in range(SLOT)]
        return jnp.concatenate(parts, axis=0).astype(BF16)

    right = jnp.concatenate([column(2 * g), column(2 * g + 1)], axis=1)
    done = jnp.dot(table[0], right, preferred_element_type=F32).astype(BF16)
    for half in range(2):
        out_ref[:, half] = done[:, half * C : half * C + C].reshape(LATS, PAD, C)


def analyse(table, x):
    return pl.pallas_call(
        analyse_kernel,
        grid=(ORDERS,),
        out_shape=jax.ShapeDtypeStruct((LATS, Q, PAD, C), BF16),
        in_specs=[
            pl.BlockSpec((1, LATS * PAD, DEVICES * SLOT), lambda g: (g, 0, 0)),
            pl.BlockSpec((DEVICES * CHUNK, C), lambda g: (0, 0)),
        ],
        out_specs=pl.BlockSpec((LATS, 2, PAD, C), lambda g: (0, g, 0, 0)),
        scratch_shapes=[pltpu.VMEM((DEVICES * CHUNK, C), F32)],
        name="analyse",
    )(table, x)


def mix_kernel(x_ref, weights, gathered, out_ref, wide, made):
    g = pl.program_id(0)
    each = weights.shape[0]

    @pl.when(g == 0)
    def _():
        wide[...] = x_ref[...].astype(F32)
        made[...] = jnp.zeros_like(made)

    for offset in range(each):
        rows = pl.ds(g * each + offset, LATS * Q, stride=PAD)
        part = wide[rows, :].astype(BF16)
        gathered[offset] = part
        made[rows, :] = lax.dot_general(
            part, weights[offset], (((1,), (1,)), ((), ())), preferred_element_type=F32
        )

    @pl.when(g == pl.num_programs(0) - 1)
    def _():
        out_ref[...] = made[...].astype(BF16)


def mix(x, weights):
    steps = 10
    each = DEGREES // steps
    whole = LATS * Q * PAD
    return pl.pallas_call(
        mix_kernel,
        grid=(steps,),
        out_shape=(
            jax.ShapeDtypeStruct((DEGREES, LATS * Q, C), BF16),
            jax.ShapeDtypeStruct((whole, C), BF16),
        ),
        in_specs=[
            pl.BlockSpec((whole, C), lambda g: (0, 0)),
            pl.BlockSpec((each, C, C), lambda g: (g, 0, 0)),
        ],
        out_specs=(
            pl.BlockSpec((each, LATS * Q, C), lambda g: (g, 0, 0)),
            pl.BlockSpec((whole, C), lambda g: (0, 0)),
        ),
        scratch_shapes=[pltpu.VMEM((whole, C), F32), pltpu.VMEM((whole, C), F32)],
        name="mix",
    )(x, weights)


def synthesise_kernel(table, x_ref, out_ref, made):
    g = pl.program_id(0)
    right = jnp.concatenate([x_ref[:, half].reshape(LATS * PAD, C) for half in range(2)], axis=1)
    done = jnp.dot(table[0], right, preferred_element_type=F32)
    for half in range(2):
        for tt in range(SLOT):
            made[pl.ds((2 * g + half) * SLOT + tt, DEVICES, stride=CHUNK), :] = done[
                tt * DEVICES : tt * DEVICES + DEVICES, half * C : half * C + C
            ]

    @pl.when(g == ORDERS - 1)
    def _():
        out_ref[...] = made[...].astype(BF16)


def synthesise(table, x):
    return pl.pallas_call(
        synthesise_kernel,
        grid=(ORDERS,),
        out_shape=jax.ShapeDtypeStruct((DEVICES * CHUNK, C), BF16),
        in_specs=[
            pl.BlockSpec((1, DEVICES * SLOT, LATS * PAD), lambda g: (g, 0, 0)),
            pl.BlockSpec((LATS, 2, PAD, C), lambda g: (0, g, 0, 0)),
        ],
        out_specs=pl.BlockSpec((DEVICES * CHUNK, C), lambda g: (0, 0)),
        scratch_shapes=[pltpu.VMEM((DEVICES * CHUNK, C), F32)],
        name="synthesise",
    )(table, x)


def backward_kernel(table, x_ref, out_ref, wide, right):
    @pl.when(pl.program_id(0) == 0)
    def _():
        wide[...] = x_ref[...].astype(F32)
        for tt in range(SLOT):
            right[:, tt * C : tt * C + C] = wide[pl.ds(tt, 2 * M, stride=SLOT), :].astype(BF16)

    for pair in range(SLOT // 2):
        both = right[:, 2 * pair * C : 2 * pair * C + 2 * C]
        done = jnp.dot(table[...], both, preferred_element_type=F32).astype(BF16)
        for half in range(2):
            for j in range(out_ref.shape[0]):
                out_ref[j, 2 * pair + half] = done[
                    j * PAD : j * PAD + PAD, half * C : half * C + C
                ]


def fourier_backward(table, x):
    steps = 4
    each = LONS // steps
    return pl.pallas_call(
        backward_kernel,
        grid=(steps,),
        out_shape=jax.ShapeDtypeStruct((LONS, SLOT, PAD, C), BF16),
        in_specs=[
            pl.BlockSpec((each * PAD, 2 * M), lambda g: (g, 0)),
            pl.BlockSpec((DEVICES * CHUNK, C), lambda g: (0, 0)),
        ],
        out_specs=pl.BlockSpec((each, SLOT, PAD, C), lambda g: (g, 0, 0, 0)),
        scratch_shapes=[
            pltpu.VMEM((DEVICES * CHUNK, C), F32),
            pltpu.VMEM((2 * M, SLOT * C), BF16),
        ],
        name="fourier_backward",
    )(table, x)


def exchange(x, axis):
    return lax.all_to_all(x, axis, split_axis=0, concat_axis=0, tiled=True)


def halve(held, bit, axis):
    mine = (lax.axis_index("lon") >> bit) & 1
    keep = lax.dynamic_index_in_dim(held, mine, axis, keepdims=False)
    give = lax.dynamic_index_in_dim(held, 1 - mine, axis, keepdims=False)
    got = lax.ppermute(give.astype(BF16), "lon", [(k, k ^ (1 << bit)) for k in range(LONS)])
    return keep.astype(F32) + got.astype(F32)


def cells(x):
    return x.reshape(DEVICES, CHUNK // 2, 2, C)


def on_device(grad_out, spectrum, weights):
    both = ("lon", "lat")
    first_order = (lax.axis_index("lon") * LATS + lax.axis_index("lat")) * ORDERS
    rows = jnp.swapaxes(grad_out[0], 1, 2)
    rows = jnp.pad(rows, ((0, LONS * SLOT - ROWS), (0, PAD - COLS), (0, 0)))
    rows = exchange(rows.reshape(LONS, SLOT, PAD, C), "lon")
    forward, backward = fourier_tables()
    legendre = legendre_table(first_order)
    rows, forward, legendre = lax.optimization_barrier((rows, forward, legendre))

    spectra = fourier_forward(forward, rows)
    columns = exchange(cells(spectra), both).reshape(DEVICES * CHUNK, C)
    turned = jnp.swapaxes(legendre, 1, 2)
    stored = spectrum.reshape(LATS * ORDERS, DEGREES, 2, C).transpose(1, 0, 2, 3)
    stored = stored.reshape(DEGREES, LATS * Q, C)
    columns, turned, stored = lax.optimization_barrier((columns, turned, stored))

    analysed = exchange(analyse(legendre, columns), "lat").reshape(LATS * Q * PAD, C)
    analysed, backward = lax.optimization_barrier((analysed, backward))
    gathered, spec_local = mix(analysed, weights)
    spec_grad = exchange(spec_local.reshape(LATS, Q, PAD, C), "lat")

    held = jnp.einsum("lrc,lrd->lcd", stored, gathered, preferred_element_type=F32)
    held = held.reshape(DEGREES, 2, 2, 2, 2, C // LONS, C)
    held = halve(halve(held, 0, 4), 2, 2)
    spec_grad, held = lax.optimization_barrier((spec_grad, held))

    row_block = exchange(cells(synthesise(turned, spec_grad)), both)
    held = halve(held, 3, 1)
    row_block, held = lax.optimization_barrier((row_block, held))
    grid_part = fourier_backward(backward, row_block.reshape(DEVICES * CHUNK, C))
    grid_part = exchange(grid_part, "lon")
    weight_grad = halve(held, 1, 1)
    grad_in = grid_part[:USED].reshape(ROWS, PAD, C)[:, :COLS]
    return jnp.swapaxes(grad_in, 1, 2)[None], weight_grad


def solution(mesh):
    in_specs = (
        P(None, "lat", None, "lon"),
        P("lon", "lat", None, None, None),
        P("lat", None, None),
    )
    out_specs = (P(None, "lat", None, "lon"), P("lat", "lon", None))
    return jax.shard_map(
        on_device, mesh=mesh, in_specs=in_specs, out_specs=out_specs, check_vma=False
    )
```

time: 314 us -> 280 us (0.89)
  local copies, waits for them, and re-layouts: 49.6 us -> 30 us
  Pallas kernels: 60.5 us -> 51.8 us
  waiting for transfers between devices: 125 us -> 119 us
    all_to_all x6, waiting for transfers between devices: 88 us -> 41.3 us  [exchange(): return lax.all_to_all(x, axis, split_axis=0, concat_axis=0, tiled=True)]
    ppermute x4, waiting for transfers between devices: 36.8 us -> 77.9 us  [halve(): lax.ppermute(give.astype(BF16), 'lon', [(k, k ^ 1 << bit) for k in range(...]
    transpose x6 -> x0, local copies, waits for them, and re-layouts: 17.4 us -> none  [the longest x2 5.26 us: on_device(): columns = columns.transpose(1, 0, 2, 3, 4).reshape(Q, LAT, C)]
    pallas_call x4 -> x3, Pallas kernels: 35 us -> 25.4 us  [the longest x1 11.2 us: mix(): pl.pallas_call(mix_kernel, grid=(steps,), out_shape=(jax.ShapeDtypeStruct...]
    optimization_barrier x0 -> x1, local copies, waits for them, and re-layouts: none -> 8.99 us  [on_device(): lax.optimization_barrier((rows, forward, legendre))]
    pallas_call x1 -> x0, local copies, waits for them, and re-layouts: 8.83 us -> none  [legendre_table(): pl.pallas_call(legendre_kernel, out_shape=jax.ShapeDtypeStruct((ORDERS, L...]
    unnamed x12 -> x14, local copies, waits for them, and re-layouts: 11.2 us -> 7.78 us
    pad x0 -> x1, local copies, waits for them, and re-layouts: none -> 3.27 us  [on_device(): rows = jnp.pad(rows, ((0, LONS * SLOT - ROWS), (0, PAD - COLS), (0, 0)))]
  transfers between devices with their start and end apart: 10 -> 10, of which waited for: 7 -> 7; matrix products, arithmetic and copies ran while one was open for 18% -> 16% of each run, Pallas kernels for 8% -> 4%
where the time goes in v2:
time: 280 us; the launch traced here: 278 us
  waiting for transfers between devices  119 us (42%)
  Pallas kernels  51.8 us (18%)
  starting transfers between devices  46.7 us (17%)
  local copies, waits for them, and re-layouts  30 us (11%)
  other arithmetic  26.7 us (10%)
  matrix products  3.05 us (1%)
    ppermute x4, waiting for transfers between devices, halve(): lax.ppermute(give.astype(BF16), 'lon', [(k, k ^ 1 << bit) for k in range(...  77.9 us
    all_to_all x6, waiting for transfers between devices, exchange(): return lax.all_to_all(x, axis, split_axis=0, concat_axis=0, tiled=True)  41.3 us
    all_to_all x6, starting transfers between devices, exchange(): return lax.all_to_all(x, axis, split_axis=0, concat_axis=0, tiled=True)  39.3 us
    pallas_call x1, Pallas kernels, legendre_table(): pl.pallas_call(legendre_kernel, out_shape=jax.ShapeDtypeStruct((ORDERS, L...  11.9 us
    pallas_call x1, Pallas kernels, mix(): pl.pallas_call(mix_kernel, grid=(steps,), out_shape=(jax.ShapeDtypeStruct...  11.2 us
    optimization_barrier x1, local copies, waits for them, and re-layouts, on_device(): lax.optimization_barrier((rows, forward, legendre))  8.99 us
    convert_element_type x1, other arithmetic, fourier_tables(): backward = (cosine_values(position, order, part) * live).astype(BF16)  8.25 us
    convert_element_type x1, other arithmetic, fourier_tables(): forward = (cosine_values(position, order, part) * live).astype(BF16)  8.09 us
  transfers between devices with their start and end apart: 10, of which 7 were waited for; matrix products, arithmetic and copies ran while one was open for 16% of the time, Pallas kernels for 4%

profile of v2, /device:TPU:0, one launch (start us, length us, event | category | flops | bytes accessed | tf_op | source)
XLA Modules:
  0.0 278.3 jit_solution(16119017354867078761)
XLA Ops:
  0.6 3.3 %pad.4 = bf16[96,96,128]{2,1,0:T(8,128)(2,1)} pad(bf16[90,90,128]{2,1,0:T(8,128)(2,1)} %bitcast.49, bf16[]{:T(256)} %constant.224.clone.1), padding=0_6x0_6x0_0 | pad | bytes 4432898 | tf_op jit(solution)/shard_map/jit(_pad)/pad | solution.py:361
  3.9 8.2 %all-to-all-start = ((bf16[16,6,96,128]{3,2,1,0:T(8,128)(2,1)}), bf16[16,6,96,128]{3,2,1,0:T(8,128)(2,1)S(1)}, u32[]{:S(2)}, u32[]{:S(2)}) async-start(bf16[16,6,96,128]{3,2,1,0:T(8,128)(2,1)} %bitcast.2), calls=%async_computation | async-start | bytes 4718592 | tf_op jit(solution)/shard_map/all_to_all | solution.py:342
  12.2 0.6 fusion.50.order
  12.8 0.7 sqrt_select_fusion.2
  13.5 0.7 fusion.49.sine_ref
  14.1 0.1 fusion.10
  14.2 0.1 gt.23
  14.3 0.1 subtract_multiply_fusion
  14.4 0.1 mul.331
  14.5 0.1 mul.333
  14.5 0.1 sub.132
  14.6 0.1 div.98
  14.7 0.7 reshape.346.start
  15.4 1.3 dynamic_slice.31.seed
  16.6 0.6 sqrt_select_fusion
  17.3 11.9 %legendre.1.table = bf16[5,768,768]{2,1,0:T(8,128)(2,1)} custom-call(f32[3600]{0:T(1024)} %get-tuple-element.31.up, f32[3600]{0:T(1024)} %get-tuple-element.30.back, f32[3600]{0:T(1024)} %reshape.346.start, f32[5]{0:T(128)} %dynamic_slice.31.seed, f32[5]{0:T(128)} %fusion.50.order, f32[8,128]{1,0:T(8,128)} %get-tuple-element.39.x_ref, ...), custom_call_target="tpu_custom_call" | custom-call | tf_op jit(solution)/shard_map/legendre/pallas_call | solution.py:157
  29.2 8.1 %multiply_convert_fusion.1.table = bf16[1280,1536]{1,0:T(8,128)(2,1)} fusion(f32[1536]{0:T(1024)S(1)} %fusion.32, f32[1280]{0:T(1024)S(1)} %fusion.30, f32[1280]{0:T(1024)S(1)} %fusion.26, f32[1536]{0:T(1024)S(1)} %fusion.25), kind=kLoop, calls=%fused_computation.7 | loop fusion | flops 49152000 | bytes 3954688 | tf_op jit(solution)/shard_map/convert_element_type | solution.py:60
  37.3 6.8 %all-to-all-done.x_ref = bf16[16,6,96,128]{3,2,1,0:T(8,128)(2,1)S(1)} async-done(((bf16[16,6,96,128]{3,2,1,0:T(8,128)(2,1)}), bf16[16,6,96,128]{3,2,1,0:T(8,128)(2,1)S(1)}, u32[]{:S(2)}, u32[]{:S(2)}) %all-to-all-start) | async-done | bytes 2359328 | tf_op jit(solution)/shard_map/all_to_all | solution.py:342
  44.1 0.0 copy-start.1
  44.1 1.4 copy-done.1
  45.6 6.8 %fourier_forward.1 = bf16[7680,128]{1,0:T(8,128)(2,1)} custom-call(bf16[1280,1536]{1,0:T(8,128)(2,1)} %multiply_convert_fusion.1.table, bf16[16,6,96,128]{3,2,1,0:T(8,128)(2,1)} %copy-done.1), custom_call_target="tpu_custom_call" | custom-call | tf_op jit(solution)/shard_map/fourier_forward/pallas_call | solution.py:182
  52.3 6.2 %all-to-all-start.1 = ((bf16[128,30,2,128]{3,2,1,0:T(2,128)(2,1)}), bf16[128,30,2,128]{3,2,1,0:T(2,128)(2,1)S(1)}, u32[]{:S(2)}, u32[]{:S(2)}) async-start(bf16[128,30,2,128]{3,2,1,0:T(2,128)(2,1)} %bitcast.47), calls=%async_computation.1 | async-start | bytes 3932160 | tf_op jit(solution)/shard_map/all_to_all | solution.py:342
  58.6 4.0 %copy.10 = bf16[90,40,2,128]{3,2,1,0:T(2,128)(2,1)} copy(bf16[90,40,2,128]{3,2,0,1:T(2,128)(2,1)} %bitcast.50) | data formatting | bytes 3686400 | tf_op jit(solution)/shard_map/transpose | solution.py:370
  62.6 9.0 %copy.9 = bf16[5,768,768]{1,2,0:T(8,128)(2,1)} copy(bf16[5,768,768]{2,1,0:T(8,128)(2,1)} %legendre.1.table) | data formatting | bytes 11796480 | tf_op jit(solution)/shard_map/optimization_barrier | solution.py:365
  71.6 16.1 %all-to-all-done.1 = bf16[128,30,2,128]{3,2,1,0:T(2,128)(2,1)S(1)} async-done(((bf16[128,30,2,128]{3,2,1,0:T(2,128)(2,1)}), bf16[128,30,2,128]{3,2,1,0:T(2,128)(2,1)S(1)}, u32[]{:S(2)}, u32[]{:S(2)}) %all-to-all-start.1) | async-done | bytes 1966112 | tf_op jit(solution)/shard_map/all_to_all | solution.py:342
  87.6 0.0 copy-start.2
  87.6 1.3 copy-done.2
  88.9 7.3 %analyse.1 = bf16[8,10,96,128]{3,2,1,0:T(8,128)(2,1)} custom-call(bf16[5,768,768]{2,1,0:T(8,128)(2,1)} %legendre.1.table, bf16[7680,128]{1,0:T(8,128)(2,1)} %bitcast.44), custom_call_target="tpu_custom_call" | custom-call | tf_op jit(solution)/shard_map/analyse/pallas_call | solution.py:214
  96.2 3.6 %all-to-all-start.2 = ((bf16[8,10,96,128]{3,2,1,0:T(8,128)(2,1)}), bf16[8,10,96,128]{3,2,1,0:T(8,128)(2,1)S(1)}, u32[]{:S(2)}, u32[]{:S(2)}) async-start(bf16[8,10,96,128]{3,2,1,0:T(8,128)(2,1)} %analyse.1), calls=%async_computation.2 | async-start | bytes 3932160 | tf_op jit(solution)/shard_map/all_to_all | solution.py:342
  99.8 8.3 %multiply_convert_fusion.table = bf16[1536,1280]{1,0:T(8,128)(2,1)} fusion(f32[1536]{0:T(1024)S(1)} %fusion.32, f32[1280]{0:T(1024)S(1)} %fusion.30, f32[1280]{0:T(1024)S(1)} %fusion.26, f32[1536]{0:T(1024)S(1)} %fusion.25), kind=kLoop, calls=%fused_computation | loop fusion | flops 49152000 | bytes 3954688 | tf_op jit(solution)/shard_map/convert_element_type | solution.py:63
  108.0 16.9 %all-to-all-done.2 = bf16[8,10,96,128]{3,2,1,0:T(8,128)(2,1)S(1)} async-done(((bf16[8,10,96,128]{3,2,1,0:T(8,128)(2,1)}), bf16[8,10,96,128]{3,2,1,0:T(8,128)(2,1)S(1)}, u32[]{:S(2)}, u32[]{:S(2)}) %all-to-all-start.2) | async-done | bytes 1966112 | tf_op jit(solution)/shard_map/all_to_all | solution.py:342
  124.9 1.3 copy-done.3
  126.2 11.2 %mix.1 = (bf16[90,80,128]{2,1,0:T(8,128)(2,1)}, bf16[7680,128]{1,0:T(8,128)(2,1)}) custom-call(bf16[7680,128]{1,0:T(8,128)(2,1)} %bitcast.45, bf16[90,128,128]{2,1,0:T(8,128)(2,1)} %weights.1), custom_call_target="tpu_custom_call" | custom-call | tf_op jit(solution)/shard_map/mix/pallas_call | solution.py:254
  137.4 3.1 %fusion.51 = f32[90,128,128]{2,1,0:T(8,128)S(1)} fusion(bf16[90,80,128]{2,1,0:T(8,128)(2,1)} %bitcast.48, bf16[90,80,128]{2,1,0:T(8,128)(2,1)} %get-tuple-element.25), kind=kOutput, calls=%fused_computation.106 | convolution fusion | flops 235929600 | bytes 9584640 | tf_op jit(solution)/shard_map/lrc,lrd->lcd/dot_general | solution.py:379
  140.4 0.0 copy-start
  140.4 2.5 copy-done
  143.0 0.2 fusion.6
  143.2 0.3 collective-permute-start
  143.4 4.4 %all-to-all-start.3 = ((bf16[8,10,96,128]{3,2,1,0:T(8,128)(2,1)}), bf16[8,10,96,128]{3,2,1,0:T(8,128)(2,1)}, u32[]{:S(2)}, u32[]{:S(2)}) async-start(bf16[8,10,96,128]{3,2,1,0:T(8,128)(2,1)} %bitcast.10), calls=%async_computation.3 | async-start | bytes 3932160 | tf_op jit(solution)/shard_map/all_to_all | solution.py:342
  147.8 0.0 collective-permute-done
  147.8 2.5 bitcast_add_fusion
  150.3 1.0 fusion.7
  151.3 0.8 collective-permute-start.1
  152.2 18.4 %collective-permute-done.1 = bf16[90,2,2,8,128]{4,3,0,2,1:T(8,128)(2,1)} collective-permute-done((bf16[90,2,2,8,128]{4,3,0,2,1:T(8,128)(2,1)}, bf16[90,2,2,8,128]{4,3,0,2,1:T(8,128)(2,1)}, u32[]{:S(2)}, u32[]{:S(2)}) %collective-permute-start.1) | collective-permute-done | bytes 737312 | tf_op jit(solution)/shard_map/ppermute | solution.py:349
  170.5 2.4 bitcast_add_fusion.1
  172.9 1.4 all-to-all-done.3.x_ref
  174.3 7.0 %synthesise.1 = bf16[7680,128]{1,0:T(8,128)(2,1)} custom-call(bf16[5,768,768]{2,1,0:T(8,128)(2,1)} %bitcast.39, bf16[8,10,96,128]{3,2,1,0:T(8,128)(2,1)} %all-to-all-done.3.x_ref), custom_call_target="tpu_custom_call" | custom-call | tf_op jit(solution)/shard_map/synthesise/pallas_call | solution.py:290
  181.3 12.3 %all-to-all-start.4 = ((bf16[128,30,2,128]{3,2,1,0:T(2,128)(2,1)}), bf16[128,30,2,128]{3,2,1,0:T(2,128)(2,1)S(1)}, u32[]{:S(2)}, u32[]{:S(2)}) async-start(bf16[128,30,2,128]{3,2,1,0:T(2,128)(2,1)} %bitcast.43), calls=%async_computation.4 | async-start | bytes 3932160 | tf_op jit(solution)/shard_map/all_to_all | solution.py:342
  193.6 0.0 copy-done.5
  193.6 0.8 fusion.8
  194.4 2.9 %collective-permute-start.2 = (bf16[90,2,8,128]{3,2,0,1:T(8,128)(2,1)}, bf16[90,2,8,128]{3,2,0,1:T(8,128)(2,1)}, u32[]{:S(2)}, u32[]{:S(2)}) collective-permute-start(bf16[90,2,8,128]{3,2,0,1:T(8,128)(2,1)} %fusion.8), channel_id=1, source_target_pairs={{0,8},{1,9},{2,10},{3,11},{4,12},{5,13},{6,14},{7,15},{8,0},{9,1},... | collective-permute-start | bytes 1105928 | tf_op jit(solution)/shard_map/ppermute | solution.py:349
  197.3 28.7 %collective-permute-done.2 = bf16[90,2,8,128]{3,2,0,1:T(8,128)(2,1)} collective-permute-done((bf16[90,2,8,128]{3,2,0,1:T(8,128)(2,1)}, bf16[90,2,8,128]{3,2,0,1:T(8,128)(2,1)}, u32[]{:S(2)}, u32[]{:S(2)}) %collective-permute-start.2) | collective-permute-done | bytes 368672 | tf_op jit(solution)/shard_map/ppermute | solution.py:349
  226.0 1.9 bitcast_add_fusion.2
  227.9 0.0 all-to-all-done.4
  227.9 1.3 copy-done.4
  229.2 7.7 %fourier_backward.1 = bf16[16,6,96,128]{3,2,1,0:T(8,128)(2,1)} custom-call(bf16[1536,1280]{1,0:T(8,128)(2,1)} %multiply_convert_fusion.table, bf16[7680,128]{1,0:T(8,128)(2,1)} %bitcast.46), custom_call_target="tpu_custom_call" | custom-call | tf_op jit(solution)/shard_map/fourier_backward/pallas_call | solution.py:324
  236.8 4.6 %all-to-all-start.5 = ((bf16[16,6,96,128]{3,2,1,0:T(8,128)(2,1)}), bf16[16,6,96,128]{3,2,1,0:T(8,128)(2,1)S(1)}, u32[]{:S(2)}, u32[]{:S(2)}) async-start(bf16[16,6,96,128]{3,2,1,0:T(8,128)(2,1)} %fourier_backward.1), calls=%async_computation.5 | async-start | bytes 4718592 | tf_op jit(solution)/shard_map/all_to_all | solution.py:342
  241.5 0.0 copy-done.6
  241.5 3.5 %collective-permute-start.3 = (bf16[90,8,128]{2,1,0:T(8,128)(2,1)S(1)}, bf16[90,8,128]{2,1,0:T(8,128)(2,1)S(1)}, u32[]{:S(2)}, u32[]{:S(2)}) collective-permute-start(bf16[90,8,128]{2,1,0:T(8,128)(2,1)S(1)} %fusion.9), channel_id=1, source_target_pairs={{0,2},{1,3},{2,0},{3,1},{4,6},{5,7},{6,4},{7,5},{8,10},{9,11},{10,... | collective-permute-start | bytes 552968 | tf_op jit(solution)/shard_map/ppermute | solution.py:349
  245.0 30.9 %collective-permute-done.3 = bf16[90,8,128]{2,1,0:T(8,128)(2,1)S(1)} collective-permute-done((bf16[90,8,128]{2,1,0:T(8,128)(2,1)S(1)}, bf16[90,8,128]{2,1,0:T(8,128)(2,1)S(1)}, u32[]{:S(2)}, u32[]{:S(2)}) %collective-permute-start.3) | collective-permute-done | bytes 184352 | tf_op jit(solution)/shard_map/ppermute | solution.py:349
  275.9 0.8 bitcast_add_fusion.3
  276.7 0.0 all-to-all-done.5
  276.7 0.1 slice.8
  276.8 1.5 slice_bitcast_fusion
  (17 shorter events, 0.1 us)
Async XLA Ops:
  3.9 40.2 %all-to-all-start = ((bf16[16,6,96,128]{3,2,1,0:T(8,128)(2,1)}), bf16[16,6,96,128]{3,2,1,0:T(8,128)(2,1)S(1)}, u32[]{:S(2)}, u32[]{:S(2)}) async-start(bf16[16,6,96,128]{3,2,1,0:T(8,128)(2,1)} %bitcast.2), calls=%async_computation | async-start | bytes 4718592 | tf_op jit(solution)/shard_map/all_to_all | solution.py:342
  44.1 1.4 copy-start.1
  52.3 35.3 %all-to-all-start.1 = ((bf16[128,30,2,128]{3,2,1,0:T(2,128)(2,1)}), bf16[128,30,2,128]{3,2,1,0:T(2,128)(2,1)S(1)}, u32[]{:S(2)}, u32[]{:S(2)}) async-start(bf16[128,30,2,128]{3,2,1,0:T(2,128)(2,1)} %bitcast.47), calls=%async_computation.1 | async-start | bytes 3932160 | tf_op jit(solution)/shard_map/all_to_all | solution.py:342
  87.6 1.3 copy-start.2
  96.2 28.8 %all-to-all-start.2 = ((bf16[8,10,96,128]{3,2,1,0:T(8,128)(2,1)}), bf16[8,10,96,128]{3,2,1,0:T(8,128)(2,1)S(1)}, u32[]{:S(2)}, u32[]{:S(2)}) async-start(bf16[8,10,96,128]{3,2,1,0:T(8,128)(2,1)} %analyse.1), calls=%async_computation.2 | async-start | bytes 3932160 | tf_op jit(solution)/shard_map/all_to_all | solution.py:342
  124.9 1.3 copy-start.3
  140.4 2.5 copy-start
  143.2 4.7 %collective-permute-start = (bf16[90,2,2,2,8,128]{5,4,0,3,1,2:T(8,128)(2,1)S(1)}, bf16[90,2,2,2,8,128]{5,4,0,3,1,2:T(8,128)(2,1)}, u32[]{:S(2)}, u32[]{:S(2)}) collective-permute-start(bf16[90,2,2,2,8,128]{5,4,0,3,1,2:T(8,128)(2,1)S(1)} %fusion.6), channel_id=1, source_target_pairs={{0,1},{1,0},{2,3},{3,2},{4,5},{5,4},{6,7},{7,6},{8,9},{9,8},{10,11... | collective-permute-start | bytes 4423688 | tf_op jit(solution)/shard_map/ppermute | solution.py:349
  143.4 30.9 %all-to-all-start.3 = ((bf16[8,10,96,128]{3,2,1,0:T(8,128)(2,1)}), bf16[8,10,96,128]{3,2,1,0:T(8,128)(2,1)}, u32[]{:S(2)}, u32[]{:S(2)}) async-start(bf16[8,10,96,128]{3,2,1,0:T(8,128)(2,1)} %bitcast.10), calls=%async_computation.3 | async-start | bytes 3932160 | tf_op jit(solution)/shard_map/all_to_all | solution.py:342
  151.3 19.2 %collective-permute-start.1 = (bf16[90,2,2,8,128]{4,3,0,2,1:T(8,128)(2,1)}, bf16[90,2,2,8,128]{4,3,0,2,1:T(8,128)(2,1)}, u32[]{:S(2)}, u32[]{:S(2)}) collective-permute-start(bf16[90,2,2,8,128]{4,3,0,2,1:T(8,128)(2,1)} %fusion.7), channel_id=1, source_target_pairs={{0,4},{1,5},{2,6},{3,7},{4,0},{5,1},{6,2},{7,3},{8,12},{9,13},{10,... | collective-permute-start | bytes 2211848 | tf_op jit(solution)/shard_map/ppermute | solution.py:349
  172.9 20.8 %copy-start.5 = (f32[90,2,2,8,128]{4,3,0,2,1:T(8,128)S(1)}, f32[90,2,2,8,128]{4,3,0,2,1:T(8,128)}, u32[]{:S(2)}) copy-start(f32[90,2,2,8,128]{4,3,0,2,1:T(8,128)} %bitcast_add_fusion.1) | copy-start | bytes 4423684
  181.3 46.6 %all-to-all-start.4 = ((bf16[128,30,2,128]{3,2,1,0:T(2,128)(2,1)}), bf16[128,30,2,128]{3,2,1,0:T(2,128)(2,1)S(1)}, u32[]{:S(2)}, u32[]{:S(2)}) async-start(bf16[128,30,2,128]{3,2,1,0:T(2,128)(2,1)} %bitcast.43), calls=%async_computation.4 | async-start | bytes 3932160 | tf_op jit(solution)/shard_map/all_to_all | solution.py:342
  194.4 31.5 %collective-permute-start.2 = (bf16[90,2,8,128]{3,2,0,1:T(8,128)(2,1)}, bf16[90,2,8,128]{3,2,0,1:T(8,128)(2,1)}, u32[]{:S(2)}, u32[]{:S(2)}) collective-permute-start(bf16[90,2,8,128]{3,2,0,1:T(8,128)(2,1)} %fusion.8), channel_id=1, source_target_pairs={{0,8},{1,9},{2,10},{3,11},{4,12},{5,13},{6,14},{7,15},{8,0},{9,1},... | collective-permute-start | bytes 1105928 | tf_op jit(solution)/shard_map/ppermute | solution.py:349
  227.9 1.3 copy-start.4
  229.2 12.3 %copy-start.6 = (f32[90,2,8,128]{3,2,0,1:T(8,128)S(1)}, f32[90,2,8,128]{3,2,0,1:T(8,128)}, u32[]{:S(2)}) copy-start(f32[90,2,8,128]{3,2,0,1:T(8,128)} %bitcast_add_fusion.2) | copy-start | bytes 2211844
  236.8 39.9 %all-to-all-start.5 = ((bf16[16,6,96,128]{3,2,1,0:T(8,128)(2,1)}), bf16[16,6,96,128]{3,2,1,0:T(8,128)(2,1)S(1)}, u32[]{:S(2)}, u32[]{:S(2)}) async-start(bf16[16,6,96,128]{3,2,1,0:T(8,128)(2,1)} %fourier_backward.1), calls=%async_computation.5 | async-start | bytes 4718592 | tf_op jit(solution)/shard_map/all_to_all | solution.py:342
  241.5 34.4 %collective-permute-start.3 = (bf16[90,8,128]{2,1,0:T(8,128)(2,1)S(1)}, bf16[90,8,128]{2,1,0:T(8,128)(2,1)S(1)}, u32[]{:S(2)}, u32[]{:S(2)}) collective-permute-start(bf16[90,8,128]{2,1,0:T(8,128)(2,1)S(1)} %fusion.9), channel_id=1, source_target_pairs={{0,2},{1,3},{2,0},{3,1},{4,6},{5,7},{6,4},{7,5},{8,10},{9,11},{10,... | collective-permute-start | bytes 552968 | tf_op jit(solution)/shard_map/ppermute | solution.py:349

commit v3 on v2

--- a/solution.py
+++ b/solution.py
@@ -21,6 +21,7 @@
 SLOT = 6
 USED = ROWS // SLOT
 PAD = 96
+ODD = PAD + 1
 ORDERS = M // (LATS * LONS)
 Q = 2 * ORDERS
 CHUNK = Q * SLOT
@@ -30,6 +31,14 @@
 
 F32 = jnp.float32
 BF16 = jnp.bfloat16
+
+
+def limit(mebibytes):
+    return pltpu.CompilerParams(vmem_limit_bytes=mebibytes << 20)
+
+
+def far(x):
+    return pltpu.with_memory_space_constraint(x, pltpu.HBM)
 
 
 def cosine_values(position, order, part):
@@ -160,6 +169,7 @@
         in_specs=[smem] * 5 + [vmem] * 3,
         out_specs=vmem,
         scratch_shapes=[pltpu.VMEM((ORDERS, 8 * BLOCK, 128), F32)],
+        compiler_params=limit(16),
         name="legendre",
     )(up.reshape(-1), back.reshape(-1), start.reshape(-1), seed, order, x, root, log_sine)
 
@@ -177,18 +187,19 @@
 
 
 def fourier_forward(table, x):
-    steps = 2
+    steps = 4
     rows = 2 * M // steps
     return pl.pallas_call(
         forward_kernel,
         grid=(steps,),
-        out_shape=jax.ShapeDtypeStruct((2 * M * SLOT, C), BF16),
+        out_shape=pltpu.HBM((2 * M * SLOT, C), BF16),
         in_specs=[
             pl.BlockSpec((rows, LONS * PAD), lambda g: (g, 0)),
             pl.BlockSpec((LONS, SLOT, PAD, C), lambda g: (0, 0, 0, 0)),
         ],
         out_specs=pl.BlockSpec((rows * SLOT, C), lambda g: (g, 0)),
         scratch_shapes=[pltpu.VMEM((rows * SLOT, C), F32)],
+        compiler_params=limit(24),
         name="fourier_forward",
     )(table, x)
 
@@ -214,13 +225,14 @@
     return pl.pallas_call(
         analyse_kernel,
         grid=(ORDERS,),
-        out_shape=jax.ShapeDtypeStruct((LATS, Q, PAD, C), BF16),
+        out_shape=pltpu.HBM((LATS, Q, PAD, C), BF16),
         in_specs=[
             pl.BlockSpec((1, LATS * PAD, DEVICES * SLOT), lambda g: (g, 0, 0)),
             pl.BlockSpec((DEVICES * CHUNK, C), lambda g: (0, 0)),
         ],
         out_specs=pl.BlockSpec((LATS, 2, PAD, C), lambda g: (0, g, 0, 0)),
         scratch_shapes=[pltpu.VMEM((DEVICES * CHUNK, C), F32)],
+        compiler_params=limit(22),
         name="analyse",
     )(table, x)
 
@@ -228,14 +240,18 @@
 def mix_kernel(x_ref, weights, gathered, out_ref, wide, made):
     g = pl.program_id(0)
     each = weights.shape[0]
+    slabs = LATS * Q
 
     @pl.when(g == 0)
     def _():
-        wide[...] = x_ref[...].astype(F32)
-        made[...] = jnp.zeros_like(made)
+        for slab in range(slabs):
+            wide[slab * ODD : slab * ODD + PAD, :] = x_ref[
+                slab * PAD : slab * PAD + PAD, :
+            ].astype(F32)
+            made[slab * ODD + PAD - 8 : slab * ODD + PAD, :] = jnp.zeros((8, C), F32)
 
     for offset in range(each):
-        rows = pl.ds(g * each + offset, LATS * Q, stride=PAD)
+        rows = pl.ds(g * each + offset, slabs, stride=ODD)
         part = wide[rows, :].astype(BF16)
         gathered[offset] = part
         made[rows, :] = lax.dot_general(
@@ -244,7 +260,10 @@
 
     @pl.when(g == pl.num_programs(0) - 1)
     def _():
-        out_ref[...] = made[...].astype(BF16)
+        for slab in range(slabs):
+            out_ref[slab * PAD : slab * PAD + PAD, :] = made[
+                slab * ODD : slab * ODD + PAD, :
+            ].astype(BF16)
 
 
 def mix(x, weights):
@@ -255,8 +274,8 @@
         mix_kernel,
         grid=(steps,),
         out_shape=(
-            jax.ShapeDtypeStruct((DEGREES, LATS * Q, C), BF16),
-            jax.ShapeDtypeStruct((whole, C), BF16),
+            pltpu.HBM((DEGREES, LATS * Q, C), BF16),
+            pltpu.HBM((whole, C), BF16),
         ),
         in_specs=[
             pl.BlockSpec((whole, C), lambda g: (0, 0)),
@@ -266,7 +285,8 @@
             pl.BlockSpec((each, LATS * Q, C), lambda g: (g, 0, 0)),
             pl.BlockSpec((whole, C), lambda g: (0, 0)),
         ),
-        scratch_shapes=[pltpu.VMEM((whole, C), F32), pltpu.VMEM((whole, C), F32)],
+        scratch_shapes=[pltpu.VMEM((LATS * Q * ODD, C), F32)] * 2,
+        compiler_params=limit(26),
         name="mix",
     )(x, weights)
 
@@ -290,13 +310,14 @@
     return pl.pallas_call(
         synthesise_kernel,
         grid=(ORDERS,),
-        out_shape=jax.ShapeDtypeStruct((DEVICES * CHUNK, C), BF16),
+        out_shape=pltpu.HBM((DEVICES * CHUNK, C), BF16),
         in_specs=[
             pl.BlockSpec((1, DEVICES * SLOT, LATS * PAD), lambda g: (g, 0, 0)),
             pl.BlockSpec((LATS, 2, PAD, C), lambda g: (0, g, 0, 0)),
         ],
         out_specs=pl.BlockSpec((DEVICES * CHUNK, C), lambda g: (0, 0)),
         scratch_shapes=[pltpu.VMEM((DEVICES * CHUNK, C), F32)],
+        compiler_params=limit(22),
         name="synthesise",
     )(table, x)
 
@@ -324,7 +345,7 @@
     return pl.pallas_call(
         backward_kernel,
         grid=(steps,),
-        out_shape=jax.ShapeDtypeStruct((LONS, SLOT, PAD, C), BF16),
+        out_shape=pltpu.HBM((LONS, SLOT, PAD, C), BF16),
         in_specs=[
             pl.BlockSpec((each * PAD, 2 * M), lambda g: (g, 0)),
             pl.BlockSpec((DEVICES * CHUNK, C), lambda g: (0, 0)),
@@ -334,6 +355,7 @@
             pltpu.VMEM((DEVICES * CHUNK, C), F32),
             pltpu.VMEM((2 * M, SLOT * C), BF16),
         ],
+        compiler_params=limit(22),
         name="fourier_backward",
     )(table, x)
 
@@ -342,12 +364,30 @@
     return lax.all_to_all(x, axis, split_axis=0, concat_axis=0, tiled=True)
 
 
-def halve(held, bit, axis):
-    mine = (lax.axis_index("lon") >> bit) & 1
-    keep = lax.dynamic_index_in_dim(held, mine, axis, keepdims=False)
-    give = lax.dynamic_index_in_dim(held, 1 - mine, axis, keepdims=False)
-    got = lax.ppermute(give.astype(BF16), "lon", [(k, k ^ (1 << bit)) for k in range(LONS)])
-    return keep.astype(F32) + got.astype(F32)
+def share_cores(held):
+    core = lax.axis_index("lon") & 1
+    held = held.reshape(DEGREES, LONS // 2, 2, C // LONS, C)
+    keep = lax.dynamic_index_in_dim(held, core, 2, keepdims=False)
+    give = lax.dynamic_index_in_dim(held, 1 - core, 2, keepdims=False).astype(BF16)
+    return keep + lax.ppermute(give, "lon", [(k, k ^ 1) for k in range(LONS)]).astype(F32)
+
+
+def share_columns(held):
+    z = lax.axis_index("lon") >> 2
+    held = held.reshape(DEGREES, 4, 2, C // LONS, C)
+    got = []
+    for step in (1, 3, 2):
+        give = lax.dynamic_index_in_dim(held, (z + step) % 4, 1, keepdims=False).astype(BF16)
+        pairs = [(k, (k + 4 * step) % LONS) for k in range(LONS)]
+        got.append(lax.ppermute(give, "lon", pairs))
+    return lax.dynamic_index_in_dim(held, z, 1, keepdims=False), got
+
+
+def share_pair(held):
+    y = (lax.axis_index("lon") >> 1) & 1
+    keep = lax.dynamic_index_in_dim(held, y, 1, keepdims=False)
+    give = lax.dynamic_index_in_dim(held, 1 - y, 1, keepdims=False).astype(BF16)
+    return keep + lax.ppermute(give, "lon", [(k, k ^ 2) for k in range(LONS)]).astype(F32)
 
 
 def cells(x):
@@ -364,29 +404,32 @@
     legendre = legendre_table(first_order)
     rows, forward, legendre = lax.optimization_barrier((rows, forward, legendre))
 
-    spectra = fourier_forward(forward, rows)
+    spectra = fourier_forward(far(forward), rows)
     columns = exchange(cells(spectra), both).reshape(DEVICES * CHUNK, C)
     turned = jnp.swapaxes(legendre, 1, 2)
     stored = spectrum.reshape(LATS * ORDERS, DEGREES, 2, C).transpose(1, 0, 2, 3)
     stored = stored.reshape(DEGREES, LATS * Q, C)
     columns, turned, stored = lax.optimization_barrier((columns, turned, stored))
 
-    analysed = exchange(analyse(legendre, columns), "lat").reshape(LATS * Q * PAD, C)
+    analysed = exchange(analyse(far(legendre), columns), "lat").reshape(LATS * Q * PAD, C)
     analysed, backward = lax.optimization_barrier((analysed, backward))
-    gathered, spec_local = mix(analysed, weights)
+    gathered, spec_local = mix(analysed, far(weights))
     spec_grad = exchange(spec_local.reshape(LATS, Q, PAD, C), "lat")
 
     held = jnp.einsum("lrc,lrd->lcd", stored, gathered, preferred_element_type=F32)
-    held = held.reshape(DEGREES, 2, 2, 2, 2, C // LONS, C)
-    held = halve(halve(held, 0, 4), 2, 2)
+    held = share_cores(held)
+    held, got = share_columns(held)
     spec_grad, held = lax.optimization_barrier((spec_grad, held))
 
-    row_block = exchange(cells(synthesise(turned, spec_grad)), both)
-    held = halve(held, 3, 1)
-    row_block, held = lax.optimization_barrier((row_block, held))
-    grid_part = fourier_backward(backward, row_block.reshape(DEVICES * CHUNK, C))
+    row_block = synthesise(far(turned), spec_grad)
+    row_block = exchange(cells(row_block), both)
+    row_block, held, *got = lax.optimization_barrier((row_block, held, *got))
+    for part in got:
+        held = held + part.astype(F32)
+    grid_part = fourier_backward(far(backward), row_block.reshape(DEVICES * CHUNK, C))
     grid_part = exchange(grid_part, "lon")
-    weight_grad = halve(held, 1, 1)
+    weight_grad = share_pair(held)
+    grid_part, weight_grad = lax.optimization_barrier((grid_part, weight_grad))
     grad_in = grid_part[:USED].reshape(ROWS, PAD, C)[:, :COLS]
     return jnp.swapaxes(grad_in, 1, 2)[None], weight_grad
 

time: 280 us -> 277 us (0.989)
  waiting for transfers between devices: 119 us -> 128 us
  Pallas kernels: 51.8 us -> 45.3 us
  other arithmetic: 26.7 us -> 22.5 us
    all_to_all x6, waiting for transfers between devices: 41.3 us -> 65.1 us  [exchange(): return lax.all_to_all(x, axis, split_axis=0, concat_axis=0, tiled=True)]
    ppermute x4 -> x5, waiting for transfers between devices: 77.9 us -> 62.8 us  [the longest x3 34 us: share_columns(): got.append(lax.ppermute(give, 'lon', pairs))]
    pallas_call x5, Pallas kernels: 39.8 us -> 36.1 us  [the longest x1 9.46 us: mix(): pl.pallas_call(mix_kernel, grid=(steps,), out_shape=(pltpu.HBM((DEGREES,...]
    add x4 -> x3, other arithmetic: 7.58 us -> 5.78 us  [the longest x1 2.78 us: share_cores(): keep + lax.ppermute(give, 'lon', [(k, k ^ 1) for k in range(LONS)]).astyp...]
    ppermute x4 -> x5, starting transfers between devices: 7.46 us -> 8.54 us  [the longest x3 4.95 us: share_columns(): got.append(lax.ppermute(give, 'lon', pairs))]
    unnamed x14 -> x12, local copies, waits for them, and re-layouts: 7.78 us -> 7.5 us
  transfers between devices with their start and end apart: 10 -> 11, of which waited for: 7 -> 7; matrix products, arithmetic and copies ran while one was open for 16% -> 14% of each run, Pallas kernels for 4% -> 3%
where the time goes in v3:
time: 277 us; the launch traced here: 276 us
  waiting for transfers between devices  128 us (46%)
  starting transfers between devices  47.5 us (17%)
  Pallas kernels  45.3 us (16%)
  local copies, waits for them, and re-layouts  29 us (10%)
  other arithmetic  22.5 us (8%)
    all_to_all x6, waiting for transfers between devices, exchange(): return lax.all_to_all(x, axis, split_axis=0, concat_axis=0, tiled=True)  65.1 us
    all_to_all x6, starting transfers between devices, exchange(): return lax.all_to_all(x, axis, split_axis=0, concat_axis=0, tiled=True)  39 us
    ppermute x3, waiting for transfers between devices, share_columns(): got.append(lax.ppermute(give, 'lon', pairs))  34 us
    ppermute x1, waiting for transfers between devices, share_pair(): lax.ppermute(give, 'lon', [(k, k ^ 2) for k in range(LONS)]).astype(F32)  28.8 us
    pallas_call x1, Pallas kernels, mix(): pl.pallas_call(mix_kernel, grid=(steps,), out_shape=(pltpu.HBM((DEGREES,...  9.46 us
    pallas_call x1, Pallas kernels, legendre_table(): pl.pallas_call(legendre_kernel, out_shape=jax.ShapeDtypeStruct((ORDERS, L...  9.14 us
    optimization_barrier x1, local copies, waits for them, and re-layouts, on_device(): lax.optimization_barrier((rows, forward, legendre))  8.99 us
    convert_element_type x1, other arithmetic, fourier_tables(): backward = (cosine_values(position, order, part) * live).astype(BF16)  8.24 us
  transfers between devices with their start and end apart: 11, of which 7 were waited for; matrix products, arithmetic and copies ran while one was open for 14% of the time, Pallas kernels for 3%

profile of v3, /device:TPU:0, one launch (start us, length us, event | category | flops | bytes accessed | tf_op | source)
XLA Modules:
  0.0 275.6 jit_solution(14211163443797527108)
XLA Ops:
  0.6 3.3 %pad.4 = bf16[96,96,128]{2,1,0:T(8,128)(2,1)} pad(bf16[90,90,128]{2,1,0:T(8,128)(2,1)} %bitcast.53, bf16[]{:T(256)} %constant.238.clone.1), padding=0_6x0_6x0_0 | pad | bytes 4432898 | tf_op jit(solution)/shard_map/jit(_pad)/pad | solution.py:401
  3.9 8.2 %all-to-all-start = ((bf16[16,6,96,128]{3,2,1,0:T(8,128)(2,1)}), bf16[16,6,96,128]{3,2,1,0:T(8,128)(2,1)S(1)}, u32[]{:S(2)}, u32[]{:S(2)}) async-start(bf16[16,6,96,128]{3,2,1,0:T(8,128)(2,1)} %bitcast.46), calls=%async_computation | async-start | bytes 4718592 | tf_op jit(solution)/shard_map/all_to_all | solution.py:364
  12.2 0.1 sqrt_select_fusion.2
  12.3 0.1 fusion.50.sine_ref
  12.4 0.1 fusion.11
  12.5 0.1 gt.23
  12.6 0.1 subtract_multiply_fusion
  12.6 0.1 mul.331
  12.7 0.1 mul.333
  12.8 0.1 sub.126
  12.9 0.1 div.98
  13.0 0.1 reshape.351.start
  13.0 0.8 dynamic_slice.30.seed
  13.8 9.1 %legendre.1.table = bf16[5,768,768]{2,1,0:T(8,128)(2,1)S(1)} custom-call(f32[3600]{0:T(1024)S(1)} %get-tuple-element.44.up, f32[3600]{0:T(1024)S(1)} %get-tuple-element.43.back, f32[3600]{0:T(1024)S(1)} %reshape.351.start, f32[5]{0:T(128)S(1)} %dynamic_slice.30.seed, f32[5]{0:T(128)S(1)} %fusion.51.order, f32[8,128]{1,0:T(8,128)S(1)} %get-tuple-element.52.x_ref, ...), custom_call_target="tpu_custom_call" | custom-call | tf_op jit(solution)/shard_map/legendre/pallas_call | solution.py:166
  23.0 0.0 copy-start
  23.0 2.5 copy-done
  25.5 8.1 %multiply_convert_fusion.1.table = bf16[1280,1536]{1,0:T(8,128)(2,1)} fusion(f32[1536]{0:T(1024)S(1)} %fusion.33, f32[1280]{0:T(1024)S(1)} %fusion.31, f32[1280]{0:T(1024)S(1)} %fusion.27, f32[1536]{0:T(1024)S(1)} %fusion.26), kind=kLoop, calls=%fused_computation.7 | loop fusion | flops 49152000 | bytes 3954688 | tf_op jit(solution)/shard_map/convert_element_type | solution.py:69
  33.6 10.6 %all-to-all-done.x_ref = bf16[16,6,96,128]{3,2,1,0:T(8,128)(2,1)S(1)} async-done(((bf16[16,6,96,128]{3,2,1,0:T(8,128)(2,1)}), bf16[16,6,96,128]{3,2,1,0:T(8,128)(2,1)S(1)}, u32[]{:S(2)}, u32[]{:S(2)}) %all-to-all-start) | async-done | bytes 2359328 | tf_op jit(solution)/shard_map/all_to_all | solution.py:364
  44.2 6.4 %fourier_forward.1 = bf16[7680,128]{1,0:T(8,128)(2,1)} custom-call(bf16[1280,1536]{1,0:T(8,128)(2,1)} %multiply_convert_fusion.1.table, bf16[16,6,96,128]{3,2,1,0:T(8,128)(2,1)S(1)} %all-to-all-done.x_ref), custom_call_target="tpu_custom_call" | custom-call | tf_op jit(solution)/shard_map/fourier_forward/pallas_call | solution.py:192
  50.5 6.2 %all-to-all-start.1 = ((bf16[128,30,2,128]{3,2,1,0:T(2,128)(2,1)}), bf16[128,30,2,128]{3,2,1,0:T(2,128)(2,1)S(1)}, u32[]{:S(2)}, u32[]{:S(2)}) async-start(bf16[128,30,2,128]{3,2,1,0:T(2,128)(2,1)} %bitcast.49), calls=%async_computation.1 | async-start | bytes 3932160 | tf_op jit(solution)/shard_map/all_to_all | solution.py:364
  56.7 4.0 %copy.9 = bf16[90,40,2,128]{3,2,1,0:T(2,128)(2,1)} copy(bf16[90,40,2,128]{3,2,0,1:T(2,128)(2,1)} %bitcast.55) | data formatting | bytes 3686400 | tf_op jit(solution)/shard_map/transpose | solution.py:410
  60.7 9.0 %copy.8 = bf16[5,768,768]{1,2,0:T(8,128)(2,1)} copy(bf16[5,768,768]{2,1,0:T(8,128)(2,1)} %copy-done) | data formatting | bytes 11796480 | tf_op jit(solution)/shard_map/optimization_barrier | solution.py:405
  69.7 16.1 %all-to-all-done.1 = bf16[128,30,2,128]{3,2,1,0:T(2,128)(2,1)S(1)} async-done(((bf16[128,30,2,128]{3,2,1,0:T(2,128)(2,1)}), bf16[128,30,2,128]{3,2,1,0:T(2,128)(2,1)S(1)}, u32[]{:S(2)}, u32[]{:S(2)}) %all-to-all-start.1) | async-done | bytes 1966112 | tf_op jit(solution)/shard_map/all_to_all | solution.py:364
  85.8 6.6 %analyse.1 = bf16[8,10,96,128]{3,2,1,0:T(8,128)(2,1)} custom-call(bf16[5,768,768]{2,1,0:T(8,128)(2,1)} %copy-done, bf16[7680,128]{1,0:T(8,128)(2,1)S(1)} %bitcast.40), custom_call_target="tpu_custom_call" | custom-call | tf_op jit(solution)/shard_map/analyse/pallas_call | solution.py:225
  92.4 3.6 %all-to-all-start.2 = ((bf16[8,10,96,128]{3,2,1,0:T(8,128)(2,1)}), bf16[8,10,96,128]{3,2,1,0:T(8,128)(2,1)S(1)}, u32[]{:S(2)}, u32[]{:S(2)}) async-start(bf16[8,10,96,128]{3,2,1,0:T(8,128)(2,1)} %analyse.1), calls=%async_computation.2 | async-start | bytes 3932160 | tf_op jit(solution)/shard_map/all_to_all | solution.py:364
  96.0 8.2 %multiply_convert_fusion.table = bf16[1536,1280]{1,0:T(8,128)(2,1)} fusion(f32[1536]{0:T(1024)S(1)} %fusion.33, f32[1280]{0:T(1024)S(1)} %fusion.31, f32[1280]{0:T(1024)S(1)} %fusion.27, f32[1536]{0:T(1024)S(1)} %fusion.26), kind=kLoop, calls=%fused_computation | loop fusion | flops 49152000 | bytes 3954688 | tf_op jit(solution)/shard_map/convert_element_type | solution.py:72
  104.3 16.9 %all-to-all-done.2 = bf16[8,10,96,128]{3,2,1,0:T(8,128)(2,1)S(1)} async-done(((bf16[8,10,96,128]{3,2,1,0:T(8,128)(2,1)}), bf16[8,10,96,128]{3,2,1,0:T(8,128)(2,1)S(1)}, u32[]{:S(2)}, u32[]{:S(2)}) %all-to-all-start.2) | async-done | bytes 1966112 | tf_op jit(solution)/shard_map/all_to_all | solution.py:364
  121.2 0.0 copy-start.3
  121.2 9.5 %mix.1 = (bf16[90,80,128]{2,1,0:T(8,128)(2,1)}, bf16[7680,128]{1,0:T(8,128)(2,1)}) custom-call(bf16[7680,128]{1,0:T(8,128)(2,1)S(1)} %bitcast.41, bf16[90,128,128]{2,1,0:T(8,128)(2,1)} %weights.1), custom_call_target="tpu_custom_call" | custom-call | tf_op jit(solution)/shard_map/mix/pallas_call | solution.py:273
  130.7 0.0 copy-done.3
  130.7 2.5 fusion.52
  133.2 0.0 copy-start.1
  133.2 2.5 copy-done.1
  135.7 0.3 fusion.6
  136.0 0.1 collective-permute-start
  136.1 3.9 %all-to-all-start.3 = ((bf16[8,10,96,128]{3,2,1,0:T(8,128)(2,1)}), bf16[8,10,96,128]{3,2,1,0:T(8,128)(2,1)S(1)}, u32[]{:S(2)}, u32[]{:S(2)}) async-start(bf16[8,10,96,128]{3,2,1,0:T(8,128)(2,1)} %bitcast.54), calls=%async_computation.3 | async-start | bytes 3932160 | tf_op jit(solution)/shard_map/all_to_all | solution.py:364
  140.0 0.0 collective-permute-done
  140.0 2.8 %bitcast_add_fusion = f32[90,8,8,128]{3,2,1,0:T(8,128)S(1)} fusion(bf16[90,8,8,128]{3,2,1,0:T(8,128)(2,1)} %collective-permute-done, f32[90,8,2,8,128]{4,3,2,1,0:T(8,128)} %bitcast.45, s32[]{:T(128)S(6)} %select_n.230), kind=kLoop, calls=%fused_computation.14 | loop fusion | flops 1474560 | bytes 7372804 | tf_op jit(solution)/shard_map/add | solution.py:372
  142.8 0.2 copy.10
  143.0 0.0 copy-start.2
  143.0 1.6 copy-done.2
  144.6 21.5 %all-to-all-done.3.x_ref = bf16[8,10,96,128]{3,2,1,0:T(8,128)(2,1)S(1)} async-done(((bf16[8,10,96,128]{3,2,1,0:T(8,128)(2,1)}), bf16[8,10,96,128]{3,2,1,0:T(8,128)(2,1)S(1)}, u32[]{:S(2)}, u32[]{:S(2)}) %all-to-all-start.3) | async-done | bytes 1966112 | tf_op jit(solution)/shard_map/all_to_all | solution.py:364
  166.2 6.8 %synthesise.1 = bf16[7680,128]{1,0:T(8,128)(2,1)} custom-call(bf16[5,768,768]{2,1,0:T(8,128)(2,1)} %bitcast.43, bf16[8,10,96,128]{3,2,1,0:T(8,128)(2,1)S(1)} %all-to-all-done.3.x_ref), custom_call_target="tpu_custom_call" | custom-call | tf_op jit(solution)/shard_map/synthesise/pallas_call | solution.py:310
  172.9 13.0 %all-to-all-start.4 = ((bf16[128,30,2,128]{3,2,1,0:T(2,128)(2,1)}), bf16[128,30,2,128]{3,2,1,0:T(2,128)(2,1)S(1)}, u32[]{:S(2)}, u32[]{:S(2)}) async-start(bf16[128,30,2,128]{3,2,1,0:T(2,128)(2,1)} %bitcast.48), calls=%async_computation.4 | async-start | bytes 3932160 | tf_op jit(solution)/shard_map/all_to_all | solution.py:364
  186.0 1.7 fusion.9
  187.7 1.1 collective-permute-start.1
  188.8 2.2 collective-permute-start.2
  191.0 1.6 collective-permute-start.3
  192.6 25.9 %collective-permute-done.1 = bf16[90,2,8,128]{3,2,0,1:T(8,128)(2,1)S(1)} collective-permute-done((bf16[90,2,8,128]{3,2,0,1:T(8,128)(2,1)S(1)}, bf16[90,2,8,128]{3,2,0,1:T(8,128)(2,1)S(1)}, u32[]{:S(2)}, u32[]{:S(2)}) %collective-permute-start.1) | collective-permute-done | bytes 368672 | tf_op jit(solution)/shard_map/ppermute | solution.py:382
  218.6 0.0 collective-permute-done.2
  218.6 8.1 %collective-permute-done.3 = bf16[90,2,8,128]{3,2,0,1:T(8,128)(2,1)} collective-permute-done((bf16[90,2,8,128]{3,2,0,1:T(8,128)(2,1)S(1)}, bf16[90,2,8,128]{3,2,0,1:T(8,128)(2,1)}, u32[]{:S(2)}, u32[]{:S(2)}) %collective-permute-start.3) | collective-permute-done | bytes 368672 | tf_op jit(solution)/shard_map/ppermute | solution.py:382
  226.7 0.0 all-to-all-done.4
  226.7 6.9 %fourier_backward.1 = bf16[16,6,96,128]{3,2,1,0:T(8,128)(2,1)} custom-call(bf16[1536,1280]{1,0:T(8,128)(2,1)} %multiply_convert_fusion.table, bf16[7680,128]{1,0:T(8,128)(2,1)S(1)} %bitcast.42), custom_call_target="tpu_custom_call" | custom-call | tf_op jit(solution)/shard_map/fourier_backward/pallas_call | solution.py:345
  233.6 0.0 copy-done.5
  233.6 4.2 %all-to-all-start.5 = ((bf16[16,6,96,128]{3,2,1,0:T(8,128)(2,1)}), bf16[16,6,96,128]{3,2,1,0:T(8,128)(2,1)S(1)}, u32[]{:S(2)}, u32[]{:S(2)}) async-start(bf16[16,6,96,128]{3,2,1,0:T(8,128)(2,1)} %fourier_backward.1), calls=%async_computation.5 | async-start | bytes 4718592 | tf_op jit(solution)/shard_map/all_to_all | solution.py:364
  237.8 1.2 convert_add_fusion
  239.0 0.0 copy-start.4
  239.0 0.9 copy-done.4
  239.9 3.5 %collective-permute-start.4 = (bf16[90,8,128]{2,1,0:T(8,128)(2,1)S(1)}, bf16[90,8,128]{2,1,0:T(8,128)(2,1)S(1)}, u32[]{:S(2)}, u32[]{:S(2)}) collective-permute-start(bf16[90,8,128]{2,1,0:T(8,128)(2,1)S(1)} %fusion.10), channel_id=1, source_target_pairs={{0,2},{1,3},{2,0},{3,1},{4,6},{5,7},{6,4},{7,5},{8,10},{9,11},{10,... | collective-permute-start | bytes 552968 | tf_op jit(solution)/shard_map/ppermute | solution.py:390
  243.4 28.8 %collective-permute-done.4 = bf16[90,8,128]{2,1,0:T(8,128)(2,1)S(1)} collective-permute-done((bf16[90,8,128]{2,1,0:T(8,128)(2,1)S(1)}, bf16[90,8,128]{2,1,0:T(8,128)(2,1)S(1)}, u32[]{:S(2)}, u32[]{:S(2)}) %collective-permute-start.4) | collective-permute-done | bytes 184352 | tf_op jit(solution)/shard_map/ppermute | solution.py:390
  272.2 1.8 bitcast_add_fusion.1
  274.0 0.0 all-to-all-done.5
  274.0 0.1 slice.6
  274.1 1.5 slice_bitcast_fusion
  (17 shorter events, 0.2 us)
Async XLA Ops:
  3.9 40.2 %all-to-all-start = ((bf16[16,6,96,128]{3,2,1,0:T(8,128)(2,1)}), bf16[16,6,96,128]{3,2,1,0:T(8,128)(2,1)S(1)}, u32[]{:S(2)}, u32[]{:S(2)}) async-start(bf16[16,6,96,128]{3,2,1,0:T(8,128)(2,1)} %bitcast.46), calls=%async_computation | async-start | bytes 4718592 | tf_op jit(solution)/shard_map/all_to_all | solution.py:364
  23.0 2.5 copy-start
  50.5 35.3 %all-to-all-start.1 = ((bf16[128,30,2,128]{3,2,1,0:T(2,128)(2,1)}), bf16[128,30,2,128]{3,2,1,0:T(2,128)(2,1)S(1)}, u32[]{:S(2)}, u32[]{:S(2)}) async-start(bf16[128,30,2,128]{3,2,1,0:T(2,128)(2,1)} %bitcast.49), calls=%async_computation.1 | async-start | bytes 3932160 | tf_op jit(solution)/shard_map/all_to_all | solution.py:364
  92.4 28.8 %all-to-all-start.2 = ((bf16[8,10,96,128]{3,2,1,0:T(8,128)(2,1)}), bf16[8,10,96,128]{3,2,1,0:T(8,128)(2,1)S(1)}, u32[]{:S(2)}, u32[]{:S(2)}) async-start(bf16[8,10,96,128]{3,2,1,0:T(8,128)(2,1)} %analyse.1), calls=%async_computation.2 | async-start | bytes 3932160 | tf_op jit(solution)/shard_map/all_to_all | solution.py:364
  121.2 9.5 %copy-start.3 = (bf16[90,40,2,128]{3,2,1,0:T(2,128)(2,1)S(1)}, bf16[90,40,2,128]{3,2,1,0:T(2,128)(2,1)}, u32[]{:S(2)}) copy-start(bf16[90,40,2,128]{3,2,1,0:T(2,128)(2,1)} %copy.9) | copy-start | bytes 5529604
  133.2 2.5 copy-start.1
  136.0 4.0 %collective-permute-start = (bf16[90,8,8,128]{3,2,1,0:T(8,128)(2,1)S(1)}, bf16[90,8,8,128]{3,2,1,0:T(8,128)(2,1)}, u32[]{:S(2)}, u32[]{:S(2)}) collective-permute-start(bf16[90,8,8,128]{3,2,1,0:T(8,128)(2,1)S(1)} %fusion.6), channel_id=1, source_target_pairs={{0,1},{1,0},{2,3},{3,2},{4,5},{5,4},{6,7},{7,6},{8,9},{9,8},{10,11... | collective-permute-start | bytes 4423688 | tf_op jit(solution)/shard_map/ppermute | solution.py:372
  136.1 30.0 %all-to-all-start.3 = ((bf16[8,10,96,128]{3,2,1,0:T(8,128)(2,1)}), bf16[8,10,96,128]{3,2,1,0:T(8,128)(2,1)S(1)}, u32[]{:S(2)}, u32[]{:S(2)}) async-start(bf16[8,10,96,128]{3,2,1,0:T(8,128)(2,1)} %bitcast.54), calls=%async_computation.3 | async-start | bytes 3932160 | tf_op jit(solution)/shard_map/all_to_all | solution.py:364
  143.0 1.6 copy-start.2
  172.9 53.8 %all-to-all-start.4 = ((bf16[128,30,2,128]{3,2,1,0:T(2,128)(2,1)}), bf16[128,30,2,128]{3,2,1,0:T(2,128)(2,1)S(1)}, u32[]{:S(2)}, u32[]{:S(2)}) async-start(bf16[128,30,2,128]{3,2,1,0:T(2,128)(2,1)} %bitcast.48), calls=%async_computation.4 | async-start | bytes 3932160 | tf_op jit(solution)/shard_map/all_to_all | solution.py:364
  187.7 30.9 %collective-permute-start.1 = (bf16[90,2,8,128]{3,2,0,1:T(8,128)(2,1)S(1)}, bf16[90,2,8,128]{3,2,0,1:T(8,128)(2,1)S(1)}, u32[]{:S(2)}, u32[]{:S(2)}) collective-permute-start(bf16[90,2,8,128]{3,2,0,1:T(8,128)(2,1)S(1)} %get-tuple-element.42), channel_id=1, source_target_pairs={{0,4},{1,5},{2,6},{3,7},{4,8},{5,9},{6,10},{7,11},{8,12},{9,13},{1... | collective-permute-start | bytes 1105928 | tf_op jit(solution)/shard_map/ppermute | solution.py:382
  188.8 29.7 %collective-permute-start.2 = (bf16[90,2,8,128]{3,2,0,1:T(8,128)(2,1)S(1)}, bf16[90,2,8,128]{3,2,0,1:T(8,128)(2,1)S(1)}, u32[]{:S(2)}, u32[]{:S(2)}) collective-permute-start(bf16[90,2,8,128]{3,2,0,1:T(8,128)(2,1)S(1)} %get-tuple-element.41), channel_id=1, source_target_pairs={{0,12},{1,13},{2,14},{3,15},{4,0},{5,1},{6,2},{7,3},{8,4},{9,5},{1... | collective-permute-start | bytes 1105928 | tf_op jit(solution)/shard_map/ppermute | solution.py:382
  191.0 35.7 %collective-permute-start.3 = (bf16[90,2,8,128]{3,2,0,1:T(8,128)(2,1)S(1)}, bf16[90,2,8,128]{3,2,0,1:T(8,128)(2,1)}, u32[]{:S(2)}, u32[]{:S(2)}) collective-permute-start(bf16[90,2,8,128]{3,2,0,1:T(8,128)(2,1)S(1)} %get-tuple-element.40), channel_id=1, source_target_pairs={{0,8},{1,9},{2,10},{3,11},{4,12},{5,13},{6,14},{7,15},{8,0},{9,1},... | collective-permute-start | bytes 1105928 | tf_op jit(solution)/shard_map/ppermute | solution.py:382
  218.6 15.0 %copy-start.5 = (bf16[90,2,8,128]{3,2,0,1:T(8,128)(2,1)}, bf16[90,2,8,128]{3,2,0,1:T(8,128)(2,1)S(1)}, u32[]{:S(2)}) copy-start(bf16[90,2,8,128]{3,2,0,1:T(8,128)(2,1)S(1)} %collective-permute-done.2) | copy-start | bytes 1105924
  233.6 40.4 %all-to-all-start.5 = ((bf16[16,6,96,128]{3,2,1,0:T(8,128)(2,1)}), bf16[16,6,96,128]{3,2,1,0:T(8,128)(2,1)S(1)}, u32[]{:S(2)}, u32[]{:S(2)}) async-start(bf16[16,6,96,128]{3,2,1,0:T(8,128)(2,1)} %fourier_backward.1), calls=%async_computation.5 | async-start | bytes 4718592 | tf_op jit(solution)/shard_map/all_to_all | solution.py:364
  239.0 0.9 copy-start.4
  239.9 32.3 %collective-permute-start.4 = (bf16[90,8,128]{2,1,0:T(8,128)(2,1)S(1)}, bf16[90,8,128]{2,1,0:T(8,128)(2,1)S(1)}, u32[]{:S(2)}, u32[]{:S(2)}) collective-permute-start(bf16[90,8,128]{2,1,0:T(8,128)(2,1)S(1)} %fusion.10), channel_id=1, source_target_pairs={{0,2},{1,3},{2,0},{3,1},{4,6},{5,7},{6,4},{7,5},{8,10},{9,11},{10,... | collective-permute-start | bytes 552968 | tf_op jit(solution)/shard_map/ppermute | solution.py:390

commit v4 on v3

--- a/solution.py
+++ b/solution.py
@@ -27,6 +27,7 @@
 CHUNK = Q * SLOT
 DEGREES = L // LATS
 BLOCK = 16
+TAIL = 2
 SHIFT = 40
 
 F32 = jnp.float32
@@ -37,8 +38,39 @@
     return pltpu.CompilerParams(vmem_limit_bytes=mebibytes << 20)
 
 
+def near(x):
+    return pltpu.with_memory_space_constraint(x, pltpu.VMEM)
+
+
 def far(x):
     return pltpu.with_memory_space_constraint(x, pltpu.HBM)
+
+
+def whole(space=pltpu.VMEM):
+    return pl.BlockSpec(memory_space=space)
+
+
+def stream(table, held, ready, steps):
+    g = pl.program_id(0)
+
+    def copy(step):
+        return pltpu.make_async_copy(table.at[step], held.at[step], ready.at[step])
+
+    @pl.when(g == 0)
+    def _():
+        for step in range(steps):
+            copy(step).start()
+
+    def arrive():
+        @pl.when(g < steps)
+        def _():
+            copy(jnp.minimum(g, steps - 1)).wait()
+
+    return arrive
+
+
+def streamed(table):
+    return [pltpu.VMEM(table.shape, table.dtype), pltpu.SemaphoreType.DMA((table.shape[0],))]
 
 
 def cosine_values(position, order, part):
@@ -174,38 +206,39 @@
     )(up.reshape(-1), back.reshape(-1), start.reshape(-1), seed, order, x, root, log_sine)
 
 
-def forward_kernel(table, x_ref, out_ref, buf):
-    rows = table.shape[0]
+def forward_kernel(table, x_ref, out_ref, buf, held, ready):
+    steps, rows, _ = held.shape
+    arrive = stream(table, held, ready, steps)
+    arrive()
     for pair in range(SLOT // 2):
         right = jnp.concatenate(
             [x_ref[:, 2 * pair + half].reshape(LONS * PAD, C) for half in range(2)], axis=1
         )
-        done = jnp.dot(table[...], right, preferred_element_type=F32)
+        done = jnp.dot(held[pl.program_id(0)], right, preferred_element_type=F32)
         for half in range(2):
             buf[pl.ds(2 * pair + half, rows, stride=SLOT), :] = done[:, half * C : half * C + C]
     out_ref[...] = buf[...].astype(BF16)
 
 
 def fourier_forward(table, x):
-    steps = 4
+    steps = 2
     rows = 2 * M // steps
+    table = table.reshape(steps, rows, LONS * PAD)
     return pl.pallas_call(
         forward_kernel,
         grid=(steps,),
         out_shape=pltpu.HBM((2 * M * SLOT, C), BF16),
-        in_specs=[
-            pl.BlockSpec((rows, LONS * PAD), lambda g: (g, 0)),
-            pl.BlockSpec((LONS, SLOT, PAD, C), lambda g: (0, 0, 0, 0)),
-        ],
+        in_specs=[whole(pltpu.HBM), whole()],
         out_specs=pl.BlockSpec((rows * SLOT, C), lambda g: (g, 0)),
-        scratch_shapes=[pltpu.VMEM((rows * SLOT, C), F32)],
+        scratch_shapes=[pltpu.VMEM((rows * SLOT, C), F32)] + streamed(table),
         compiler_params=limit(24),
         name="fourier_forward",
-    )(table, x)
-
-
-def analyse_kernel(table, x_ref, out_ref, wide):
+    )(far(table), near(x))
+
+
+def analyse_kernel(table, x_ref, out_ref, wide, held, ready):
     g = pl.program_id(0)
+    arrive = stream(table, held, ready, ORDERS)
 
     @pl.when(g == 0)
     def _():
@@ -216,7 +249,8 @@
         return jnp.concatenate(parts, axis=0).astype(BF16)
 
     right = jnp.concatenate([column(2 * g), column(2 * g + 1)], axis=1)
-    done = jnp.dot(table[0], right, preferred_element_type=F32).astype(BF16)
+    arrive()
+    done = jnp.dot(held[g], right, preferred_element_type=F32).astype(BF16)
     for half in range(2):
         out_ref[:, half] = done[:, half * C : half * C + C].reshape(LATS, PAD, C)
 
@@ -226,21 +260,19 @@
         analyse_kernel,
         grid=(ORDERS,),
         out_shape=pltpu.HBM((LATS, Q, PAD, C), BF16),
-        in_specs=[
-            pl.BlockSpec((1, LATS * PAD, DEVICES * SLOT), lambda g: (g, 0, 0)),
-            pl.BlockSpec((DEVICES * CHUNK, C), lambda g: (0, 0)),
-        ],
+        in_specs=[whole(pltpu.HBM), whole()],
         out_specs=pl.BlockSpec((LATS, 2, PAD, C), lambda g: (0, g, 0, 0)),
-        scratch_shapes=[pltpu.VMEM((DEVICES * CHUNK, C), F32)],
-        compiler_params=limit(22),
+        scratch_shapes=[pltpu.VMEM((DEVICES * CHUNK, C), F32)] + streamed(table),
+        compiler_params=limit(26),
         name="analyse",
-    )(table, x)
-
-
-def mix_kernel(x_ref, weights, gathered, out_ref, wide, made):
+    )(far(table), near(x))
+
+
+def mix_kernel(x_ref, weights, gathered, out_ref, wide, made, held, ready):
     g = pl.program_id(0)
-    each = weights.shape[0]
+    steps, each = held.shape[:2]
     slabs = LATS * Q
+    arrive = stream(weights, held, ready, steps)
 
     @pl.when(g == 0)
     def _():
@@ -250,88 +282,105 @@
             ].astype(F32)
             made[slab * ODD + PAD - 8 : slab * ODD + PAD, :] = jnp.zeros((8, C), F32)
 
-    for offset in range(each):
-        rows = pl.ds(g * each + offset, slabs, stride=ODD)
-        part = wide[rows, :].astype(BF16)
-        gathered[offset] = part
-        made[rows, :] = lax.dot_general(
-            part, weights[offset], (((1,), (1,)), ((), ())), preferred_element_type=F32
-        )
-
-    @pl.when(g == pl.num_programs(0) - 1)
-    def _():
-        for slab in range(slabs):
-            out_ref[slab * PAD : slab * PAD + PAD, :] = made[
-                slab * ODD : slab * ODD + PAD, :
-            ].astype(BF16)
+    arrive()
+
+    @pl.when(g < steps)
+    def _():
+        for offset in range(each):
+            rows = pl.ds(g * each + offset, slabs, stride=ODD)
+            part = wide[rows, :].astype(BF16)
+            gathered[offset] = part
+            made[rows, :] = lax.dot_general(
+                part, held[g, offset], (((1,), (1,)), ((), ())), preferred_element_type=F32
+            )
+
+    for step in range(TAIL):
+
+        @pl.when(g == steps + step)
+        def _():
+            for slab in range(slabs // TAIL):
+                first = (step * (slabs // TAIL) + slab) * ODD
+                out_ref[slab * PAD : slab * PAD + PAD, :] = made[first : first + PAD, :].astype(
+                    BF16
+                )
 
 
 def mix(x, weights):
-    steps = 10
+    steps = 5
     each = DEGREES // steps
-    whole = LATS * Q * PAD
+    size = LATS * Q * PAD
+    weights = weights.reshape(steps, each, C, C)
     return pl.pallas_call(
         mix_kernel,
-        grid=(steps,),
+        grid=(steps + TAIL,),
         out_shape=(
             pltpu.HBM((DEGREES, LATS * Q, C), BF16),
-            pltpu.HBM((whole, C), BF16),
+            pltpu.HBM((size, C), BF16),
         ),
-        in_specs=[
-            pl.BlockSpec((whole, C), lambda g: (0, 0)),
-            pl.BlockSpec((each, C, C), lambda g: (g, 0, 0)),
-        ],
+        in_specs=[whole(), whole(pltpu.HBM)],
         out_specs=(
-            pl.BlockSpec((each, LATS * Q, C), lambda g: (g, 0, 0)),
-            pl.BlockSpec((whole, C), lambda g: (0, 0)),
+            pl.BlockSpec((each, LATS * Q, C), lambda g: (jnp.minimum(g, steps - 1), 0, 0)),
+            pl.BlockSpec((size // TAIL, C), lambda g: (jnp.maximum(g - steps, 0), 0)),
         ),
-        scratch_shapes=[pltpu.VMEM((LATS * Q * ODD, C), F32)] * 2,
+        scratch_shapes=[pltpu.VMEM((LATS * Q * ODD, C), F32)] * 2 + streamed(weights),
         compiler_params=limit(26),
         name="mix",
-    )(x, weights)
-
-
-def synthesise_kernel(table, x_ref, out_ref, made):
+    )(near(x), far(weights))
+
+
+def synthesise_kernel(table, x_ref, out_ref, made, held, ready):
     g = pl.program_id(0)
-    right = jnp.concatenate([x_ref[:, half].reshape(LATS * PAD, C) for half in range(2)], axis=1)
-    done = jnp.dot(table[0], right, preferred_element_type=F32)
-    for half in range(2):
-        for tt in range(SLOT):
-            made[pl.ds((2 * g + half) * SLOT + tt, DEVICES, stride=CHUNK), :] = done[
-                tt * DEVICES : tt * DEVICES + DEVICES, half * C : half * C + C
-            ]
-
-    @pl.when(g == ORDERS - 1)
-    def _():
-        out_ref[...] = made[...].astype(BF16)
+    arrive = stream(table, held, ready, ORDERS)
+    arrive()
+
+    @pl.when(g < ORDERS)
+    def _():
+        right = jnp.concatenate(
+            [x_ref[:, 2 * g + half].reshape(LATS * PAD, C) for half in range(2)], axis=1
+        )
+        done = jnp.dot(held[g], right, preferred_element_type=F32)
+        for half in range(2):
+            for tt in range(SLOT):
+                made[pl.ds((2 * g + half) * SLOT + tt, DEVICES, stride=CHUNK), :] = done[
+                    tt * DEVICES : tt * DEVICES + DEVICES, half * C : half * C + C
+                ]
+
+    rows = out_ref.shape[0]
+    for step in range(TAIL):
+
+        @pl.when(g == ORDERS + step)
+        def _():
+            out_ref[...] = made[step * rows : step * rows + rows, :].astype(BF16)
 
 
 def synthesise(table, x):
     return pl.pallas_call(
         synthesise_kernel,
-        grid=(ORDERS,),
+        grid=(ORDERS + TAIL,),
         out_shape=pltpu.HBM((DEVICES * CHUNK, C), BF16),
-        in_specs=[
-            pl.BlockSpec((1, DEVICES * SLOT, LATS * PAD), lambda g: (g, 0, 0)),
-            pl.BlockSpec((LATS, 2, PAD, C), lambda g: (0, g, 0, 0)),
-        ],
-        out_specs=pl.BlockSpec((DEVICES * CHUNK, C), lambda g: (0, 0)),
-        scratch_shapes=[pltpu.VMEM((DEVICES * CHUNK, C), F32)],
-        compiler_params=limit(22),
+        in_specs=[whole(pltpu.HBM), whole()],
+        out_specs=pl.BlockSpec(
+            (DEVICES * CHUNK // TAIL, C), lambda g: (jnp.maximum(g - ORDERS, 0), 0)
+        ),
+        scratch_shapes=[pltpu.VMEM((DEVICES * CHUNK, C), F32)] + streamed(table),
+        compiler_params=limit(26),
         name="synthesise",
-    )(table, x)
-
-
-def backward_kernel(table, x_ref, out_ref, wide, right):
+    )(far(table), near(x))
+
+
+def backward_kernel(table, x_ref, out_ref, wide, right, held, ready):
+    arrive = stream(table, held, ready, held.shape[0])
+
     @pl.when(pl.program_id(0) == 0)
     def _():
         wide[...] = x_ref[...].astype(F32)
         for tt in range(SLOT):
             right[:, tt * C : tt * C + C] = wide[pl.ds(tt, 2 * M, stride=SLOT), :].astype(BF16)
 
+    arrive()
     for pair in range(SLOT // 2):
         both = right[:, 2 * pair * C : 2 * pair * C + 2 * C]
-        done = jnp.dot(table[...], both, preferred_element_type=F32).astype(BF16)
+        done = jnp.dot(held[pl.program_id(0)], both, preferred_element_type=F32).astype(BF16)
         for half in range(2):
             for j in range(out_ref.shape[0]):
                 out_ref[j, 2 * pair + half] = done[
@@ -342,22 +391,21 @@
 def fourier_backward(table, x):
     steps = 4
     each = LONS // steps
+    table = table.reshape(steps, each * PAD, 2 * M)
     return pl.pallas_call(
         backward_kernel,
         grid=(steps,),
         out_shape=pltpu.HBM((LONS, SLOT, PAD, C), BF16),
-        in_specs=[
-            pl.BlockSpec((each * PAD, 2 * M), lambda g: (g, 0)),
-            pl.BlockSpec((DEVICES * CHUNK, C), lambda g: (0, 0)),
-        ],
+        in_specs=[whole(pltpu.HBM), whole()],
         out_specs=pl.BlockSpec((each, SLOT, PAD, C), lambda g: (g, 0, 0, 0)),
         scratch_shapes=[
             pltpu.VMEM((DEVICES * CHUNK, C), F32),
             pltpu.VMEM((2 * M, SLOT * C), BF16),
-        ],
-        compiler_params=limit(22),
+        ]
+        + streamed(table),
+        compiler_params=limit(24),
         name="fourier_backward",
-    )(table, x)
+    )(far(table), near(x))
 
 
 def exchange(x, axis):
@@ -404,16 +452,16 @@
     legendre = legendre_table(first_order)
     rows, forward, legendre = lax.optimization_barrier((rows, forward, legendre))
 
-    spectra = fourier_forward(far(forward), rows)
+    spectra = fourier_forward(forward, rows)
     columns = exchange(cells(spectra), both).reshape(DEVICES * CHUNK, C)
     turned = jnp.swapaxes(legendre, 1, 2)
     stored = spectrum.reshape(LATS * ORDERS, DEGREES, 2, C).transpose(1, 0, 2, 3)
     stored = stored.reshape(DEGREES, LATS * Q, C)
     columns, turned, stored = lax.optimization_barrier((columns, turned, stored))
 
-    analysed = exchange(analyse(far(legendre), columns), "lat").reshape(LATS * Q * PAD, C)
+    analysed = exchange(analyse(legendre, columns), "lat").reshape(LATS * Q * PAD, C)
     analysed, backward = lax.optimization_barrier((analysed, backward))
-    gathered, spec_local = mix(analysed, far(weights))
+    gathered, spec_local = mix(analysed, weights)
     spec_grad = exchange(spec_local.reshape(LATS, Q, PAD, C), "lat")
 
     held = jnp.einsum("lrc,lrd->lcd", stored, gathered, preferred_element_type=F32)
@@ -421,15 +469,14 @@
     held, got = share_columns(held)
     spec_grad, held = lax.optimization_barrier((spec_grad, held))
 
-    row_block = synthesise(far(turned), spec_grad)
+    row_block = synthesise(turned, spec_grad)
     row_block = exchange(cells(row_block), both)
-    row_block, held, *got = lax.optimization_barrier((row_block, held, *got))
     for part in got:
         held = held + part.astype(F32)
-    grid_part = fourier_backward(far(backward), row_block.reshape(DEVICES * CHUNK, C))
+    row_block, held = lax.optimization_barrier((row_block, held))
+    grid_part = fourier_backward(backward, row_block.reshape(DEVICES * CHUNK, C))
     grid_part = exchange(grid_part, "lon")
     weight_grad = share_pair(held)
-    grid_part, weight_grad = lax.optimization_barrier((grid_part, weight_grad))
     grad_in = grid_part[:USED].reshape(ROWS, PAD, C)[:, :COLS]
     return jnp.swapaxes(grad_in, 1, 2)[None], weight_grad
 

time: 277 us -> 269 us (0.971)
  Pallas kernels: 45.3 us -> 37.3 us
    pallas_call x2, Pallas kernels: 16.2 us -> 11.1 us  [the longest x1 5.88 us: mix(): pl.pallas_call(mix_kernel, grid=(steps + TAIL,), out_shape=(pltpu.HBM((DE...]
    unnamed x12 -> x8, local copies, waits for them, and re-layouts: 7.5 us -> 6.67 us
  transfers between devices with their start and end apart: 11 -> 11, of which waited for: 7 -> 8; matrix products, arithmetic and copies ran while one was open for 14% -> 14% of each run, Pallas kernels for 3% -> 3%
where the time goes in v4:
time: 269 us; the launch traced here: 267 us
  waiting for transfers between devices  129 us (48%)
  starting transfers between devices  48.2 us (18%)
  Pallas kernels  37.3 us (14%)
  local copies, waits for them, and re-layouts  28.9 us (11%)
  other arithmetic  20.5 us (8%)
    all_to_all x6, waiting for transfers between devices, exchange(): return lax.all_to_all(x, axis, split_axis=0, concat_axis=0, tiled=True)  65 us
    all_to_all x6, starting transfers between devices, exchange(): return lax.all_to_all(x, axis, split_axis=0, concat_axis=0, tiled=True)  39.7 us
    ppermute x3, waiting for transfers between devices, share_columns(): got.append(lax.ppermute(give, 'lon', pairs))  33.8 us
    ppermute x1, waiting for transfers between devices, share_pair(): lax.ppermute(give, 'lon', [(k, k ^ 2) for k in range(LONS)]).astype(F32)  30.3 us
    pallas_call x1, Pallas kernels, legendre_table(): pl.pallas_call(legendre_kernel, out_shape=jax.ShapeDtypeStruct((ORDERS, L...  9.14 us
    optimization_barrier x1, local copies, waits for them, and re-layouts, on_device(): lax.optimization_barrier((rows, forward, legendre))  9.07 us
    convert_element_type x1, other arithmetic, fourier_tables(): backward = (cosine_values(position, order, part) * live).astype(BF16)  8.25 us
    convert_element_type x1, other arithmetic, fourier_tables(): forward = (cosine_values(position, order, part) * live).astype(BF16)  8.1 us
  transfers between devices with their start and end apart: 11, of which 8 were waited for; matrix products, arithmetic and copies ran while one was open for 14% of the time, Pallas kernels for 3%

profile of v4, /device:TPU:0, one launch (start us, length us, event | category | flops | bytes accessed | tf_op | source)
XLA Modules:
  0.0 267.3 jit_solution(5578406159088788994)
XLA Ops:
  0.6 3.3 %pad.4 = bf16[96,96,128]{2,1,0:T(8,128)(2,1)} pad(bf16[90,90,128]{2,1,0:T(8,128)(2,1)} %bitcast.59, bf16[]{:T(256)} %constant.238.clone.1), padding=0_6x0_6x0_0 | pad | bytes 4432898 | tf_op jit(solution)/shard_map/jit(_pad)/pad | solution.py:449
  3.9 8.2 %all-to-all-start = ((bf16[16,6,96,128]{3,2,1,0:T(8,128)(2,1)}), bf16[16,6,96,128]{3,2,1,0:T(8,128)(2,1)S(1)}, u32[]{:S(2)}, u32[]{:S(2)}) async-start(bf16[16,6,96,128]{3,2,1,0:T(8,128)(2,1)} %bitcast.51), calls=%async_computation | async-start | bytes 4718592 | tf_op jit(solution)/shard_map/all_to_all | solution.py:412
  12.2 0.1 sqrt_select_fusion.2
  12.3 0.1 fusion.50.sine_ref
  12.4 0.1 fusion.11
  12.4 0.1 gt.23
  12.6 0.1 subtract_multiply_fusion
  12.6 0.1 mul.331
  12.7 0.1 mul.333
  12.8 0.1 sub.126
  12.9 0.1 div.98
  13.0 0.1 reshape.363.start
  13.0 0.8 dynamic_slice.30.seed
  13.8 9.1 %legendre.1.table = bf16[5,768,768]{2,1,0:T(8,128)(2,1)S(1)} custom-call(f32[3600]{0:T(1024)S(1)} %get-tuple-element.34.up, f32[3600]{0:T(1024)S(1)} %get-tuple-element.33.back, f32[3600]{0:T(1024)S(1)} %reshape.363.start, f32[5]{0:T(128)S(1)} %dynamic_slice.30.seed, f32[5]{0:T(128)S(1)} %fusion.51.order, f32[8,128]{1,0:T(8,128)S(1)} %get-tuple-element.42.x_ref, ...), custom_call_target="tpu_custom_call" | custom-call | tf_op jit(solution)/shard_map/legendre/pallas_call | solution.py:198
  23.0 0.0 copy-start
  23.0 2.5 copy-done
  25.5 8.1 %multiply_convert_fusion.1 = bf16[1280,1536]{1,0:T(8,128)(2,1)} fusion(f32[1536]{0:T(1024)S(1)} %fusion.33, f32[1280]{0:T(1024)S(1)} %fusion.31, f32[1280]{0:T(1024)S(1)} %fusion.27, f32[1536]{0:T(1024)S(1)} %fusion.26), kind=kLoop, calls=%fused_computation.7 | loop fusion | flops 49152000 | bytes 3954688 | tf_op jit(solution)/shard_map/convert_element_type | solution.py:101
  33.6 10.5 %all-to-all-done.x_ref = bf16[16,6,96,128]{3,2,1,0:T(8,128)(2,1)S(1)} async-done(((bf16[16,6,96,128]{3,2,1,0:T(8,128)(2,1)}), bf16[16,6,96,128]{3,2,1,0:T(8,128)(2,1)S(1)}, u32[]{:S(2)}, u32[]{:S(2)}) %all-to-all-start) | async-done | bytes 2359328 | tf_op jit(solution)/shard_map/all_to_all | solution.py:412
  44.1 6.1 %fourier_forward.1 = bf16[7680,128]{1,0:T(8,128)(2,1)} custom-call(bf16[2,640,1536]{2,1,0:T(8,128)(2,1)} %bitcast.50, bf16[16,6,96,128]{3,2,1,0:T(8,128)(2,1)S(1)} %all-to-all-done.x_ref), custom_call_target="tpu_custom_call" | custom-call | tf_op jit(solution)/shard_map/fourier_forward/pallas_call | solution.py:227
  50.2 6.2 %all-to-all-start.1 = ((bf16[128,30,2,128]{3,2,1,0:T(2,128)(2,1)}), bf16[128,30,2,128]{3,2,1,0:T(2,128)(2,1)S(1)}, u32[]{:S(2)}, u32[]{:S(2)}) async-start(bf16[128,30,2,128]{3,2,1,0:T(2,128)(2,1)} %bitcast.54), calls=%async_computation.1 | async-start | bytes 3932160 | tf_op jit(solution)/shard_map/all_to_all | solution.py:412
  56.4 4.0 %copy.9 = bf16[90,40,2,128]{3,2,1,0:T(2,128)(2,1)} copy(bf16[90,40,2,128]{3,2,0,1:T(2,128)(2,1)} %bitcast.61) | data formatting | bytes 3686400 | tf_op jit(solution)/shard_map/transpose | solution.py:458
  60.4 9.1 %copy.8 = bf16[5,768,768]{1,2,0:T(8,128)(2,1)} copy(bf16[5,768,768]{2,1,0:T(8,128)(2,1)} %copy-done) | data formatting | bytes 11796480 | tf_op jit(solution)/shard_map/optimization_barrier | solution.py:453
  69.5 16.0 %all-to-all-done.1 = bf16[128,30,2,128]{3,2,1,0:T(2,128)(2,1)S(1)} async-done(((bf16[128,30,2,128]{3,2,1,0:T(2,128)(2,1)}), bf16[128,30,2,128]{3,2,1,0:T(2,128)(2,1)S(1)}, u32[]{:S(2)}, u32[]{:S(2)}) %all-to-all-start.1) | async-done | bytes 1966112 | tf_op jit(solution)/shard_map/all_to_all | solution.py:412
  85.5 5.1 %analyse.1 = bf16[8,10,96,128]{3,2,1,0:T(8,128)(2,1)} custom-call(bf16[5,768,768]{2,1,0:T(8,128)(2,1)} %copy-done, bf16[7680,128]{1,0:T(8,128)(2,1)S(1)} %bitcast.43), custom_call_target="tpu_custom_call" | custom-call | tf_op jit(solution)/shard_map/analyse/pallas_call | solution.py:259
  90.6 3.6 %all-to-all-start.2 = ((bf16[8,10,96,128]{3,2,1,0:T(8,128)(2,1)}), bf16[8,10,96,128]{3,2,1,0:T(8,128)(2,1)S(1)}, u32[]{:S(2)}, u32[]{:S(2)}) async-start(bf16[8,10,96,128]{3,2,1,0:T(8,128)(2,1)} %analyse.1), calls=%async_computation.2 | async-start | bytes 3932160 | tf_op jit(solution)/shard_map/all_to_all | solution.py:412
  94.2 8.3 %multiply_convert_fusion = bf16[1536,1280]{1,0:T(8,128)(2,1)} fusion(f32[1536]{0:T(1024)S(1)} %fusion.33, f32[1280]{0:T(1024)S(1)} %fusion.31, f32[1280]{0:T(1024)S(1)} %fusion.27, f32[1536]{0:T(1024)S(1)} %fusion.26), kind=kLoop, calls=%fused_computation | loop fusion | flops 49152000 | bytes 3954688 | tf_op jit(solution)/shard_map/convert_element_type | solution.py:104
  102.5 16.9 %all-to-all-done.2 = bf16[8,10,96,128]{3,2,1,0:T(8,128)(2,1)S(1)} async-done(((bf16[8,10,96,128]{3,2,1,0:T(8,128)(2,1)}), bf16[8,10,96,128]{3,2,1,0:T(8,128)(2,1)S(1)}, u32[]{:S(2)}, u32[]{:S(2)}) %all-to-all-start.2) | async-done | bytes 1966112 | tf_op jit(solution)/shard_map/all_to_all | solution.py:412
  119.4 0.0 copy-start.3
  119.4 5.9 %mix.1 = (bf16[90,80,128]{2,1,0:T(8,128)(2,1)}, bf16[7680,128]{1,0:T(8,128)(2,1)}) custom-call(bf16[7680,128]{1,0:T(8,128)(2,1)S(1)} %bitcast.44, bf16[5,18,128,128]{3,2,1,0:T(8,128)(2,1)} %bitcast.58), custom_call_target="tpu_custom_call" | custom-call | tf_op jit(solution)/shard_map/mix/pallas_call | solution.py:313
  125.3 0.0 copy-done.3
  125.3 2.5 fusion.52
  127.8 0.0 copy-start.1
  127.8 2.5 copy-done.1
  130.3 0.3 fusion.6
  130.6 0.1 collective-permute-start
  130.7 3.9 %all-to-all-start.3 = ((bf16[8,10,96,128]{3,2,1,0:T(8,128)(2,1)}), bf16[8,10,96,128]{3,2,1,0:T(8,128)(2,1)S(1)}, u32[]{:S(2)}, u32[]{:S(2)}) async-start(bf16[8,10,96,128]{3,2,1,0:T(8,128)(2,1)} %bitcast.60), calls=%async_computation.3 | async-start | bytes 3932160 | tf_op jit(solution)/shard_map/all_to_all | solution.py:412
  134.6 0.0 collective-permute-done
  134.6 2.8 %bitcast_add_fusion = f32[90,8,8,128]{3,2,1,0:T(8,128)S(1)} fusion(bf16[90,8,8,128]{3,2,1,0:T(8,128)(2,1)} %collective-permute-done, f32[90,8,2,8,128]{4,3,2,1,0:T(8,128)} %bitcast.48, s32[]{:T(128)S(6)} %select_n.230), kind=kLoop, calls=%fused_computation.14 | loop fusion | flops 1474560 | bytes 7372804 | tf_op jit(solution)/shard_map/add | solution.py:420
  137.4 0.2 copy.10
  137.6 0.0 copy-start.2
  137.6 1.6 copy-done.2
  139.3 21.5 %all-to-all-done.3.x_ref = bf16[8,10,96,128]{3,2,1,0:T(8,128)(2,1)S(1)} async-done(((bf16[8,10,96,128]{3,2,1,0:T(8,128)(2,1)}), bf16[8,10,96,128]{3,2,1,0:T(8,128)(2,1)S(1)}, u32[]{:S(2)}, u32[]{:S(2)}) %all-to-all-start.3) | async-done | bytes 1966112 | tf_op jit(solution)/shard_map/all_to_all | solution.py:412
  160.8 5.3 %synthesise.1 = bf16[7680,128]{1,0:T(8,128)(2,1)} custom-call(bf16[5,768,768]{2,1,0:T(8,128)(2,1)} %bitcast.46, bf16[8,10,96,128]{3,2,1,0:T(8,128)(2,1)S(1)} %all-to-all-done.3.x_ref), custom_call_target="tpu_custom_call" | custom-call | tf_op jit(solution)/shard_map/synthesise/pallas_call | solution.py:357
  166.0 13.0 %all-to-all-start.4 = ((bf16[128,30,2,128]{3,2,1,0:T(2,128)(2,1)}), bf16[128,30,2,128]{3,2,1,0:T(2,128)(2,1)S(1)}, u32[]{:S(2)}, u32[]{:S(2)}) async-start(bf16[128,30,2,128]{3,2,1,0:T(2,128)(2,1)} %bitcast.53), calls=%async_computation.4 | async-start | bytes 3932160 | tf_op jit(solution)/shard_map/all_to_all | solution.py:412
  179.1 1.7 fusion.7
  180.8 2.9 %collective-permute-start.3 = (bf16[90,2,8,128]{3,2,0,1:T(8,128)(2,1)S(1)}, bf16[90,2,8,128]{3,2,0,1:T(8,128)(2,1)S(1)}, u32[]{:S(2)}, u32[]{:S(2)}) collective-permute-start(bf16[90,2,8,128]{3,2,0,1:T(8,128)(2,1)S(1)} %get-tuple-element.31), channel_id=1, source_target_pairs={{0,8},{1,9},{2,10},{3,11},{4,12},{5,13},{6,14},{7,15},{8,0},{9,1},... | collective-permute-start | bytes 1105928 | tf_op jit(solution)/shard_map/ppermute | solution.py:430
  183.7 0.9 collective-permute-start.2
  184.6 1.1 collective-permute-start.1
  185.8 26.0 %collective-permute-done.3 = bf16[90,2,8,128]{3,2,0,1:T(8,128)(2,1)S(1)} collective-permute-done((bf16[90,2,8,128]{3,2,0,1:T(8,128)(2,1)S(1)}, bf16[90,2,8,128]{3,2,0,1:T(8,128)(2,1)S(1)}, u32[]{:S(2)}, u32[]{:S(2)}) %collective-permute-start.3) | collective-permute-done | bytes 368672 | tf_op jit(solution)/shard_map/ppermute | solution.py:430
  211.8 5.8 %collective-permute-done.2 = bf16[90,2,8,128]{3,2,0,1:T(8,128)(2,1)S(1)} collective-permute-done((bf16[90,2,8,128]{3,2,0,1:T(8,128)(2,1)S(1)}, bf16[90,2,8,128]{3,2,0,1:T(8,128)(2,1)S(1)}, u32[]{:S(2)}, u32[]{:S(2)}) %collective-permute-start.2) | collective-permute-done | bytes 368672 | tf_op jit(solution)/shard_map/ppermute | solution.py:430
  217.6 2.0 collective-permute-done.1
  219.6 0.2 convert_add_fusion
  219.7 0.0 all-to-all-done.4
  219.8 5.9 %fourier_backward.1 = bf16[16,6,96,128]{3,2,1,0:T(8,128)(2,1)} custom-call(bf16[4,384,1280]{2,1,0:T(8,128)(2,1)} %bitcast.49, bf16[7680,128]{1,0:T(8,128)(2,1)S(1)} %bitcast.45), custom_call_target="tpu_custom_call" | custom-call | tf_op jit(solution)/shard_map/fourier_backward/pallas_call | solution.py:395
  225.6 4.8 %all-to-all-start.5 = ((bf16[16,6,96,128]{3,2,1,0:T(8,128)(2,1)}), bf16[16,6,96,128]{3,2,1,0:T(8,128)(2,1)S(1)}, u32[]{:S(2)}, u32[]{:S(2)}) async-start(bf16[16,6,96,128]{3,2,1,0:T(8,128)(2,1)} %fourier_backward.1), calls=%async_computation.5 | async-start | bytes 4718592 | tf_op jit(solution)/shard_map/all_to_all | solution.py:412
  230.5 0.7 fusion.10
  231.2 3.4 %collective-permute-start.4 = (bf16[90,8,128]{2,1,0:T(8,128)(2,1)}, bf16[90,8,128]{2,1,0:T(8,128)(2,1)S(1)}, u32[]{:S(2)}, u32[]{:S(2)}) collective-permute-start(bf16[90,8,128]{2,1,0:T(8,128)(2,1)} %fusion.10), channel_id=1, source_target_pairs={{0,2},{1,3},{2,0},{3,1},{4,6},{5,7},{6,4},{7,5},{8,10},{9,11},{10,... | collective-permute-start | bytes 552968 | tf_op jit(solution)/shard_map/ppermute | solution.py:438
  234.6 30.3 %collective-permute-done.4 = bf16[90,8,128]{2,1,0:T(8,128)(2,1)S(1)} collective-permute-done((bf16[90,8,128]{2,1,0:T(8,128)(2,1)}, bf16[90,8,128]{2,1,0:T(8,128)(2,1)S(1)}, u32[]{:S(2)}, u32[]{:S(2)}) %collective-permute-start.4) | collective-permute-done | bytes 184352 | tf_op jit(solution)/shard_map/ppermute | solution.py:438
  264.9 0.8 bitcast_add_fusion.1
  265.7 0.0 all-to-all-done.5
  265.7 0.1 slice.8
  265.8 1.5 slice_bitcast_fusion
  (15 shorter events, 0.2 us)
Async XLA Ops:
  3.9 40.2 %all-to-all-start = ((bf16[16,6,96,128]{3,2,1,0:T(8,128)(2,1)}), bf16[16,6,96,128]{3,2,1,0:T(8,128)(2,1)S(1)}, u32[]{:S(2)}, u32[]{:S(2)}) async-start(bf16[16,6,96,128]{3,2,1,0:T(8,128)(2,1)} %bitcast.51), calls=%async_computation | async-start | bytes 4718592 | tf_op jit(solution)/shard_map/all_to_all | solution.py:412
  23.0 2.5 copy-start
  50.2 35.3 %all-to-all-start.1 = ((bf16[128,30,2,128]{3,2,1,0:T(2,128)(2,1)}), bf16[128,30,2,128]{3,2,1,0:T(2,128)(2,1)S(1)}, u32[]{:S(2)}, u32[]{:S(2)}) async-start(bf16[128,30,2,128]{3,2,1,0:T(2,128)(2,1)} %bitcast.54), calls=%async_computation.1 | async-start | bytes 3932160 | tf_op jit(solution)/shard_map/all_to_all | solution.py:412
  90.6 28.8 %all-to-all-start.2 = ((bf16[8,10,96,128]{3,2,1,0:T(8,128)(2,1)}), bf16[8,10,96,128]{3,2,1,0:T(8,128)(2,1)S(1)}, u32[]{:S(2)}, u32[]{:S(2)}) async-start(bf16[8,10,96,128]{3,2,1,0:T(8,128)(2,1)} %analyse.1), calls=%async_computation.2 | async-start | bytes 3932160 | tf_op jit(solution)/shard_map/all_to_all | solution.py:412
  119.4 5.9 %copy-start.3 = (bf16[90,40,2,128]{3,2,1,0:T(2,128)(2,1)S(1)}, bf16[90,40,2,128]{3,2,1,0:T(2,128)(2,1)}, u32[]{:S(2)}) copy-start(bf16[90,40,2,128]{3,2,1,0:T(2,128)(2,1)} %copy.9) | copy-start | bytes 5529604
  127.8 2.5 copy-start.1
  130.6 4.0 %collective-permute-start = (bf16[90,8,8,128]{3,2,1,0:T(8,128)(2,1)S(1)}, bf16[90,8,8,128]{3,2,1,0:T(8,128)(2,1)}, u32[]{:S(2)}, u32[]{:S(2)}) collective-permute-start(bf16[90,8,8,128]{3,2,1,0:T(8,128)(2,1)S(1)} %fusion.6), channel_id=1, source_target_pairs={{0,1},{1,0},{2,3},{3,2},{4,5},{5,4},{6,7},{7,6},{8,9},{9,8},{10,11... | collective-permute-start | bytes 4423688 | tf_op jit(solution)/shard_map/ppermute | solution.py:420
  130.7 30.1 %all-to-all-start.3 = ((bf16[8,10,96,128]{3,2,1,0:T(8,128)(2,1)}), bf16[8,10,96,128]{3,2,1,0:T(8,128)(2,1)S(1)}, u32[]{:S(2)}, u32[]{:S(2)}) async-start(bf16[8,10,96,128]{3,2,1,0:T(8,128)(2,1)} %bitcast.60), calls=%async_computation.3 | async-start | bytes 3932160 | tf_op jit(solution)/shard_map/all_to_all | solution.py:412
  137.6 1.6 copy-start.2
  166.0 53.7 %all-to-all-start.4 = ((bf16[128,30,2,128]{3,2,1,0:T(2,128)(2,1)}), bf16[128,30,2,128]{3,2,1,0:T(2,128)(2,1)S(1)}, u32[]{:S(2)}, u32[]{:S(2)}) async-start(bf16[128,30,2,128]{3,2,1,0:T(2,128)(2,1)} %bitcast.53), calls=%async_computation.4 | async-start | bytes 3932160 | tf_op jit(solution)/shard_map/all_to_all | solution.py:412
  180.8 31.0 %collective-permute-start.3 = (bf16[90,2,8,128]{3,2,0,1:T(8,128)(2,1)S(1)}, bf16[90,2,8,128]{3,2,0,1:T(8,128)(2,1)S(1)}, u32[]{:S(2)}, u32[]{:S(2)}) collective-permute-start(bf16[90,2,8,128]{3,2,0,1:T(8,128)(2,1)S(1)} %get-tuple-element.31), channel_id=1, source_target_pairs={{0,8},{1,9},{2,10},{3,11},{4,12},{5,13},{6,14},{7,15},{8,0},{9,1},... | collective-permute-start | bytes 1105928 | tf_op jit(solution)/shard_map/ppermute | solution.py:430
  183.7 33.8 %collective-permute-start.2 = (bf16[90,2,8,128]{3,2,0,1:T(8,128)(2,1)S(1)}, bf16[90,2,8,128]{3,2,0,1:T(8,128)(2,1)S(1)}, u32[]{:S(2)}, u32[]{:S(2)}) collective-permute-start(bf16[90,2,8,128]{3,2,0,1:T(8,128)(2,1)S(1)} %get-tuple-element.32), channel_id=1, source_target_pairs={{0,12},{1,13},{2,14},{3,15},{4,0},{5,1},{6,2},{7,3},{8,4},{9,5},{1... | collective-permute-start | bytes 1105928 | tf_op jit(solution)/shard_map/ppermute | solution.py:430
  184.6 34.9 %collective-permute-start.1 = (bf16[90,2,8,128]{3,2,0,1:T(8,128)(2,1)S(1)}, bf16[90,2,8,128]{3,2,0,1:T(8,128)(2,1)S(1)}, u32[]{:S(2)}, u32[]{:S(2)}) collective-permute-start(bf16[90,2,8,128]{3,2,0,1:T(8,128)(2,1)S(1)} %get-tuple-element.30), channel_id=1, source_target_pairs={{0,4},{1,5},{2,6},{3,7},{4,8},{5,9},{6,10},{7,11},{8,12},{9,13},{1... | collective-permute-start | bytes 1105928 | tf_op jit(solution)/shard_map/ppermute | solution.py:430
  225.6 40.0 %all-to-all-start.5 = ((bf16[16,6,96,128]{3,2,1,0:T(8,128)(2,1)}), bf16[16,6,96,128]{3,2,1,0:T(8,128)(2,1)S(1)}, u32[]{:S(2)}, u32[]{:S(2)}) async-start(bf16[16,6,96,128]{3,2,1,0:T(8,128)(2,1)} %fourier_backward.1), calls=%async_computation.5 | async-start | bytes 4718592 | tf_op jit(solution)/shard_map/all_to_all | solution.py:412
  231.2 33.7 %collective-permute-start.4 = (bf16[90,8,128]{2,1,0:T(8,128)(2,1)}, bf16[90,8,128]{2,1,0:T(8,128)(2,1)S(1)}, u32[]{:S(2)}, u32[]{:S(2)}) collective-permute-start(bf16[90,8,128]{2,1,0:T(8,128)(2,1)} %fusion.10), channel_id=1, source_target_pairs={{0,2},{1,3},{2,0},{3,1},{4,6},{5,7},{6,4},{7,5},{8,10},{9,11},{10,... | collective-permute-start | bytes 552968 | tf_op jit(solution)/shard_map/ppermute | solution.py:438

commit v5 on v4

--- a/solution.py
+++ b/solution.py
@@ -23,6 +23,7 @@
 PAD = 96
 ODD = PAD + 1
 ORDERS = M // (LATS * LONS)
+HALF = LONS // 2
 Q = 2 * ORDERS
 CHUNK = Q * SLOT
 DEGREES = L // LATS
@@ -93,16 +94,20 @@
 
     def modes(shape, axis):
         at = lax.broadcasted_iota(jnp.int32, shape, axis)
-        return (at // 2).astype(F32), (at % 2).astype(F32)
-
-    wide = LONS * PAD
+        device, kind = at // Q, at % Q
+        parity, device = device // (DEVICES // 2), device % (DEVICES // 2)
+        lat = device // LONS * 2 + parity
+        order = device % LONS * (LATS * ORDERS) + kind // 2 * LATS + lat
+        return order.astype(F32), (kind % 2).astype(F32)
+
+    wide = HALF * PAD
     position, live = line((1, wide), 1)
     order, part = modes((2 * M, 1), 0)
     forward = (cosine_values(position, order, part) * live).astype(BF16)
     position, live = line((wide, 1), 0)
     order, part = modes((1, 2 * M), 1)
     backward = (cosine_values(position, order, part) * live).astype(BF16)
-    return forward, backward
+    return forward.reshape(2, M, wide), backward
 
 
 def seed_constants():
@@ -168,13 +173,15 @@
     lax.fori_loop(0, LATS, band, (none, none, none))
 
 
-def legendre_table(first_order):
-    orders = first_order + jnp.arange(ORDERS, dtype=jnp.int32)
+def legendre_table():
+    lon, lat = lax.axis_index("lon"), lax.axis_index("lat")
+    orders = (lon * ORDERS + jnp.arange(ORDERS, dtype=jnp.int32)) * LATS + lat
     order = orders.astype(F32)
-    seed = lax.dynamic_slice(jnp.asarray(seed_constants()), (first_order,), (ORDERS,))
+    seeds = jnp.asarray(seed_constants().reshape(LONS, ORDERS, LATS))
+    seed = lax.dynamic_slice(seeds, (lon, 0, lat), (1, ORDERS, 1)).reshape(ORDERS)
     slot = jnp.arange(1024, dtype=jnp.int32)
     tt, device = slot // DEVICES, slot % DEVICES
-    lon, lat = device // LATS, device % LATS
+    lat, lon = device // LONS, device % LONS
     live = (tt < SLOT) & (lon < USED)
     row = jnp.where(live, ROWS * lat + SLOT * lon + tt, 0)
     angle = (row.astype(F32) + 0.5) * (math.pi / LAT)
@@ -207,30 +214,45 @@
 
 
 def forward_kernel(table, x_ref, out_ref, buf, held, ready):
-    steps, rows, _ = held.shape
-    arrive = stream(table, held, ready, steps)
+    g = pl.program_id(0)
+    arrive = stream(table, held, ready, 2)
     arrive()
-    for pair in range(SLOT // 2):
-        right = jnp.concatenate(
-            [x_ref[:, 2 * pair + half].reshape(LONS * PAD, C) for half in range(2)], axis=1
-        )
-        done = jnp.dot(held[pl.program_id(0)], right, preferred_element_type=F32)
-        for half in range(2):
-            buf[pl.ds(2 * pair + half, rows, stride=SLOT), :] = done[:, half * C : half * C + C]
-    out_ref[...] = buf[...].astype(BF16)
+    rows = LONS * Q
+
+    for parity in range(2):
+
+        @pl.when(g == parity)
+        def _():
+            for pair in range(SLOT // 2):
+                both = []
+                for half in range(2):
+                    low = x_ref[:HALF, 2 * pair + half]
+                    high = x_ref[HALF:, 2 * pair + half]
+                    both.append((low - high if parity else low + high).reshape(HALF * PAD, C))
+                done = jnp.dot(
+                    held[parity], jnp.concatenate(both, axis=1), preferred_element_type=F32
+                )
+                for half in range(2):
+                    for lat in range(LATS // 2):
+                        first = lat * rows * SLOT + 2 * pair + half
+                        buf[pl.ds(first, rows, stride=SLOT), :] = done[
+                            lat * rows : lat * rows + rows, half * C : half * C + C
+                        ]
+
+    for lat in range(LATS // 2):
+        first = lat * rows * SLOT
+        out_ref[lat, 0] = buf[first : first + rows * SLOT, :].astype(BF16)
 
 
 def fourier_forward(table, x):
-    steps = 2
-    rows = 2 * M // steps
-    table = table.reshape(steps, rows, LONS * PAD)
+    shape = (LATS // 2, 2, LONS * CHUNK, C)
     return pl.pallas_call(
         forward_kernel,
-        grid=(steps,),
-        out_shape=pltpu.HBM((2 * M * SLOT, C), BF16),
+        grid=(2,),
+        out_shape=pltpu.HBM(shape, BF16),
         in_specs=[whole(pltpu.HBM), whole()],
-        out_specs=pl.BlockSpec((rows * SLOT, C), lambda g: (g, 0)),
-        scratch_shapes=[pltpu.VMEM((rows * SLOT, C), F32)] + streamed(table),
+        out_specs=pl.BlockSpec((shape[0], 1) + shape[2:], lambda g: (0, g, 0, 0)),
+        scratch_shapes=[pltpu.VMEM((M * SLOT, C), F32)] + streamed(table),
         compiler_params=limit(24),
         name="fourier_forward",
     )(far(table), near(x))
@@ -369,41 +391,51 @@
 
 
 def backward_kernel(table, x_ref, out_ref, wide, right, held, ready):
+    g = pl.program_id(0)
     arrive = stream(table, held, ready, held.shape[0])
-
-    @pl.when(pl.program_id(0) == 0)
+    rows = LONS * Q
+
+    @pl.when(g == 0)
     def _():
         wide[...] = x_ref[...].astype(F32)
         for tt in range(SLOT):
-            right[:, tt * C : tt * C + C] = wide[pl.ds(tt, 2 * M, stride=SLOT), :].astype(BF16)
+            part = wide[pl.ds(tt, 2 * M, stride=SLOT), :].astype(BF16)
+            for lat in range(LATS):
+                first = lat // 2 * rows
+                right[lat % 2, first : first + rows, tt * C : tt * C + C] = part[
+                    lat * rows : lat * rows + rows
+                ]
 
     arrive()
     for pair in range(SLOT // 2):
-        both = right[:, 2 * pair * C : 2 * pair * C + 2 * C]
-        done = jnp.dot(held[pl.program_id(0)], both, preferred_element_type=F32).astype(BF16)
-        for half in range(2):
-            for j in range(out_ref.shape[0]):
-                out_ref[j, 2 * pair + half] = done[
-                    j * PAD : j * PAD + PAD, half * C : half * C + C
-                ]
+        lanes = slice(2 * pair * C, 2 * pair * C + 2 * C)
+        even = jnp.dot(held[g, :, :M], right[0, :, lanes], preferred_element_type=F32)
+        odd = jnp.dot(held[g, :, M:], right[1, :, lanes], preferred_element_type=F32)
+        for side, done in enumerate((even + odd, even - odd)):
+            done = done.astype(BF16)
+            for half in range(2):
+                for j in range(out_ref.shape[1]):
+                    out_ref[side, j, 2 * pair + half] = done[
+                        j * PAD : j * PAD + PAD, half * C : half * C + C
+                    ]
 
 
 def fourier_backward(table, x):
-    steps = 4
-    each = LONS // steps
+    steps = 2
+    each = HALF // steps
     table = table.reshape(steps, each * PAD, 2 * M)
     return pl.pallas_call(
         backward_kernel,
         grid=(steps,),
-        out_shape=pltpu.HBM((LONS, SLOT, PAD, C), BF16),
+        out_shape=pltpu.HBM((2, HALF, SLOT, PAD, C), BF16),
         in_specs=[whole(pltpu.HBM), whole()],
-        out_specs=pl.BlockSpec((each, SLOT, PAD, C), lambda g: (g, 0, 0, 0)),
+        out_specs=pl.BlockSpec((2, each, SLOT, PAD, C), lambda g: (0, g, 0, 0, 0)),
         scratch_shapes=[
             pltpu.VMEM((DEVICES * CHUNK, C), F32),
-            pltpu.VMEM((2 * M, SLOT * C), BF16),
+            pltpu.VMEM((2, M, SLOT * C), BF16),
         ]
         + streamed(table),
-        compiler_params=limit(24),
+        compiler_params=limit(26),
         name="fourier_backward",
     )(far(table), near(x))
 
@@ -416,8 +448,9 @@
     core = lax.axis_index("lon") & 1
     held = held.reshape(DEGREES, LONS // 2, 2, C // LONS, C)
     keep = lax.dynamic_index_in_dim(held, core, 2, keepdims=False)
-    give = lax.dynamic_index_in_dim(held, 1 - core, 2, keepdims=False).astype(BF16)
-    return keep + lax.ppermute(give, "lon", [(k, k ^ 1) for k in range(LONS)]).astype(F32)
+    give = lax.dynamic_index_in_dim(held, 1 - core, 2, keepdims=False)
+    got = lax.ppermute(give, "lon", [(k, k ^ 1) for k in range(LONS)])
+    return (keep.astype(F32) + got.astype(F32)).astype(BF16)
 
 
 def share_columns(held):
@@ -425,7 +458,7 @@
     held = held.reshape(DEGREES, 4, 2, C // LONS, C)
     got = []
     for step in (1, 3, 2):
-        give = lax.dynamic_index_in_dim(held, (z + step) % 4, 1, keepdims=False).astype(BF16)
+        give = lax.dynamic_index_in_dim(held, (z + step) % 4, 1, keepdims=False)
         pairs = [(k, (k + 4 * step) % LONS) for k in range(LONS)]
         got.append(lax.ppermute(give, "lon", pairs))
     return lax.dynamic_index_in_dim(held, z, 1, keepdims=False), got
@@ -443,19 +476,18 @@
 
 
 def on_device(grad_out, spectrum, weights):
-    both = ("lon", "lat")
-    first_order = (lax.axis_index("lon") * LATS + lax.axis_index("lat")) * ORDERS
+    both = ("lat", "lon")
     rows = jnp.swapaxes(grad_out[0], 1, 2)
     rows = jnp.pad(rows, ((0, LONS * SLOT - ROWS), (0, PAD - COLS), (0, 0)))
     rows = exchange(rows.reshape(LONS, SLOT, PAD, C), "lon")
     forward, backward = fourier_tables()
-    legendre = legendre_table(first_order)
+    legendre = legendre_table()
     rows, forward, legendre = lax.optimization_barrier((rows, forward, legendre))
 
     spectra = fourier_forward(forward, rows)
     columns = exchange(cells(spectra), both).reshape(DEVICES * CHUNK, C)
     turned = jnp.swapaxes(legendre, 1, 2)
-    stored = spectrum.reshape(LATS * ORDERS, DEGREES, 2, C).transpose(1, 0, 2, 3)
+    stored = spectrum.reshape(ORDERS, LATS, DEGREES, 2, C).transpose(2, 1, 0, 3, 4)
     stored = stored.reshape(DEGREES, LATS * Q, C)
     columns, turned, stored = lax.optimization_barrier((columns, turned, stored))
 
@@ -465,17 +497,19 @@
     spec_grad = exchange(spec_local.reshape(LATS, Q, PAD, C), "lat")
 
     held = jnp.einsum("lrc,lrd->lcd", stored, gathered, preferred_element_type=F32)
+    held = held.astype(BF16)
     held = share_cores(held)
     held, got = share_columns(held)
     spec_grad, held = lax.optimization_barrier((spec_grad, held))
 
     row_block = synthesise(turned, spec_grad)
     row_block = exchange(cells(row_block), both)
+    held = held.astype(F32)
     for part in got:
         held = held + part.astype(F32)
     row_block, held = lax.optimization_barrier((row_block, held))
     grid_part = fourier_backward(backward, row_block.reshape(DEVICES * CHUNK, C))
-    grid_part = exchange(grid_part, "lon")
+    grid_part = exchange(grid_part.reshape(LONS, SLOT, PAD, C), "lon")
     weight_grad = share_pair(held)
     grad_in = grid_part[:USED].reshape(ROWS, PAD, C)[:, :COLS]
     return jnp.swapaxes(grad_in, 1, 2)[None], weight_grad

time: 269 us -> 264 us (0.981)
  waiting for transfers between devices: 129 us -> 140 us
  other arithmetic: 20.5 us -> 12.8 us
  local copies, waits for them, and re-layouts: 28.9 us -> 24.1 us
  Pallas kernels: 37.3 us -> 34.2 us
    all_to_all x6, waiting for transfers between devices: 65 us -> 73.9 us  [exchange(): return lax.all_to_all(x, axis, split_axis=0, concat_axis=0, tiled=True)]
    convert_element_type x1, other arithmetic: 8.1 us -> 4.28 us  [fourier_tables(): forward = (cosine_values(position, order, part) * live).astype(BF16)]
    convert_element_type x1, other arithmetic: 8.25 us -> 4.58 us  [fourier_tables(): backward = (cosine_values(position, order, part) * live).astype(BF16)]
    pallas_call x2, Pallas kernels: 11.9 us -> 8.77 us  [the longest x1 4.47 us: fourier_backward(): pl.pallas_call(backward_kernel, grid=(steps,), out_shape=pltpu.HBM((2, HA...]
    add x2 -> x0, other arithmetic: 2.78 us -> none  [the longest x1 2.78 us: share_cores(): keep + lax.ppermute(give, 'lon', [(k, k ^ 1) for k in range(LONS)]).astyp...]
    unnamed x8 -> x10, local copies, waits for them, and re-layouts: 6.67 us -> 4.26 us
  transfers between devices with their start and end apart: 11 -> 11, of which waited for: 8 -> 7; matrix products, arithmetic and copies ran while one was open for 14% -> 10% of each run, Pallas kernels for 3% -> 3%
where the time goes in v5:
time: 264 us; the launch traced here: 263 us
  waiting for transfers between devices  140 us (53%)
  starting transfers between devices  48.4 us (18%)
  Pallas kernels  34.2 us (13%)
  local copies, waits for them, and re-layouts  24.1 us (9%)
  other arithmetic  12.8 us (5%)
    all_to_all x6, waiting for transfers between devices, exchange(): return lax.all_to_all(x, axis, split_axis=0, concat_axis=0, tiled=True)  73.9 us
    all_to_all x6, starting transfers between devices, exchange(): return lax.all_to_all(x, axis, split_axis=0, concat_axis=0, tiled=True)  39.7 us
    ppermute x3, waiting for transfers between devices, share_columns(): got.append(lax.ppermute(give, 'lon', pairs))  35.1 us
    ppermute x1, waiting for transfers between devices, share_pair(): lax.ppermute(give, 'lon', [(k, k ^ 2) for k in range(LONS)]).astype(F32)  30.9 us
    pallas_call x1, Pallas kernels, legendre_table(): pl.pallas_call(legendre_kernel, out_shape=jax.ShapeDtypeStruct((ORDERS, L...  9.14 us
    optimization_barrier x1, local copies, waits for them, and re-layouts, on_device(): lax.optimization_barrier((rows, forward, legendre))  9.07 us
    pallas_call x1, Pallas kernels, mix(): pl.pallas_call(mix_kernel, grid=(steps + TAIL,), out_shape=(pltpu.HBM((DE...  5.84 us
    pallas_call x1, Pallas kernels, synthesise(): pl.pallas_call(synthesise_kernel, grid=(ORDERS + TAIL,), out_shape=pltpu....  5.29 us
  transfers between devices with their start and end apart: 11, of which 7 were waited for; matrix products, arithmetic and copies ran while one was open for 10% of the time, Pallas kernels for 3%

profile of v5, /device:TPU:0, one launch (start us, length us, event | category | flops | bytes accessed | tf_op | source)
XLA Modules:
  0.0 262.8 jit_solution(2984666679857915488)
XLA Ops:
  0.6 3.3 %pad.4 = bf16[96,96,128]{2,1,0:T(8,128)(2,1)} pad(bf16[90,90,128]{2,1,0:T(8,128)(2,1)} %bitcast.65, bf16[]{:T(256)} %constant.313.clone.1), padding=0_6x0_6x0_0 | pad | bytes 4432898 | tf_op jit(solution)/shard_map/jit(_pad)/pad | solution.py:481
  3.9 8.2 %all-to-all-start = ((bf16[16,6,96,128]{3,2,1,0:T(8,128)(2,1)}), bf16[16,6,96,128]{3,2,1,0:T(8,128)(2,1)S(1)}, u32[]{:S(2)}, u32[]{:S(2)}) async-start(bf16[16,6,96,128]{3,2,1,0:T(8,128)(2,1)} %bitcast.57), calls=%async_computation | async-start | bytes 4718592 | tf_op jit(solution)/shard_map/all_to_all | solution.py:444
  12.1 0.1 subtract_multiply_fusion
  12.2 0.1 mul.419
  12.3 0.1 sub.155
  12.3 0.1 fusion.8
  12.4 0.1 gt.23
  12.6 0.1 div.175
  12.6 0.1 mul.421
  12.7 0.1 reshape.679.start
  12.8 0.7 fusion.74.seed
  13.5 0.1 fusion.73.sine_ref
  13.6 0.1 sqrt_select_fusion.2
  13.7 9.1 %legendre.1.table = bf16[5,768,768]{2,1,0:T(8,128)(2,1)S(1)} custom-call(f32[3600]{0:T(1024)S(1)} %get-tuple-element.37.up, f32[3600]{0:T(1024)S(1)} %get-tuple-element.36.back, f32[3600]{0:T(1024)S(1)} %reshape.679.start, f32[5]{0:T(128)S(1)} %fusion.74.seed, f32[5]{0:T(128)S(1)} %get-tuple-element.30.order, f32[8,128]{1,0:T(8,128)S(1)} %get-tuple-element.43.x_ref, ...), custom_call_target="tpu_custom_call" | custom-call | tf_op jit(solution)/shard_map/legendre/pallas_call | solution.py:205
  22.8 0.0 copy-start
  22.8 2.5 copy-done
  25.4 0.1 fusion.46
  25.5 4.3 %multiply_convert_fusion.1.table = bf16[2,640,768]{2,1,0:T(8,128)(2,1)} fusion(f32[768]{0:T(1024)S(1)} %fusion.67, f32[2,640]{1,0:T(2,128)S(1)} %fusion.44, f32[2,640]{1,0:T(2,128)S(1)} %fusion.46, f32[768]{0:T(1024)S(1)} %fusion.52), kind=kLoop, calls=%fused_computation.7 | loop fusion | flops 24576000 | bytes 1982464 | tf_op jit(solution)/shard_map/convert_element_type | solution.py:106
  29.8 14.3 %all-to-all-done.x_ref = bf16[16,6,96,128]{3,2,1,0:T(8,128)(2,1)S(1)} async-done(((bf16[16,6,96,128]{3,2,1,0:T(8,128)(2,1)}), bf16[16,6,96,128]{3,2,1,0:T(8,128)(2,1)S(1)}, u32[]{:S(2)}, u32[]{:S(2)}) %all-to-all-start) | async-done | bytes 2359328 | tf_op jit(solution)/shard_map/all_to_all | solution.py:444
  44.1 4.3 %fourier_forward.1 = bf16[4,2,960,128]{3,2,1,0:T(8,128)(2,1)} custom-call(bf16[2,640,768]{2,1,0:T(8,128)(2,1)} %multiply_convert_fusion.1.table, bf16[16,6,96,128]{3,2,1,0:T(8,128)(2,1)S(1)} %all-to-all-done.x_ref), custom_call_target="tpu_custom_call" | custom-call | tf_op jit(solution)/shard_map/fourier_forward/pallas_call | solution.py:249
  48.5 6.2 %all-to-all-start.1 = ((bf16[128,30,2,128]{3,2,1,0:T(2,128)(2,1)}), bf16[128,30,2,128]{3,2,1,0:T(2,128)(2,1)S(1)}, u32[]{:S(2)}, u32[]{:S(2)}) async-start(bf16[128,30,2,128]{3,2,1,0:T(2,128)(2,1)} %bitcast.61), calls=%async_computation.1 | async-start | bytes 3932160 | tf_op jit(solution)/shard_map/all_to_all | solution.py:444
  54.7 4.0 %copy.7 = bf16[90,8,5,2,128]{4,3,2,1,0:T(2,128)(2,1)} copy(bf16[90,8,5,2,128]{4,3,0,1,2:T(2,128)(2,1)} %bitcast.67) | data formatting | bytes 3686400 | tf_op jit(solution)/shard_map/transpose | solution.py:490
  58.7 9.1 %copy.6 = bf16[5,768,768]{1,2,0:T(8,128)(2,1)} copy(bf16[5,768,768]{2,1,0:T(8,128)(2,1)} %copy-done) | data formatting | bytes 11796480 | tf_op jit(solution)/shard_map/optimization_barrier | solution.py:485
  67.8 14.4 %all-to-all-done.1 = bf16[128,30,2,128]{3,2,1,0:T(2,128)(2,1)S(1)} async-done(((bf16[128,30,2,128]{3,2,1,0:T(2,128)(2,1)}), bf16[128,30,2,128]{3,2,1,0:T(2,128)(2,1)S(1)}, u32[]{:S(2)}, u32[]{:S(2)}) %all-to-all-start.1) | async-done | bytes 1966112 | tf_op jit(solution)/shard_map/all_to_all | solution.py:444
  82.1 5.1 %analyse.1 = bf16[8,10,96,128]{3,2,1,0:T(8,128)(2,1)} custom-call(bf16[5,768,768]{2,1,0:T(8,128)(2,1)} %copy-done, bf16[7680,128]{1,0:T(8,128)(2,1)S(1)} %bitcast.50), custom_call_target="tpu_custom_call" | custom-call | tf_op jit(solution)/shard_map/analyse/pallas_call | solution.py:281
  87.3 3.8 %all-to-all-start.2 = ((bf16[8,10,96,128]{3,2,1,0:T(8,128)(2,1)}), bf16[8,10,96,128]{3,2,1,0:T(8,128)(2,1)S(1)}, u32[]{:S(2)}, u32[]{:S(2)}) async-start(bf16[8,10,96,128]{3,2,1,0:T(8,128)(2,1)} %analyse.1), calls=%async_computation.2 | async-start | bytes 3932160 | tf_op jit(solution)/shard_map/all_to_all | solution.py:444
  91.1 4.6 %multiply_convert_fusion = bf16[768,1280]{1,0:T(8,128)(2,1)} fusion(f32[768]{0:T(1024)S(1)} %fusion.67, f32[1280]{0:T(1024)S(1)} %fusion.23, f32[1280]{0:T(1024)S(1)} %fusion.18, f32[768]{0:T(1024)S(1)} %fusion.52), kind=kLoop, calls=%fused_computation | loop fusion | flops 24576000 | bytes 1982464 | tf_op jit(solution)/shard_map/convert_element_type | solution.py:109
  95.7 21.9 %all-to-all-done.2 = bf16[8,10,96,128]{3,2,1,0:T(8,128)(2,1)S(1)} async-done(((bf16[8,10,96,128]{3,2,1,0:T(8,128)(2,1)}), bf16[8,10,96,128]{3,2,1,0:T(8,128)(2,1)S(1)}, u32[]{:S(2)}, u32[]{:S(2)}) %all-to-all-start.2) | async-done | bytes 1966112 | tf_op jit(solution)/shard_map/all_to_all | solution.py:444
  117.6 0.0 copy-start.2
  117.6 5.8 %mix.1 = (bf16[90,80,128]{2,1,0:T(8,128)(2,1)}, bf16[7680,128]{1,0:T(8,128)(2,1)}) custom-call(bf16[7680,128]{1,0:T(8,128)(2,1)S(1)} %bitcast.52, bf16[5,18,128,128]{3,2,1,0:T(8,128)(2,1)} %bitcast.64), custom_call_target="tpu_custom_call" | custom-call | tf_op jit(solution)/shard_map/mix/pallas_call | solution.py:335
  123.4 0.0 copy-done.2
  123.4 2.5 convolution_convert_fusion
  125.9 0.0 copy-start.1
  126.0 1.6 copy-done.1
  127.6 0.3 dynamic-slice_bitcast_fusion
  127.9 0.1 collective-permute-start
  128.0 8.5 %all-to-all-start.3 = ((bf16[8,10,96,128]{3,2,1,0:T(8,128)(2,1)}), bf16[8,10,96,128]{3,2,1,0:T(8,128)(2,1)S(1)}, u32[]{:S(2)}, u32[]{:S(2)}) async-start(bf16[8,10,96,128]{3,2,1,0:T(8,128)(2,1)} %bitcast.66), calls=%async_computation.3 | async-start | bytes 3932160 | tf_op jit(solution)/shard_map/all_to_all | solution.py:444
  136.5 0.0 collective-permute-done
  136.5 2.4 fusion.6
  138.9 0.4 constant_dynamic-slice_fusion.2
  139.4 23.3 %all-to-all-done.3.x_ref = bf16[8,10,96,128]{3,2,1,0:T(8,128)(2,1)S(1)} async-done(((bf16[8,10,96,128]{3,2,1,0:T(8,128)(2,1)}), bf16[8,10,96,128]{3,2,1,0:T(8,128)(2,1)S(1)}, u32[]{:S(2)}, u32[]{:S(2)}) %all-to-all-start.3) | async-done | bytes 1966112 | tf_op jit(solution)/shard_map/all_to_all | solution.py:444
  162.7 5.3 %synthesise.1 = bf16[7680,128]{1,0:T(8,128)(2,1)} custom-call(bf16[5,768,768]{2,1,0:T(8,128)(2,1)} %bitcast.53, bf16[8,10,96,128]{3,2,1,0:T(8,128)(2,1)S(1)} %all-to-all-done.3.x_ref), custom_call_target="tpu_custom_call" | custom-call | tf_op jit(solution)/shard_map/synthesise/pallas_call | solution.py:379
  168.0 8.3 %all-to-all-start.4 = ((bf16[128,30,2,128]{3,2,1,0:T(2,128)(2,1)}), bf16[128,30,2,128]{3,2,1,0:T(2,128)(2,1)S(1)}, u32[]{:S(2)}, u32[]{:S(2)}) async-start(bf16[128,30,2,128]{3,2,1,0:T(2,128)(2,1)} %bitcast.59), calls=%async_computation.4 | async-start | bytes 3932160 | tf_op jit(solution)/shard_map/all_to_all | solution.py:444
  176.4 1.1 collective-permute-start.1
  177.5 2.2 collective-permute-start.2
  179.8 1.7 collective-permute-start.3
  181.5 27.5 %collective-permute-done.1 = bf16[90,2,8,128]{3,2,0,1:T(8,128)(2,1)S(1)} collective-permute-done((bf16[90,2,8,128]{3,2,0,1:T(8,128)(2,1)S(1)}, bf16[90,2,8,128]{3,2,0,1:T(8,128)(2,1)S(1)}, u32[]{:S(2)}, u32[]{:S(2)}) %collective-permute-start.1) | collective-permute-done | bytes 368672 | tf_op jit(solution)/shard_map/ppermute | solution.py:463
  209.0 0.0 collective-permute-done.2
  209.0 7.6 %collective-permute-done.3 = bf16[90,2,8,128]{3,2,0,1:T(8,128)(2,1)S(1)} collective-permute-done((bf16[90,2,8,128]{3,2,0,1:T(8,128)(2,1)S(1)}, bf16[90,2,8,128]{3,2,0,1:T(8,128)(2,1)S(1)}, u32[]{:S(2)}, u32[]{:S(2)}) %collective-permute-start.3) | collective-permute-done | bytes 368672 | tf_op jit(solution)/shard_map/ppermute | solution.py:463
  216.6 0.2 convert_add_fusion.1
  216.8 0.0 all-to-all-done.4
  216.8 4.5 %fourier_backward.1 = bf16[2,8,6,96,128]{4,3,2,1,0:T(8,128)(2,1)} custom-call(bf16[2,384,1280]{2,1,0:T(8,128)(2,1)} %bitcast.60, bf16[7680,128]{1,0:T(8,128)(2,1)S(1)} %bitcast.51), custom_call_target="tpu_custom_call" | custom-call | tf_op jit(solution)/shard_map/fourier_backward/pallas_call | solution.py:427
  221.3 4.7 %all-to-all-start.5 = ((bf16[16,6,96,128]{3,2,1,0:T(8,128)(2,1)}), bf16[16,6,96,128]{3,2,1,0:T(8,128)(2,1)S(1)}, u32[]{:S(2)}, u32[]{:S(2)}) async-start(bf16[16,6,96,128]{3,2,1,0:T(8,128)(2,1)} %bitcast.56), calls=%async_computation.5 | async-start | bytes 4718592 | tf_op jit(solution)/shard_map/all_to_all | solution.py:444
  226.0 3.5 %collective-permute-start.4 = (bf16[90,8,128]{2,1,0:T(8,128)(2,1)S(1)}, bf16[90,8,128]{2,1,0:T(8,128)(2,1)S(1)}, u32[]{:S(2)}, u32[]{:S(2)}) collective-permute-start(bf16[90,8,128]{2,1,0:T(8,128)(2,1)S(1)} %fusion.7), channel_id=1, source_target_pairs={{0,2},{1,3},{2,0},{3,1},{4,6},{5,7},{6,4},{7,5},{8,10},{9,11},{10,... | collective-permute-start | bytes 552968 | tf_op jit(solution)/shard_map/ppermute | solution.py:471
  229.5 30.9 %collective-permute-done.4 = bf16[90,8,128]{2,1,0:T(8,128)(2,1)S(1)} collective-permute-done((bf16[90,8,128]{2,1,0:T(8,128)(2,1)S(1)}, bf16[90,8,128]{2,1,0:T(8,128)(2,1)S(1)}, u32[]{:S(2)}, u32[]{:S(2)}) %collective-permute-start.4) | collective-permute-done | bytes 184352 | tf_op jit(solution)/shard_map/ppermute | solution.py:471
  260.4 0.8 bitcast_add_fusion
  261.2 0.0 all-to-all-done.5
  261.2 0.1 slice.8
  261.3 1.5 slice_bitcast_fusion
  (19 shorter events, 0.3 us)
Async XLA Ops:
  3.9 40.2 %all-to-all-start = ((bf16[16,6,96,128]{3,2,1,0:T(8,128)(2,1)}), bf16[16,6,96,128]{3,2,1,0:T(8,128)(2,1)S(1)}, u32[]{:S(2)}, u32[]{:S(2)}) async-start(bf16[16,6,96,128]{3,2,1,0:T(8,128)(2,1)} %bitcast.57), calls=%async_computation | async-start | bytes 4718592 | tf_op jit(solution)/shard_map/all_to_all | solution.py:444
  22.8 2.5 copy-start
  48.5 33.7 %all-to-all-start.1 = ((bf16[128,30,2,128]{3,2,1,0:T(2,128)(2,1)}), bf16[128,30,2,128]{3,2,1,0:T(2,128)(2,1)S(1)}, u32[]{:S(2)}, u32[]{:S(2)}) async-start(bf16[128,30,2,128]{3,2,1,0:T(2,128)(2,1)} %bitcast.61), calls=%async_computation.1 | async-start | bytes 3932160 | tf_op jit(solution)/shard_map/all_to_all | solution.py:444
  87.3 30.3 %all-to-all-start.2 = ((bf16[8,10,96,128]{3,2,1,0:T(8,128)(2,1)}), bf16[8,10,96,128]{3,2,1,0:T(8,128)(2,1)S(1)}, u32[]{:S(2)}, u32[]{:S(2)}) async-start(bf16[8,10,96,128]{3,2,1,0:T(8,128)(2,1)} %analyse.1), calls=%async_computation.2 | async-start | bytes 3932160 | tf_op jit(solution)/shard_map/all_to_all | solution.py:444
  117.6 5.9 %copy-start.2 = (bf16[90,8,5,2,128]{4,3,2,1,0:T(2,128)(2,1)S(1)}, bf16[90,8,5,2,128]{4,3,2,1,0:T(2,128)(2,1)}, u32[]{:S(2)}) copy-start(bf16[90,8,5,2,128]{4,3,2,1,0:T(2,128)(2,1)} %copy.7) | copy-start | bytes 5529604
  125.9 1.6 copy-start.1
  127.9 8.6 %collective-permute-start = (bf16[90,8,8,128]{3,2,1,0:T(8,128)(2,1)S(1)}, bf16[90,8,8,128]{3,2,1,0:T(8,128)(2,1)}, u32[]{:S(2)}, u32[]{:S(2)}) collective-permute-start(bf16[90,8,8,128]{3,2,1,0:T(8,128)(2,1)S(1)} %dynamic-slice_bitcast_fusion), channel_id=1, source_target_pairs={{0,1},{1,0},{2,3},{3,2},{4,5},{5,4},{6,7},{7,6},{8,9},{9,8},{10,11... | collective-permute-start | bytes 4423688 | tf_op jit(solution)/shard_map/ppermute | solution.py:452
  128.0 34.7 %all-to-all-start.3 = ((bf16[8,10,96,128]{3,2,1,0:T(8,128)(2,1)}), bf16[8,10,96,128]{3,2,1,0:T(8,128)(2,1)S(1)}, u32[]{:S(2)}, u32[]{:S(2)}) async-start(bf16[8,10,96,128]{3,2,1,0:T(8,128)(2,1)} %bitcast.66), calls=%async_computation.3 | async-start | bytes 3932160 | tf_op jit(solution)/shard_map/all_to_all | solution.py:444
  168.0 48.8 %all-to-all-start.4 = ((bf16[128,30,2,128]{3,2,1,0:T(2,128)(2,1)}), bf16[128,30,2,128]{3,2,1,0:T(2,128)(2,1)S(1)}, u32[]{:S(2)}, u32[]{:S(2)}) async-start(bf16[128,30,2,128]{3,2,1,0:T(2,128)(2,1)} %bitcast.59), calls=%async_computation.4 | async-start | bytes 3932160 | tf_op jit(solution)/shard_map/all_to_all | solution.py:444
  176.4 32.6 %collective-permute-start.1 = (bf16[90,2,8,128]{3,2,0,1:T(8,128)(2,1)S(1)}, bf16[90,2,8,128]{3,2,0,1:T(8,128)(2,1)S(1)}, u32[]{:S(2)}, u32[]{:S(2)}) collective-permute-start(bf16[90,2,8,128]{3,2,0,1:T(8,128)(2,1)S(1)} %bitcast.69), channel_id=1, source_target_pairs={{0,4},{1,5},{2,6},{3,7},{4,8},{5,9},{6,10},{7,11},{8,12},{9,13},{1... | collective-permute-start | bytes 1105928 | tf_op jit(solution)/shard_map/ppermute | solution.py:463
  177.5 31.4 %collective-permute-start.2 = (bf16[90,2,8,128]{3,2,0,1:T(8,128)(2,1)S(1)}, bf16[90,2,8,128]{3,2,0,1:T(8,128)(2,1)S(1)}, u32[]{:S(2)}, u32[]{:S(2)}) collective-permute-start(bf16[90,2,8,128]{3,2,0,1:T(8,128)(2,1)S(1)} %bitcast.70), channel_id=1, source_target_pairs={{0,12},{1,13},{2,14},{3,15},{4,0},{5,1},{6,2},{7,3},{8,4},{9,5},{1... | collective-permute-start | bytes 1105928 | tf_op jit(solution)/shard_map/ppermute | solution.py:463
  179.8 36.8 %collective-permute-start.3 = (bf16[90,2,8,128]{3,2,0,1:T(8,128)(2,1)S(1)}, bf16[90,2,8,128]{3,2,0,1:T(8,128)(2,1)S(1)}, u32[]{:S(2)}, u32[]{:S(2)}) collective-permute-start(bf16[90,2,8,128]{3,2,0,1:T(8,128)(2,1)S(1)} %bitcast.71), channel_id=1, source_target_pairs={{0,8},{1,9},{2,10},{3,11},{4,12},{5,13},{6,14},{7,15},{8,0},{9,1},... | collective-permute-start | bytes 1105928 | tf_op jit(solution)/shard_map/ppermute | solution.py:463
  221.3 39.9 %all-to-all-start.5 = ((bf16[16,6,96,128]{3,2,1,0:T(8,128)(2,1)}), bf16[16,6,96,128]{3,2,1,0:T(8,128)(2,1)S(1)}, u32[]{:S(2)}, u32[]{:S(2)}) async-start(bf16[16,6,96,128]{3,2,1,0:T(8,128)(2,1)} %bitcast.56), calls=%async_computation.5 | async-start | bytes 4718592 | tf_op jit(solution)/shard_map/all_to_all | solution.py:444
  226.0 34.4 %collective-permute-start.4 = (bf16[90,8,128]{2,1,0:T(8,128)(2,1)S(1)}, bf16[90,8,128]{2,1,0:T(8,128)(2,1)S(1)}, u32[]{:S(2)}, u32[]{:S(2)}) collective-permute-start(bf16[90,8,128]{2,1,0:T(8,128)(2,1)S(1)} %fusion.7), channel_id=1, source_target_pairs={{0,2},{1,3},{2,0},{3,1},{4,6},{5,7},{6,4},{7,5},{8,10},{9,11},{10,... | collective-permute-start | bytes 552968 | tf_op jit(solution)/shard_map/ppermute | solution.py:471

commit v6 on v5

--- a/solution.py
+++ b/solution.py
@@ -350,6 +350,40 @@
     )(near(x), far(weights))
 
 
+def weigh_kernel(place, stored, gathered, keep, give):
+    core, z = place[0], place[1]
+    share = C // LONS
+    for offset in range(stored.shape[0]):
+        part = lax.dot_general(
+            stored[offset], gathered[offset], (((0,), (0,)), ((), ())), preferred_element_type=F32
+        )
+        for column in range(4):
+            to = lax.rem(column + 4 - z, 4)
+            piece = part[column * 4 * share : column * 4 * share + 4 * share]
+            here = jnp.concatenate([piece[:share], piece[2 * share : 3 * share]], axis=0)
+            there = jnp.concatenate([piece[share : 2 * share], piece[3 * share :]], axis=0)
+            keep[to, offset] = jnp.where(core == 0, here, there).astype(BF16)
+            give[to, offset] = jnp.where(core == 0, there, here).astype(BF16)
+
+
+def weigh(stored, gathered):
+    steps = 5
+    each = DEGREES // steps
+    lon = lax.axis_index("lon")
+    shape = (4, DEGREES, C // 8, C)
+    rows = pl.BlockSpec((each, LATS * Q, C), lambda g: (g, 0, 0))
+    sums = pl.BlockSpec((4, each, C // 8, C), lambda g: (0, g, 0, 0))
+    return pl.pallas_call(
+        weigh_kernel,
+        grid=(steps,),
+        out_shape=(pltpu.HBM(shape, BF16), pltpu.HBM(shape, BF16)),
+        in_specs=[pl.BlockSpec(memory_space=pltpu.SMEM), rows, rows],
+        out_specs=(sums, sums),
+        compiler_params=limit(20),
+        name="weigh",
+    )(jnp.stack([lon & 1, lon >> 2]), far(stored), far(gathered))
+
+
 def synthesise_kernel(table, x_ref, out_ref, made, held, ready):
     g = pl.program_id(0)
     arrive = stream(table, held, ready, ORDERS)
@@ -444,26 +478,6 @@
     return lax.all_to_all(x, axis, split_axis=0, concat_axis=0, tiled=True)
 
 
-def share_cores(held):
-    core = lax.axis_index("lon") & 1
-    held = held.reshape(DEGREES, LONS // 2, 2, C // LONS, C)
-    keep = lax.dynamic_index_in_dim(held, core, 2, keepdims=False)
-    give = lax.dynamic_index_in_dim(held, 1 - core, 2, keepdims=False)
-    got = lax.ppermute(give, "lon", [(k, k ^ 1) for k in range(LONS)])
-    return (keep.astype(F32) + got.astype(F32)).astype(BF16)
-
-
-def share_columns(held):
-    z = lax.axis_index("lon") >> 2
-    held = held.reshape(DEGREES, 4, 2, C // LONS, C)
-    got = []
-    for step in (1, 3, 2):
-        give = lax.dynamic_index_in_dim(held, (z + step) % 4, 1, keepdims=False)
-        pairs = [(k, (k + 4 * step) % LONS) for k in range(LONS)]
-        got.append(lax.ppermute(give, "lon", pairs))
-    return lax.dynamic_index_in_dim(held, z, 1, keepdims=False), got
-
-
 def share_pair(held):
     y = (lax.axis_index("lon") >> 1) & 1
     keep = lax.dynamic_index_in_dim(held, y, 1, keepdims=False)
@@ -496,17 +510,20 @@
     gathered, spec_local = mix(analysed, weights)
     spec_grad = exchange(spec_local.reshape(LATS, Q, PAD, C), "lat")
 
-    held = jnp.einsum("lrc,lrd->lcd", stored, gathered, preferred_element_type=F32)
-    held = held.astype(BF16)
-    held = share_cores(held)
-    held, got = share_columns(held)
+    keep, give = weigh(stored, gathered)
+    got = lax.ppermute(give, "lon", [(k, k ^ 1) for k in range(LONS)])
+    sums = [keep[step].astype(F32) + got[step].astype(F32) for step in range(4)]
+    held, got = sums[0], []
+    for step in (1, 3, 2):
+        pairs = [(k, (k + 4 * step) % LONS) for k in range(LONS)]
+        got.append(lax.ppermute(sums[step].astype(BF16), "lon", pairs))
     spec_grad, held = lax.optimization_barrier((spec_grad, held))
 
     row_block = synthesise(turned, spec_grad)
     row_block = exchange(cells(row_block), both)
-    held = held.astype(F32)
     for part in got:
         held = held + part.astype(F32)
+    held = held.reshape(DEGREES, 2, C // LONS, C)
     row_block, held = lax.optimization_barrier((row_block, held))
     grid_part = fourier_backward(backward, row_block.reshape(DEVICES * CHUNK, C))
     grid_part = exchange(grid_part.reshape(LONS, SLOT, PAD, C), "lon")

time: 264 us -> 266 us (level)
  Pallas kernels: 34.2 us -> 40.1 us
    pallas_call x0 -> x1, Pallas kernels: none -> 5.91 us  [weigh(): pl.pallas_call(weigh_kernel, grid=(steps,), out_shape=(pltpu.HBM(shape, B...]
    reshape x0 -> x1, local copies, waits for them, and re-layouts: none -> 4.01 us  [on_device(): spectrum.reshape(ORDERS, LATS, DEGREES, 2, C).transpose(2, 1, 0, 3, 4)]
    transpose x1 -> x0, local copies, waits for them, and re-layouts: 4.01 us -> none  [on_device(): spectrum.reshape(ORDERS, LATS, DEGREES, 2, C).transpose(2, 1, 0, 3, 4)]
  transfers between devices with their start and end apart: 11 -> 11, of which waited for: 7 -> 7; matrix products, arithmetic and copies ran while one was open for 10% -> 11% of each run, Pallas kernels for 3% -> 3%
where the time goes in v6:
time: 266 us; the launch traced here: 264 us
  waiting for transfers between devices  138 us (52%)
  starting transfers between devices  47.9 us (18%)
  Pallas kernels  40.1 us (15%)
  local copies, waits for them, and re-layouts  23.6 us (9%)
  other arithmetic  13.3 us (5%)
    all_to_all x6, waiting for transfers between devices, exchange(): return lax.all_to_all(x, axis, split_axis=0, concat_axis=0, tiled=True)  72.8 us
    all_to_all x6, starting transfers between devices, exchange(): return lax.all_to_all(x, axis, split_axis=0, concat_axis=0, tiled=True)  39.5 us
    ppermute x3, waiting for transfers between devices, on_device(): got.append(lax.ppermute(sums[step].astype(BF16), 'lon', pairs))  35.3 us
    ppermute x1, waiting for transfers between devices, share_pair(): lax.ppermute(give, 'lon', [(k, k ^ 2) for k in range(LONS)]).astype(F32)  30.3 us
    pallas_call x1, Pallas kernels, legendre_table(): pl.pallas_call(legendre_kernel, out_shape=jax.ShapeDtypeStruct((ORDERS, L...  9.14 us
    optimization_barrier x1, local copies, waits for them, and re-layouts, on_device(): lax.optimization_barrier((rows, forward, legendre))  9.07 us
    pallas_call x1, Pallas kernels, weigh(): pl.pallas_call(weigh_kernel, grid=(steps,), out_shape=(pltpu.HBM(shape, B...  5.91 us
    pallas_call x1, Pallas kernels, mix(): pl.pallas_call(mix_kernel, grid=(steps + TAIL,), out_shape=(pltpu.HBM((DE...  5.85 us
  transfers between devices with their start and end apart: 11, of which 7 were waited for; matrix products, arithmetic and copies ran while one was open for 11% of the time, Pallas kernels for 3%

profile of v6, /device:TPU:0, one launch (start us, length us, event | category | flops | bytes accessed | tf_op | source)
XLA Modules:
  0.0 264.2 jit_solution(8191785592064136585)
XLA Ops:
  0.6 3.3 %pad.4 = bf16[96,96,128]{2,1,0:T(8,128)(2,1)} pad(bf16[90,90,128]{2,1,0:T(8,128)(2,1)} %bitcast.53, bf16[]{:T(256)} %constant.277.clone.1), padding=0_6x0_6x0_0 | pad | bytes 4432898 | tf_op jit(solution)/shard_map/jit(_pad)/pad | solution.py:495
  3.9 8.2 %all-to-all-start = ((bf16[16,6,96,128]{3,2,1,0:T(8,128)(2,1)}), bf16[16,6,96,128]{3,2,1,0:T(8,128)(2,1)S(1)}, u32[]{:S(2)}, u32[]{:S(2)}) async-start(bf16[16,6,96,128]{3,2,1,0:T(8,128)(2,1)} %bitcast.46), calls=%async_computation | async-start | bytes 4718592 | tf_op jit(solution)/shard_map/all_to_all | solution.py:478
  12.1 0.1 subtract_multiply_fusion
  12.2 0.1 mul.419
  12.3 0.1 sub.152
  12.3 0.1 fusion.10
  12.4 0.1 gt.23
  12.6 0.1 div.175
  12.6 0.1 mul.421
  12.7 0.1 reshape.688.start
  12.8 0.7 fusion.76.seed
  13.5 0.1 fusion.75.sine_ref
  13.6 0.1 sqrt_select_fusion.2
  13.7 9.1 %legendre.1.table = bf16[5,768,768]{2,1,0:T(8,128)(2,1)S(1)} custom-call(f32[3600]{0:T(1024)S(1)} %get-tuple-element.41.up, f32[3600]{0:T(1024)S(1)} %get-tuple-element.40.back, f32[3600]{0:T(1024)S(1)} %reshape.688.start, f32[5]{0:T(128)S(1)} %fusion.76.seed, f32[5]{0:T(128)S(1)} %get-tuple-element.34.order, f32[8,128]{1,0:T(8,128)S(1)} %get-tuple-element.49.x_ref, ...), custom_call_target="tpu_custom_call" | custom-call | tf_op jit(solution)/shard_map/legendre/pallas_call | solution.py:205
  22.8 0.0 copy-start
  22.8 2.5 copy-done
  25.4 0.1 fusion.48
  25.5 4.3 %multiply_convert_fusion.1.table = bf16[2,640,768]{2,1,0:T(8,128)(2,1)} fusion(f32[768]{0:T(1024)S(1)} %fusion.69, f32[2,640]{1,0:T(2,128)S(1)} %fusion.46, f32[2,640]{1,0:T(2,128)S(1)} %fusion.48, f32[768]{0:T(1024)S(1)} %fusion.54), kind=kLoop, calls=%fused_computation.7 | loop fusion | flops 24576000 | bytes 1982464 | tf_op jit(solution)/shard_map/convert_element_type | solution.py:106
  29.8 14.3 %all-to-all-done.x_ref = bf16[16,6,96,128]{3,2,1,0:T(8,128)(2,1)S(1)} async-done(((bf16[16,6,96,128]{3,2,1,0:T(8,128)(2,1)}), bf16[16,6,96,128]{3,2,1,0:T(8,128)(2,1)S(1)}, u32[]{:S(2)}, u32[]{:S(2)}) %all-to-all-start) | async-done | bytes 2359328 | tf_op jit(solution)/shard_map/all_to_all | solution.py:478
  44.1 4.3 %fourier_forward.1 = bf16[4,2,960,128]{3,2,1,0:T(8,128)(2,1)} custom-call(bf16[2,640,768]{2,1,0:T(8,128)(2,1)} %multiply_convert_fusion.1.table, bf16[16,6,96,128]{3,2,1,0:T(8,128)(2,1)S(1)} %all-to-all-done.x_ref), custom_call_target="tpu_custom_call" | custom-call | tf_op jit(solution)/shard_map/fourier_forward/pallas_call | solution.py:249
  48.5 6.2 %all-to-all-start.1 = ((bf16[128,30,2,128]{3,2,1,0:T(2,128)(2,1)}), bf16[128,30,2,128]{3,2,1,0:T(2,128)(2,1)S(1)}, u32[]{:S(2)}, u32[]{:S(2)}) async-start(bf16[128,30,2,128]{3,2,1,0:T(2,128)(2,1)} %bitcast.50), calls=%async_computation.1 | async-start | bytes 3932160 | tf_op jit(solution)/shard_map/all_to_all | solution.py:478
  54.7 4.0 %copy.7 = bf16[5,8,90,2,128]{4,3,0,1,2:T(2,128)(2,1)} copy(bf16[5,8,90,2,128]{4,3,2,1,0:T(2,128)(2,1)} %bitcast.55) | data formatting | bytes 3686400 | tf_op jit(solution)/shard_map/reshape | solution.py:504
  58.7 9.1 %copy.6 = bf16[5,768,768]{1,2,0:T(8,128)(2,1)} copy(bf16[5,768,768]{2,1,0:T(8,128)(2,1)} %copy-done) | data formatting | bytes 11796480 | tf_op jit(solution)/shard_map/optimization_barrier | solution.py:499
  67.8 14.4 %all-to-all-done.1 = bf16[128,30,2,128]{3,2,1,0:T(2,128)(2,1)S(1)} async-done(((bf16[128,30,2,128]{3,2,1,0:T(2,128)(2,1)}), bf16[128,30,2,128]{3,2,1,0:T(2,128)(2,1)S(1)}, u32[]{:S(2)}, u32[]{:S(2)}) %all-to-all-start.1) | async-done | bytes 1966112 | tf_op jit(solution)/shard_map/all_to_all | solution.py:478
  82.1 5.1 %analyse.1 = bf16[8,10,96,128]{3,2,1,0:T(8,128)(2,1)} custom-call(bf16[5,768,768]{2,1,0:T(8,128)(2,1)} %copy-done, bf16[7680,128]{1,0:T(8,128)(2,1)S(1)} %bitcast.41), custom_call_target="tpu_custom_call" | custom-call | tf_op jit(solution)/shard_map/analyse/pallas_call | solution.py:281
  87.3 3.6 %all-to-all-start.2 = ((bf16[8,10,96,128]{3,2,1,0:T(8,128)(2,1)}), bf16[8,10,96,128]{3,2,1,0:T(8,128)(2,1)S(1)}, u32[]{:S(2)}, u32[]{:S(2)}) async-start(bf16[8,10,96,128]{3,2,1,0:T(8,128)(2,1)} %analyse.1), calls=%async_computation.2 | async-start | bytes 3932160 | tf_op jit(solution)/shard_map/all_to_all | solution.py:478
  90.9 0.1 pad_add_fusion.place
  91.0 4.6 %multiply_convert_fusion = bf16[768,1280]{1,0:T(8,128)(2,1)} fusion(f32[768]{0:T(1024)S(1)} %fusion.69, f32[1280]{0:T(1024)S(1)} %fusion.25, f32[1280]{0:T(1024)S(1)} %fusion.20, f32[768]{0:T(1024)S(1)} %fusion.54), kind=kLoop, calls=%fused_computation | loop fusion | flops 24576000 | bytes 1982464 | tf_op jit(solution)/shard_map/convert_element_type | solution.py:109
  95.6 22.0 %all-to-all-done.2 = bf16[8,10,96,128]{3,2,1,0:T(8,128)(2,1)S(1)} async-done(((bf16[8,10,96,128]{3,2,1,0:T(8,128)(2,1)}), bf16[8,10,96,128]{3,2,1,0:T(8,128)(2,1)S(1)}, u32[]{:S(2)}, u32[]{:S(2)}) %all-to-all-start.2) | async-done | bytes 1966112 | tf_op jit(solution)/shard_map/all_to_all | solution.py:478
  117.6 5.8 %mix.1 = (bf16[90,80,128]{2,1,0:T(8,128)(2,1)}, bf16[7680,128]{1,0:T(8,128)(2,1)}) custom-call(bf16[7680,128]{1,0:T(8,128)(2,1)S(1)} %bitcast.43, bf16[5,18,128,128]{3,2,1,0:T(8,128)(2,1)} %bitcast.52), custom_call_target="tpu_custom_call" | custom-call | tf_op jit(solution)/shard_map/mix/pallas_call | solution.py:335
  123.4 5.9 %weigh.1 = (bf16[4,90,16,128]{3,2,1,0:T(8,128)(2,1)}, bf16[4,90,16,128]{3,2,1,0:T(8,128)(2,1)}) custom-call(s32[2]{0:T(128)S(1)} %pad_add_fusion.place, bf16[90,80,128]{2,1,0:T(8,128)(2,1)} %bitcast.51, bf16[90,80,128]{2,1,0:T(8,128)(2,1)} %get-tuple-element.27.gathered), custom_call_target="tpu_custom_call" | custom-call | tf_op jit(solution)/shard_map/weigh/pallas_call | solution.py:376
  129.3 0.0 collective-permute-start
  129.3 8.5 %all-to-all-start.3 = ((bf16[8,10,96,128]{3,2,1,0:T(8,128)(2,1)}), bf16[8,10,96,128]{3,2,1,0:T(8,128)(2,1)S(1)}, u32[]{:S(2)}, u32[]{:S(2)}) async-start(bf16[8,10,96,128]{3,2,1,0:T(8,128)(2,1)} %bitcast.54), calls=%async_computation.3 | async-start | bytes 3932160 | tf_op jit(solution)/shard_map/all_to_all | solution.py:478
  137.9 0.0 collective-permute-done
  137.9 0.0 copy-start.1
  137.9 1.2 copy-done.1
  139.1 2.9 %fusion.6 = (bf16[90,16,128]{2,1,0:T(8,128)(2,1)}, bf16[90,16,128]{2,1,0:T(8,128)(2,1)S(1)}, bf16[90,16,128]{2,1,0:T(8,128)(2,1)S(1)}, f32[90,16,128]{2,1,0:T(8,128)S(1)}) fusion(bf16[4,90,16,128]{3,2,1,0:T(8,128)(2,1)} %copy-done.1, bf16[4,90,16,128]{3,2,1,0:T(8,128)(2,1)} %get-tuple-element.28), kind=kLoop, calls=%fused_computation.20 | loop fusion | flops 2764800 | bytes 4792320 | tf_op jit(solution)/shard_map/convert_element_type | solution.py:519
  142.0 22.1 %all-to-all-done.3.x_ref = bf16[8,10,96,128]{3,2,1,0:T(8,128)(2,1)S(1)} async-done(((bf16[8,10,96,128]{3,2,1,0:T(8,128)(2,1)}), bf16[8,10,96,128]{3,2,1,0:T(8,128)(2,1)S(1)}, u32[]{:S(2)}, u32[]{:S(2)}) %all-to-all-start.3) | async-done | bytes 1966112 | tf_op jit(solution)/shard_map/all_to_all | solution.py:478
  164.1 5.3 %synthesise.1 = bf16[7680,128]{1,0:T(8,128)(2,1)} custom-call(bf16[5,768,768]{2,1,0:T(8,128)(2,1)} %bitcast.44, bf16[8,10,96,128]{3,2,1,0:T(8,128)(2,1)S(1)} %all-to-all-done.3.x_ref), custom_call_target="tpu_custom_call" | custom-call | tf_op jit(solution)/shard_map/synthesise/pallas_call | solution.py:413
  169.4 8.4 %all-to-all-start.4 = ((bf16[128,30,2,128]{3,2,1,0:T(2,128)(2,1)}), bf16[128,30,2,128]{3,2,1,0:T(2,128)(2,1)S(1)}, u32[]{:S(2)}, u32[]{:S(2)}) async-start(bf16[128,30,2,128]{3,2,1,0:T(2,128)(2,1)} %bitcast.48), calls=%async_computation.4 | async-start | bytes 3932160 | tf_op jit(solution)/shard_map/all_to_all | solution.py:478
  177.7 1.1 collective-permute-start.1
  178.9 2.2 collective-permute-start.2
  181.0 1.6 collective-permute-start.3
  182.7 27.8 %collective-permute-done.1 = bf16[90,16,128]{2,1,0:T(8,128)(2,1)S(1)} collective-permute-done((bf16[90,16,128]{2,1,0:T(8,128)(2,1)}, bf16[90,16,128]{2,1,0:T(8,128)(2,1)S(1)}, u32[]{:S(2)}, u32[]{:S(2)}) %collective-permute-start.1) | collective-permute-done | bytes 368672 | tf_op jit(solution)/shard_map/ppermute | solution.py:519
  210.5 0.0 collective-permute-done.2
  210.5 7.5 %collective-permute-done.3 = bf16[90,16,128]{2,1,0:T(8,128)(2,1)S(1)} collective-permute-done((bf16[90,16,128]{2,1,0:T(8,128)(2,1)S(1)}, bf16[90,16,128]{2,1,0:T(8,128)(2,1)S(1)}, u32[]{:S(2)}, u32[]{:S(2)}) %collective-permute-start.3) | collective-permute-done | bytes 368672 | tf_op jit(solution)/shard_map/ppermute | solution.py:519
  218.0 0.2 add_bitcast_fusion
  218.2 0.0 all-to-all-done.4
  218.2 4.5 %fourier_backward.1 = bf16[2,8,6,96,128]{4,3,2,1,0:T(8,128)(2,1)} custom-call(bf16[2,384,1280]{2,1,0:T(8,128)(2,1)} %bitcast.49, bf16[7680,128]{1,0:T(8,128)(2,1)S(1)} %bitcast.42), custom_call_target="tpu_custom_call" | custom-call | tf_op jit(solution)/shard_map/fourier_backward/pallas_call | solution.py:461
  222.7 4.7 %all-to-all-start.5 = ((bf16[16,6,96,128]{3,2,1,0:T(8,128)(2,1)}), bf16[16,6,96,128]{3,2,1,0:T(8,128)(2,1)S(1)}, u32[]{:S(2)}, u32[]{:S(2)}) async-start(bf16[16,6,96,128]{3,2,1,0:T(8,128)(2,1)} %bitcast.45), calls=%async_computation.5 | async-start | bytes 4718592 | tf_op jit(solution)/shard_map/all_to_all | solution.py:478
  227.4 0.7 fusion.9
  228.1 3.4 %collective-permute-start.4 = (bf16[90,8,128]{2,1,0:T(8,128)(2,1)}, bf16[90,8,128]{2,1,0:T(8,128)(2,1)S(1)}, u32[]{:S(2)}, u32[]{:S(2)}) collective-permute-start(bf16[90,8,128]{2,1,0:T(8,128)(2,1)} %fusion.9), channel_id=1, source_target_pairs={{0,2},{1,3},{2,0},{3,1},{4,6},{5,7},{6,4},{7,5},{8,10},{9,11},{10,... | collective-permute-start | bytes 552968 | tf_op jit(solution)/shard_map/ppermute | solution.py:485
  231.5 30.3 %collective-permute-done.4 = bf16[90,8,128]{2,1,0:T(8,128)(2,1)S(1)} collective-permute-done((bf16[90,8,128]{2,1,0:T(8,128)(2,1)}, bf16[90,8,128]{2,1,0:T(8,128)(2,1)S(1)}, u32[]{:S(2)}, u32[]{:S(2)}) %collective-permute-start.4) | collective-permute-done | bytes 184352 | tf_op jit(solution)/shard_map/ppermute | solution.py:485
  261.8 0.8 bitcast_add_fusion
  262.6 0.0 all-to-all-done.5
  262.6 0.1 slice.44
  262.7 1.5 slice_bitcast_fusion
  (14 shorter events, 0.2 us)
Async XLA Ops:
  3.9 40.2 %all-to-all-start = ((bf16[16,6,96,128]{3,2,1,0:T(8,128)(2,1)}), bf16[16,6,96,128]{3,2,1,0:T(8,128)(2,1)S(1)}, u32[]{:S(2)}, u32[]{:S(2)}) async-start(bf16[16,6,96,128]{3,2,1,0:T(8,128)(2,1)} %bitcast.46), calls=%async_computation | async-start | bytes 4718592 | tf_op jit(solution)/shard_map/all_to_all | solution.py:478
  22.8 2.5 copy-start
  48.5 33.7 %all-to-all-start.1 = ((bf16[128,30,2,128]{3,2,1,0:T(2,128)(2,1)}), bf16[128,30,2,128]{3,2,1,0:T(2,128)(2,1)S(1)}, u32[]{:S(2)}, u32[]{:S(2)}) async-start(bf16[128,30,2,128]{3,2,1,0:T(2,128)(2,1)} %bitcast.50), calls=%async_computation.1 | async-start | bytes 3932160 | tf_op jit(solution)/shard_map/all_to_all | solution.py:478
  87.3 30.3 %all-to-all-start.2 = ((bf16[8,10,96,128]{3,2,1,0:T(8,128)(2,1)}), bf16[8,10,96,128]{3,2,1,0:T(8,128)(2,1)S(1)}, u32[]{:S(2)}, u32[]{:S(2)}) async-start(bf16[8,10,96,128]{3,2,1,0:T(8,128)(2,1)} %analyse.1), calls=%async_computation.2 | async-start | bytes 3932160 | tf_op jit(solution)/shard_map/all_to_all | solution.py:478
  129.3 8.5 %collective-permute-start = (bf16[4,90,16,128]{3,2,1,0:T(8,128)(2,1)}, bf16[4,90,16,128]{3,2,1,0:T(8,128)(2,1)S(1)}, u32[]{:S(2)}, u32[]{:S(2)}) collective-permute-start(bf16[4,90,16,128]{3,2,1,0:T(8,128)(2,1)} %get-tuple-element.29), channel_id=1, source_target_pairs={{0,1},{1,0},{2,3},{3,2},{4,5},{5,4},{6,7},{7,6},{8,9},{9,8},{10,11... | collective-permute-start | bytes 4423688 | tf_op jit(solution)/shard_map/ppermute | solution.py:514
  129.3 34.7 %all-to-all-start.3 = ((bf16[8,10,96,128]{3,2,1,0:T(8,128)(2,1)}), bf16[8,10,96,128]{3,2,1,0:T(8,128)(2,1)S(1)}, u32[]{:S(2)}, u32[]{:S(2)}) async-start(bf16[8,10,96,128]{3,2,1,0:T(8,128)(2,1)} %bitcast.54), calls=%async_computation.3 | async-start | bytes 3932160 | tf_op jit(solution)/shard_map/all_to_all | solution.py:478
  137.9 1.2 copy-start.1
  169.4 48.8 %all-to-all-start.4 = ((bf16[128,30,2,128]{3,2,1,0:T(2,128)(2,1)}), bf16[128,30,2,128]{3,2,1,0:T(2,128)(2,1)S(1)}, u32[]{:S(2)}, u32[]{:S(2)}) async-start(bf16[128,30,2,128]{3,2,1,0:T(2,128)(2,1)} %bitcast.48), calls=%async_computation.4 | async-start | bytes 3932160 | tf_op jit(solution)/shard_map/all_to_all | solution.py:478
  177.7 32.8 %collective-permute-start.1 = (bf16[90,16,128]{2,1,0:T(8,128)(2,1)}, bf16[90,16,128]{2,1,0:T(8,128)(2,1)S(1)}, u32[]{:S(2)}, u32[]{:S(2)}) collective-permute-start(bf16[90,16,128]{2,1,0:T(8,128)(2,1)} %get-tuple-element.36), channel_id=1, source_target_pairs={{0,4},{1,5},{2,6},{3,7},{4,8},{5,9},{6,10},{7,11},{8,12},{9,13},{1... | collective-permute-start | bytes 1105928 | tf_op jit(solution)/shard_map/ppermute | solution.py:519
  178.9 31.6 %collective-permute-start.2 = (bf16[90,16,128]{2,1,0:T(8,128)(2,1)S(1)}, bf16[90,16,128]{2,1,0:T(8,128)(2,1)S(1)}, u32[]{:S(2)}, u32[]{:S(2)}) collective-permute-start(bf16[90,16,128]{2,1,0:T(8,128)(2,1)S(1)} %get-tuple-element.38), channel_id=1, source_target_pairs={{0,12},{1,13},{2,14},{3,15},{4,0},{5,1},{6,2},{7,3},{8,4},{9,5},{1... | collective-permute-start | bytes 1105928 | tf_op jit(solution)/shard_map/ppermute | solution.py:519
  181.0 37.0 %collective-permute-start.3 = (bf16[90,16,128]{2,1,0:T(8,128)(2,1)S(1)}, bf16[90,16,128]{2,1,0:T(8,128)(2,1)S(1)}, u32[]{:S(2)}, u32[]{:S(2)}) collective-permute-start(bf16[90,16,128]{2,1,0:T(8,128)(2,1)S(1)} %get-tuple-element.37), channel_id=1, source_target_pairs={{0,8},{1,9},{2,10},{3,11},{4,12},{5,13},{6,14},{7,15},{8,0},{9,1},... | collective-permute-start | bytes 1105928 | tf_op jit(solution)/shard_map/ppermute | solution.py:519
  222.7 39.9 %all-to-all-start.5 = ((bf16[16,6,96,128]{3,2,1,0:T(8,128)(2,1)}), bf16[16,6,96,128]{3,2,1,0:T(8,128)(2,1)S(1)}, u32[]{:S(2)}, u32[]{:S(2)}) async-start(bf16[16,6,96,128]{3,2,1,0:T(8,128)(2,1)} %bitcast.45), calls=%async_computation.5 | async-start | bytes 4718592 | tf_op jit(solution)/shard_map/all_to_all | solution.py:478
  228.1 33.7 %collective-permute-start.4 = (bf16[90,8,128]{2,1,0:T(8,128)(2,1)}, bf16[90,8,128]{2,1,0:T(8,128)(2,1)S(1)}, u32[]{:S(2)}, u32[]{:S(2)}) collective-permute-start(bf16[90,8,128]{2,1,0:T(8,128)(2,1)} %fusion.9), channel_id=1, source_target_pairs={{0,2},{1,3},{2,0},{3,1},{4,6},{5,7},{6,4},{7,5},{8,10},{9,11},{10,... | collective-permute-start | bytes 552968 | tf_op jit(solution)/shard_map/ppermute | solution.py:485

commit v7 on v6

--- a/solution.py
+++ b/solution.py
@@ -28,7 +28,8 @@
 CHUNK = Q * SLOT
 DEGREES = L // LATS
 BLOCK = 16
-TAIL = 2
+AHEAD = 2
+TAIL = 4
 SHIFT = 40
 
 F32 = jnp.float32
@@ -59,13 +60,17 @@
 
     @pl.when(g == 0)
     def _():
-        for step in range(steps):
+        for step in range(min(AHEAD, steps)):
             copy(step).start()
 
     def arrive():
         @pl.when(g < steps)
         def _():
             copy(jnp.minimum(g, steps - 1)).wait()
+
+        @pl.when(g + AHEAD < steps)
+        def _():
+            copy(jnp.minimum(g + AHEAD, steps - 1)).start()
 
     return arrive
 
@@ -478,13 +483,6 @@
     return lax.all_to_all(x, axis, split_axis=0, concat_axis=0, tiled=True)
 
 
-def share_pair(held):
-    y = (lax.axis_index("lon") >> 1) & 1
-    keep = lax.dynamic_index_in_dim(held, y, 1, keepdims=False)
-    give = lax.dynamic_index_in_dim(held, 1 - y, 1, keepdims=False).astype(BF16)
-    return keep + lax.ppermute(give, "lon", [(k, k ^ 2) for k in range(LONS)]).astype(F32)
-
-
 def cells(x):
     return x.reshape(DEVICES, CHUNK // 2, 2, C)
 
@@ -524,10 +522,14 @@
     for part in got:
         held = held + part.astype(F32)
     held = held.reshape(DEGREES, 2, C // LONS, C)
-    row_block, held = lax.optimization_barrier((row_block, held))
+    y = (lax.axis_index("lon") >> 1) & 1
+    keep = lax.dynamic_index_in_dim(held, y, 1, keepdims=False)
+    give = lax.dynamic_index_in_dim(held, 1 - y, 1, keepdims=False).astype(BF16)
+    row_block, keep, give = lax.optimization_barrier((row_block, keep, give))
     grid_part = fourier_backward(backward, row_block.reshape(DEVICES * CHUNK, C))
     grid_part = exchange(grid_part.reshape(LONS, SLOT, PAD, C), "lon")
-    weight_grad = share_pair(held)
+    got = lax.ppermute(give, "lon", [(k, k ^ 2) for k in range(LONS)])
+    weight_grad = keep + got.astype(F32)
     grad_in = grid_part[:USED].reshape(ROWS, PAD, C)[:, :COLS]
     return jnp.swapaxes(grad_in, 1, 2)[None], weight_grad
 

time: 266 us -> 269 us (1.011)
  no operation moved by 1% of the time
where the time goes in v7:
time: 269 us; the launch traced here: 267 us
  waiting for transfers between devices  139 us (52%)
  starting transfers between devices  47.9 us (18%)
  Pallas kernels  41.9 us (16%)
  local copies, waits for them, and re-layouts  23 us (9%)
  other arithmetic  14.4 us (5%)
    all_to_all x6, waiting for transfers between devices, exchange(): return lax.all_to_all(x, axis, split_axis=0, concat_axis=0, tiled=True)  72.7 us
    all_to_all x6, starting transfers between devices, exchange(): return lax.all_to_all(x, axis, split_axis=0, concat_axis=0, tiled=True)  39.5 us
    ppermute x3, waiting for transfers between devices, on_device(): got.append(lax.ppermute(sums[step].astype(BF16), 'lon', pairs))  35.4 us
    ppermute x1, waiting for transfers between devices, on_device(): got = lax.ppermute(give, 'lon', [(k, k ^ 2) for k in range(LONS)])  31 us
    pallas_call x1, Pallas kernels, legendre_table(): pl.pallas_call(legendre_kernel, out_shape=jax.ShapeDtypeStruct((ORDERS, L...  9.14 us
    optimization_barrier x1, local copies, waits for them, and re-layouts, on_device(): lax.optimization_barrier((rows, forward, legendre))  9.07 us
    pallas_call x1, Pallas kernels, synthesise(): pl.pallas_call(synthesise_kernel, grid=(ORDERS + TAIL,), out_shape=pltpu....  6.43 us
    pallas_call x1, Pallas kernels, mix(): pl.pallas_call(mix_kernel, grid=(steps + TAIL,), out_shape=(pltpu.HBM((DE...  6.36 us
  transfers between devices with their start and end apart: 11, of which 7 were waited for; matrix products, arithmetic and copies ran while one was open for 11% of the time, Pallas kernels for 3%

profile of v7, /device:TPU:0, one launch (start us, length us, event | category | flops | bytes accessed | tf_op | source)
XLA Modules:
  0.0 267.2 jit_solution(12066539833073155215)
XLA Ops:
  0.6 3.3 %pad.4 = bf16[96,96,128]{2,1,0:T(8,128)(2,1)} pad(bf16[90,90,128]{2,1,0:T(8,128)(2,1)} %bitcast.57, bf16[]{:T(256)} %constant.277.clone.1), padding=0_6x0_6x0_0 | pad | bytes 4432898 | tf_op jit(solution)/shard_map/jit(_pad)/pad | solution.py:493
  3.9 8.2 %all-to-all-start = ((bf16[16,6,96,128]{3,2,1,0:T(8,128)(2,1)}), bf16[16,6,96,128]{3,2,1,0:T(8,128)(2,1)S(1)}, u32[]{:S(2)}, u32[]{:S(2)}) async-start(bf16[16,6,96,128]{3,2,1,0:T(8,128)(2,1)} %bitcast.50), calls=%async_computation | async-start | bytes 4718592 | tf_op jit(solution)/shard_map/all_to_all | solution.py:483
  12.1 0.1 subtract_multiply_fusion
  12.2 0.1 mul.419
  12.3 0.1 sub.152
  12.3 0.1 fusion.10
  12.4 0.1 gt.23
  12.6 0.1 div.175
  12.6 0.1 mul.421
  12.7 0.1 reshape.688.start
  12.8 0.7 fusion.76.seed
  13.5 0.1 fusion.75.sine_ref
  13.6 0.1 sqrt_select_fusion.2
  13.7 9.1 %legendre.1.table = bf16[5,768,768]{2,1,0:T(8,128)(2,1)S(1)} custom-call(f32[3600]{0:T(1024)S(1)} %get-tuple-element.43.up, f32[3600]{0:T(1024)S(1)} %get-tuple-element.42.back, f32[3600]{0:T(1024)S(1)} %reshape.688.start, f32[5]{0:T(128)S(1)} %fusion.76.seed, f32[5]{0:T(128)S(1)} %get-tuple-element.36.order, f32[8,128]{1,0:T(8,128)S(1)} %get-tuple-element.51.x_ref, ...), custom_call_target="tpu_custom_call" | custom-call | tf_op jit(solution)/shard_map/legendre/pallas_call | solution.py:210
  22.8 0.0 copy-start
  22.8 2.5 copy-done
  25.4 0.1 fusion.48
  25.5 4.3 %multiply_convert_fusion.1.table = bf16[2,640,768]{2,1,0:T(8,128)(2,1)} fusion(f32[768]{0:T(1024)S(1)} %fusion.69, f32[2,640]{1,0:T(2,128)S(1)} %fusion.46, f32[2,640]{1,0:T(2,128)S(1)} %fusion.48, f32[768]{0:T(1024)S(1)} %fusion.54), kind=kLoop, calls=%fused_computation.7 | loop fusion | flops 24576000 | bytes 1982464 | tf_op jit(solution)/shard_map/convert_element_type | solution.py:111
  29.8 14.3 %all-to-all-done.x_ref = bf16[16,6,96,128]{3,2,1,0:T(8,128)(2,1)S(1)} async-done(((bf16[16,6,96,128]{3,2,1,0:T(8,128)(2,1)}), bf16[16,6,96,128]{3,2,1,0:T(8,128)(2,1)S(1)}, u32[]{:S(2)}, u32[]{:S(2)}) %all-to-all-start) | async-done | bytes 2359328 | tf_op jit(solution)/shard_map/all_to_all | solution.py:483
  44.1 4.3 %fourier_forward.1 = bf16[4,2,960,128]{3,2,1,0:T(8,128)(2,1)} custom-call(bf16[2,640,768]{2,1,0:T(8,128)(2,1)} %multiply_convert_fusion.1.table, bf16[16,6,96,128]{3,2,1,0:T(8,128)(2,1)S(1)} %all-to-all-done.x_ref), custom_call_target="tpu_custom_call" | custom-call | tf_op jit(solution)/shard_map/fourier_forward/pallas_call | solution.py:254
  48.5 6.2 %all-to-all-start.1 = ((bf16[128,30,2,128]{3,2,1,0:T(2,128)(2,1)}), bf16[128,30,2,128]{3,2,1,0:T(2,128)(2,1)S(1)}, u32[]{:S(2)}, u32[]{:S(2)}) async-start(bf16[128,30,2,128]{3,2,1,0:T(2,128)(2,1)} %bitcast.54), calls=%async_computation.1 | async-start | bytes 3932160 | tf_op jit(solution)/shard_map/all_to_all | solution.py:483
  54.7 4.0 %copy.7 = bf16[5,8,90,2,128]{4,3,0,1,2:T(2,128)(2,1)} copy(bf16[5,8,90,2,128]{4,3,2,1,0:T(2,128)(2,1)} %bitcast.59) | data formatting | bytes 3686400 | tf_op jit(solution)/shard_map/reshape | solution.py:502
  58.7 9.1 %copy.6 = bf16[5,768,768]{1,2,0:T(8,128)(2,1)} copy(bf16[5,768,768]{2,1,0:T(8,128)(2,1)} %copy-done) | data formatting | bytes 11796480 | tf_op jit(solution)/shard_map/optimization_barrier | solution.py:497
  67.7 14.4 %all-to-all-done.1 = bf16[128,30,2,128]{3,2,1,0:T(2,128)(2,1)S(1)} async-done(((bf16[128,30,2,128]{3,2,1,0:T(2,128)(2,1)}), bf16[128,30,2,128]{3,2,1,0:T(2,128)(2,1)S(1)}, u32[]{:S(2)}, u32[]{:S(2)}) %all-to-all-start.1) | async-done | bytes 1966112 | tf_op jit(solution)/shard_map/all_to_all | solution.py:483
  82.1 5.3 %analyse.1 = bf16[8,10,96,128]{3,2,1,0:T(8,128)(2,1)} custom-call(bf16[5,768,768]{2,1,0:T(8,128)(2,1)} %copy-done, bf16[7680,128]{1,0:T(8,128)(2,1)S(1)} %bitcast.45), custom_call_target="tpu_custom_call" | custom-call | tf_op jit(solution)/shard_map/analyse/pallas_call | solution.py:286
  87.4 3.6 %all-to-all-start.2 = ((bf16[8,10,96,128]{3,2,1,0:T(8,128)(2,1)}), bf16[8,10,96,128]{3,2,1,0:T(8,128)(2,1)S(1)}, u32[]{:S(2)}, u32[]{:S(2)}) async-start(bf16[8,10,96,128]{3,2,1,0:T(8,128)(2,1)} %analyse.1), calls=%async_computation.2 | async-start | bytes 3932160 | tf_op jit(solution)/shard_map/all_to_all | solution.py:483
  91.0 0.1 pad_add_fusion.place
  91.2 4.6 %multiply_convert_fusion = bf16[768,1280]{1,0:T(8,128)(2,1)} fusion(f32[768]{0:T(1024)S(1)} %fusion.69, f32[1280]{0:T(1024)S(1)} %fusion.25, f32[1280]{0:T(1024)S(1)} %fusion.20, f32[768]{0:T(1024)S(1)} %fusion.54), kind=kLoop, calls=%fused_computation | loop fusion | flops 24576000 | bytes 1982464 | tf_op jit(solution)/shard_map/convert_element_type | solution.py:114
  95.7 22.0 %all-to-all-done.2 = bf16[8,10,96,128]{3,2,1,0:T(8,128)(2,1)S(1)} async-done(((bf16[8,10,96,128]{3,2,1,0:T(8,128)(2,1)}), bf16[8,10,96,128]{3,2,1,0:T(8,128)(2,1)S(1)}, u32[]{:S(2)}, u32[]{:S(2)}) %all-to-all-start.2) | async-done | bytes 1966112 | tf_op jit(solution)/shard_map/all_to_all | solution.py:483
  117.7 6.4 %mix.1 = (bf16[90,80,128]{2,1,0:T(8,128)(2,1)}, bf16[7680,128]{1,0:T(8,128)(2,1)}) custom-call(bf16[7680,128]{1,0:T(8,128)(2,1)S(1)} %bitcast.47, bf16[5,18,128,128]{3,2,1,0:T(8,128)(2,1)} %bitcast.56), custom_call_target="tpu_custom_call" | custom-call | tf_op jit(solution)/shard_map/mix/pallas_call | solution.py:340
  124.1 5.9 %weigh.1 = (bf16[4,90,16,128]{3,2,1,0:T(8,128)(2,1)}, bf16[4,90,16,128]{3,2,1,0:T(8,128)(2,1)}) custom-call(s32[2]{0:T(128)S(1)} %pad_add_fusion.place, bf16[90,80,128]{2,1,0:T(8,128)(2,1)} %bitcast.55, bf16[90,80,128]{2,1,0:T(8,128)(2,1)} %get-tuple-element.28.gathered), custom_call_target="tpu_custom_call" | custom-call | tf_op jit(solution)/shard_map/weigh/pallas_call | solution.py:381
  130.0 0.0 collective-permute-start
  130.0 8.5 %all-to-all-start.3 = ((bf16[8,10,96,128]{3,2,1,0:T(8,128)(2,1)}), bf16[8,10,96,128]{3,2,1,0:T(8,128)(2,1)S(1)}, u32[]{:S(2)}, u32[]{:S(2)}) async-start(bf16[8,10,96,128]{3,2,1,0:T(8,128)(2,1)} %bitcast.58), calls=%async_computation.3 | async-start | bytes 3932160 | tf_op jit(solution)/shard_map/all_to_all | solution.py:483
  138.5 0.0 collective-permute-done
  138.5 0.0 copy-start.1
  138.5 1.2 copy-done.1
  139.8 3.0 %fusion.6 = (bf16[90,16,128]{2,1,0:T(8,128)(2,1)}, bf16[90,16,128]{2,1,0:T(8,128)(2,1)}, bf16[90,16,128]{2,1,0:T(8,128)(2,1)}, f32[90,16,128]{2,1,0:T(8,128)S(1)}) fusion(bf16[4,90,16,128]{3,2,1,0:T(8,128)(2,1)} %copy-done.1, bf16[4,90,16,128]{3,2,1,0:T(8,128)(2,1)} %get-tuple-element.29), kind=kLoop, calls=%fused_computation.20 | loop fusion | flops 2764800 | bytes 4792320 | tf_op jit(solution)/shard_map/convert_element_type | solution.py:517
  142.8 22.0 %all-to-all-done.3.x_ref = bf16[8,10,96,128]{3,2,1,0:T(8,128)(2,1)S(1)} async-done(((bf16[8,10,96,128]{3,2,1,0:T(8,128)(2,1)}), bf16[8,10,96,128]{3,2,1,0:T(8,128)(2,1)S(1)}, u32[]{:S(2)}, u32[]{:S(2)}) %all-to-all-start.3) | async-done | bytes 1966112 | tf_op jit(solution)/shard_map/all_to_all | solution.py:483
  164.7 6.4 %synthesise.1 = bf16[7680,128]{1,0:T(8,128)(2,1)} custom-call(bf16[5,768,768]{2,1,0:T(8,128)(2,1)} %bitcast.48, bf16[8,10,96,128]{3,2,1,0:T(8,128)(2,1)S(1)} %all-to-all-done.3.x_ref), custom_call_target="tpu_custom_call" | custom-call | tf_op jit(solution)/shard_map/synthesise/pallas_call | solution.py:418
  171.2 8.4 %all-to-all-start.4 = ((bf16[128,30,2,128]{3,2,1,0:T(2,128)(2,1)}), bf16[128,30,2,128]{3,2,1,0:T(2,128)(2,1)S(1)}, u32[]{:S(2)}, u32[]{:S(2)}) async-start(bf16[128,30,2,128]{3,2,1,0:T(2,128)(2,1)} %bitcast.52), calls=%async_computation.4 | async-start | bytes 3932160 | tf_op jit(solution)/shard_map/all_to_all | solution.py:483
  179.5 1.1 collective-permute-start.1
  180.7 2.2 collective-permute-start.2
  182.8 1.6 collective-permute-start.3
  184.5 27.8 %collective-permute-done.1 = bf16[90,16,128]{2,1,0:T(8,128)(2,1)S(1)} collective-permute-done((bf16[90,16,128]{2,1,0:T(8,128)(2,1)}, bf16[90,16,128]{2,1,0:T(8,128)(2,1)S(1)}, u32[]{:S(2)}, u32[]{:S(2)}) %collective-permute-start.1) | collective-permute-done | bytes 368672 | tf_op jit(solution)/shard_map/ppermute | solution.py:517
  212.3 0.0 collective-permute-done.2
  212.3 7.6 %collective-permute-done.3 = bf16[90,16,128]{2,1,0:T(8,128)(2,1)} collective-permute-done((bf16[90,16,128]{2,1,0:T(8,128)(2,1)}, bf16[90,16,128]{2,1,0:T(8,128)(2,1)}, u32[]{:S(2)}, u32[]{:S(2)}) %collective-permute-start.3) | collective-permute-done | bytes 368672 | tf_op jit(solution)/shard_map/ppermute | solution.py:517
  219.9 1.2 add_bitcast_fusion
  221.2 0.0 all-to-all-done.4
  221.2 4.5 %fourier_backward.1 = bf16[2,8,6,96,128]{4,3,2,1,0:T(8,128)(2,1)} custom-call(bf16[2,384,1280]{2,1,0:T(8,128)(2,1)} %bitcast.53, bf16[7680,128]{1,0:T(8,128)(2,1)S(1)} %bitcast.46), custom_call_target="tpu_custom_call" | custom-call | tf_op jit(solution)/shard_map/fourier_backward/pallas_call | solution.py:466
  225.7 4.7 %all-to-all-start.5 = ((bf16[16,6,96,128]{3,2,1,0:T(8,128)(2,1)}), bf16[16,6,96,128]{3,2,1,0:T(8,128)(2,1)S(1)}, u32[]{:S(2)}, u32[]{:S(2)}) async-start(bf16[16,6,96,128]{3,2,1,0:T(8,128)(2,1)} %bitcast.49), calls=%async_computation.5 | async-start | bytes 4718592 | tf_op jit(solution)/shard_map/all_to_all | solution.py:483
  230.4 3.4 %collective-permute-start.4 = (bf16[90,8,128]{2,1,0:T(8,128)(2,1)S(1)}, bf16[90,8,128]{2,1,0:T(8,128)(2,1)S(1)}, u32[]{:S(2)}, u32[]{:S(2)}) collective-permute-start(bf16[90,8,128]{2,1,0:T(8,128)(2,1)S(1)} %fusion.9), channel_id=1, source_target_pairs={{0,2},{1,3},{2,0},{3,1},{4,6},{5,7},{6,4},{7,5},{8,10},{9,11},{10,... | collective-permute-start | bytes 552968 | tf_op jit(solution)/shard_map/ppermute | solution.py:531
  233.8 31.0 %collective-permute-done.4 = bf16[90,8,128]{2,1,0:T(8,128)(2,1)S(1)} collective-permute-done((bf16[90,8,128]{2,1,0:T(8,128)(2,1)S(1)}, bf16[90,8,128]{2,1,0:T(8,128)(2,1)S(1)}, u32[]{:S(2)}, u32[]{:S(2)}) %collective-permute-start.4) | collective-permute-done | bytes 184352 | tf_op jit(solution)/shard_map/ppermute | solution.py:531
  264.8 0.8 convert_add_fusion
  265.6 0.0 all-to-all-done.5
  265.6 0.1 slice.44
  265.7 1.5 slice_bitcast_fusion
  (16 shorter events, 0.2 us)
Async XLA Ops:
  3.9 40.2 %all-to-all-start = ((bf16[16,6,96,128]{3,2,1,0:T(8,128)(2,1)}), bf16[16,6,96,128]{3,2,1,0:T(8,128)(2,1)S(1)}, u32[]{:S(2)}, u32[]{:S(2)}) async-start(bf16[16,6,96,128]{3,2,1,0:T(8,128)(2,1)} %bitcast.50), calls=%async_computation | async-start | bytes 4718592 | tf_op jit(solution)/shard_map/all_to_all | solution.py:483
  22.8 2.5 copy-start
  48.5 33.7 %all-to-all-start.1 = ((bf16[128,30,2,128]{3,2,1,0:T(2,128)(2,1)}), bf16[128,30,2,128]{3,2,1,0:T(2,128)(2,1)S(1)}, u32[]{:S(2)}, u32[]{:S(2)}) async-start(bf16[128,30,2,128]{3,2,1,0:T(2,128)(2,1)} %bitcast.54), calls=%async_computation.1 | async-start | bytes 3932160 | tf_op jit(solution)/shard_map/all_to_all | solution.py:483
  87.4 30.3 %all-to-all-start.2 = ((bf16[8,10,96,128]{3,2,1,0:T(8,128)(2,1)}), bf16[8,10,96,128]{3,2,1,0:T(8,128)(2,1)S(1)}, u32[]{:S(2)}, u32[]{:S(2)}) async-start(bf16[8,10,96,128]{3,2,1,0:T(8,128)(2,1)} %analyse.1), calls=%async_computation.2 | async-start | bytes 3932160 | tf_op jit(solution)/shard_map/all_to_all | solution.py:483
  130.0 8.5 %collective-permute-start = (bf16[4,90,16,128]{3,2,1,0:T(8,128)(2,1)}, bf16[4,90,16,128]{3,2,1,0:T(8,128)(2,1)S(1)}, u32[]{:S(2)}, u32[]{:S(2)}) collective-permute-start(bf16[4,90,16,128]{3,2,1,0:T(8,128)(2,1)} %get-tuple-element.30), channel_id=1, source_target_pairs={{0,1},{1,0},{2,3},{3,2},{4,5},{5,4},{6,7},{7,6},{8,9},{9,8},{10,11... | collective-permute-start | bytes 4423688 | tf_op jit(solution)/shard_map/ppermute | solution.py:512
  130.0 34.7 %all-to-all-start.3 = ((bf16[8,10,96,128]{3,2,1,0:T(8,128)(2,1)}), bf16[8,10,96,128]{3,2,1,0:T(8,128)(2,1)S(1)}, u32[]{:S(2)}, u32[]{:S(2)}) async-start(bf16[8,10,96,128]{3,2,1,0:T(8,128)(2,1)} %bitcast.58), calls=%async_computation.3 | async-start | bytes 3932160 | tf_op jit(solution)/shard_map/all_to_all | solution.py:483
  138.5 1.2 copy-start.1
  171.2 50.0 %all-to-all-start.4 = ((bf16[128,30,2,128]{3,2,1,0:T(2,128)(2,1)}), bf16[128,30,2,128]{3,2,1,0:T(2,128)(2,1)S(1)}, u32[]{:S(2)}, u32[]{:S(2)}) async-start(bf16[128,30,2,128]{3,2,1,0:T(2,128)(2,1)} %bitcast.52), calls=%async_computation.4 | async-start | bytes 3932160 | tf_op jit(solution)/shard_map/all_to_all | solution.py:483
  179.5 32.8 %collective-permute-start.1 = (bf16[90,16,128]{2,1,0:T(8,128)(2,1)}, bf16[90,16,128]{2,1,0:T(8,128)(2,1)S(1)}, u32[]{:S(2)}, u32[]{:S(2)}) collective-permute-start(bf16[90,16,128]{2,1,0:T(8,128)(2,1)} %get-tuple-element.38), channel_id=1, source_target_pairs={{0,4},{1,5},{2,6},{3,7},{4,8},{5,9},{6,10},{7,11},{8,12},{9,13},{1... | collective-permute-start | bytes 1105928 | tf_op jit(solution)/shard_map/ppermute | solution.py:517
  180.7 31.6 %collective-permute-start.2 = (bf16[90,16,128]{2,1,0:T(8,128)(2,1)}, bf16[90,16,128]{2,1,0:T(8,128)(2,1)S(1)}, u32[]{:S(2)}, u32[]{:S(2)}) collective-permute-start(bf16[90,16,128]{2,1,0:T(8,128)(2,1)} %get-tuple-element.40), channel_id=1, source_target_pairs={{0,12},{1,13},{2,14},{3,15},{4,0},{5,1},{6,2},{7,3},{8,4},{9,5},{1... | collective-permute-start | bytes 1105928 | tf_op jit(solution)/shard_map/ppermute | solution.py:517
  182.8 37.1 %collective-permute-start.3 = (bf16[90,16,128]{2,1,0:T(8,128)(2,1)}, bf16[90,16,128]{2,1,0:T(8,128)(2,1)}, u32[]{:S(2)}, u32[]{:S(2)}) collective-permute-start(bf16[90,16,128]{2,1,0:T(8,128)(2,1)} %get-tuple-element.39), channel_id=1, source_target_pairs={{0,8},{1,9},{2,10},{3,11},{4,12},{5,13},{6,14},{7,15},{8,0},{9,1},... | collective-permute-start | bytes 1105928 | tf_op jit(solution)/shard_map/ppermute | solution.py:517
  225.7 39.9 %all-to-all-start.5 = ((bf16[16,6,96,128]{3,2,1,0:T(8,128)(2,1)}), bf16[16,6,96,128]{3,2,1,0:T(8,128)(2,1)S(1)}, u32[]{:S(2)}, u32[]{:S(2)}) async-start(bf16[16,6,96,128]{3,2,1,0:T(8,128)(2,1)} %bitcast.49), calls=%async_computation.5 | async-start | bytes 4718592 | tf_op jit(solution)/shard_map/all_to_all | solution.py:483
  230.4 34.4 %collective-permute-start.4 = (bf16[90,8,128]{2,1,0:T(8,128)(2,1)S(1)}, bf16[90,8,128]{2,1,0:T(8,128)(2,1)S(1)}, u32[]{:S(2)}, u32[]{:S(2)}) collective-permute-start(bf16[90,8,128]{2,1,0:T(8,128)(2,1)S(1)} %fusion.9), channel_id=1, source_target_pairs={{0,2},{1,3},{2,0},{3,1},{4,6},{5,7},{6,4},{7,5},{8,10},{9,11},{10,... | collective-permute-start | bytes 552968 | tf_op jit(solution)/shard_map/ppermute | solution.py:531

commit v8 on v7

--- a/solution.py
+++ b/solution.py
@@ -28,7 +28,6 @@
 CHUNK = Q * SLOT
 DEGREES = L // LATS
 BLOCK = 16
-AHEAD = 2
 TAIL = 4
 SHIFT = 40
 
@@ -52,27 +51,23 @@
     return pl.BlockSpec(memory_space=space)
 
 
-def stream(table, held, ready, steps):
-    g = pl.program_id(0)
-
-    def copy(step):
-        return pltpu.make_async_copy(table.at[step], held.at[step], ready.at[step])
-
-    @pl.when(g == 0)
-    def _():
-        for step in range(min(AHEAD, steps)):
-            copy(step).start()
-
-    def arrive():
-        @pl.when(g < steps)
-        def _():
-            copy(jnp.minimum(g, steps - 1)).wait()
-
-        @pl.when(g + AHEAD < steps)
-        def _():
-            copy(jnp.minimum(g + AHEAD, steps - 1)).start()
-
-    return arrive
+def fetch(table, held, ready):
+    parts = range(held.shape[0])
+    copies = [pltpu.make_async_copy(table.at[k], held.at[k], ready.at[k]) for k in parts]
+    for copy in copies:
+        copy.start()
+    return copies
+
+
+def send(made, out, done):
+    copy = pltpu.make_async_copy(made, out, done)
+    copy.start()
+    return copy
+
+
+def finish(copies):
+    for copy in copies:
+        copy.wait()
 
 
 def streamed(table):
@@ -218,139 +213,136 @@
     )(up.reshape(-1), back.reshape(-1), start.reshape(-1), seed, order, x, root, log_sine)
 
 
-def forward_kernel(table, x_ref, out_ref, buf, held, ready):
-    g = pl.program_id(0)
-    arrive = stream(table, held, ready, 2)
-    arrive()
+def forward_kernel(table, x_ref, out_ref, buf, made, held, ready, done):
+    copies = fetch(table, held, ready)
     rows = LONS * Q
-
+    sent = []
     for parity in range(2):
-
-        @pl.when(g == parity)
-        def _():
-            for pair in range(SLOT // 2):
-                both = []
-                for half in range(2):
-                    low = x_ref[:HALF, 2 * pair + half]
-                    high = x_ref[HALF:, 2 * pair + half]
-                    both.append((low - high if parity else low + high).reshape(HALF * PAD, C))
-                done = jnp.dot(
-                    held[parity], jnp.concatenate(both, axis=1), preferred_element_type=F32
-                )
-                for half in range(2):
-                    for lat in range(LATS // 2):
-                        first = lat * rows * SLOT + 2 * pair + half
-                        buf[pl.ds(first, rows, stride=SLOT), :] = done[
-                            lat * rows : lat * rows + rows, half * C : half * C + C
-                        ]
-
-    for lat in range(LATS // 2):
-        first = lat * rows * SLOT
-        out_ref[lat, 0] = buf[first : first + rows * SLOT, :].astype(BF16)
+        copies[parity].wait()
+        for pair in range(SLOT // 2):
+            both = []
+            for half in range(2):
+                low = x_ref[:HALF, 2 * pair + half]
+                high = x_ref[HALF:, 2 * pair + half]
+                both.append((low - high if parity else low + high).reshape(HALF * PAD, C))
+            part = jnp.dot(held[parity], jnp.concatenate(both, axis=1), preferred_element_type=F32)
+            for half in range(2):
+                for lat in range(LATS // 2):
+                    first = lat * rows * SLOT + 2 * pair + half
+                    buf[parity, pl.ds(first, rows, stride=SLOT), :] = part[
+                        lat * rows : lat * rows + rows, half * C : half * C + C
+                    ]
+        for lat in range(LATS // 2):
+            first = lat * rows * SLOT
+            made[parity, lat] = buf[parity, first : first + rows * SLOT, :].astype(BF16)
+        sent.append(send(made.at[parity], out_ref.at[:, parity], done.at[parity]))
+    finish(sent)
 
 
 def fourier_forward(table, x):
     shape = (LATS // 2, 2, LONS * CHUNK, C)
     return pl.pallas_call(
         forward_kernel,
-        grid=(2,),
         out_shape=pltpu.HBM(shape, BF16),
         in_specs=[whole(pltpu.HBM), whole()],
-        out_specs=pl.BlockSpec((shape[0], 1) + shape[2:], lambda g: (0, g, 0, 0)),
-        scratch_shapes=[pltpu.VMEM((M * SLOT, C), F32)] + streamed(table),
-        compiler_params=limit(24),
+        out_specs=whole(pltpu.HBM),
+        scratch_shapes=[
+            pltpu.VMEM((2, M * SLOT, C), F32),
+            pltpu.VMEM((2, shape[0]) + shape[2:], BF16),
+        ]
+        + streamed(table)
+        + [pltpu.SemaphoreType.DMA((2,))],
+        compiler_params=limit(26),
         name="fourier_forward",
     )(far(table), near(x))
 
 
-def analyse_kernel(table, x_ref, out_ref, wide, held, ready):
-    g = pl.program_id(0)
-    arrive = stream(table, held, ready, ORDERS)
-
-    @pl.when(g == 0)
-    def _():
-        wide[...] = x_ref[...].astype(F32)
+def analyse_kernel(table, x_ref, out_ref, wide, made, held, ready, done):
+    copies = fetch(table, held, ready)
+    wide[...] = x_ref[...].astype(F32)
 
     def column(q):
         parts = [wide[pl.ds(q * SLOT + tt, DEVICES, stride=CHUNK), :] for tt in range(SLOT)]
         return jnp.concatenate(parts, axis=0).astype(BF16)
 
-    right = jnp.concatenate([column(2 * g), column(2 * g + 1)], axis=1)
-    arrive()
-    done = jnp.dot(held[g], right, preferred_element_type=F32).astype(BF16)
-    for half in range(2):
-        out_ref[:, half] = done[:, half * C : half * C + C].reshape(LATS, PAD, C)
+    sent = []
+    for k in range(ORDERS):
+        right = jnp.concatenate([column(2 * k), column(2 * k + 1)], axis=1)
+        copies[k].wait()
+        part = jnp.dot(held[k], right, preferred_element_type=F32).astype(BF16)
+        for half in range(2):
+            made[k, :, half] = part[:, half * C : half * C + C].reshape(LATS, PAD, C)
+        sent.append(send(made.at[k], out_ref.at[:, pl.ds(2 * k, 2)], done.at[k]))
+    finish(sent)
 
 
 def analyse(table, x):
     return pl.pallas_call(
         analyse_kernel,
-        grid=(ORDERS,),
         out_shape=pltpu.HBM((LATS, Q, PAD, C), BF16),
         in_specs=[whole(pltpu.HBM), whole()],
-        out_specs=pl.BlockSpec((LATS, 2, PAD, C), lambda g: (0, g, 0, 0)),
-        scratch_shapes=[pltpu.VMEM((DEVICES * CHUNK, C), F32)] + streamed(table),
-        compiler_params=limit(26),
+        out_specs=whole(pltpu.HBM),
+        scratch_shapes=[
+            pltpu.VMEM((DEVICES * CHUNK, C), F32),
+            pltpu.VMEM((ORDERS, LATS, 2, PAD, C), BF16),
+        ]
+        + streamed(table)
+        + [pltpu.SemaphoreType.DMA((ORDERS,))],
+        compiler_params=limit(28),
         name="analyse",
     )(far(table), near(x))
 
 
-def mix_kernel(x_ref, weights, gathered, out_ref, wide, made, held, ready):
-    g = pl.program_id(0)
+def mix_kernel(x_ref, weights, gathered, out_ref, wide, mixed, rows, made, held, ready, done):
+    copies = fetch(weights, held, ready)
     steps, each = held.shape[:2]
     slabs = LATS * Q
-    arrive = stream(weights, held, ready, steps)
-
-    @pl.when(g == 0)
-    def _():
-        for slab in range(slabs):
-            wide[slab * ODD : slab * ODD + PAD, :] = x_ref[
-                slab * PAD : slab * PAD + PAD, :
-            ].astype(F32)
-            made[slab * ODD + PAD - 8 : slab * ODD + PAD, :] = jnp.zeros((8, C), F32)
-
-    arrive()
-
-    @pl.when(g < steps)
-    def _():
+    for slab in range(slabs):
+        wide[slab * ODD : slab * ODD + PAD, :] = x_ref[slab * PAD : slab * PAD + PAD, :].astype(
+            F32
+        )
+        mixed[slab * ODD + PAD - 8 : slab * ODD + PAD, :] = jnp.zeros((8, C), F32)
+    sent = []
+    for step in range(steps):
+        copies[step].wait()
         for offset in range(each):
-            rows = pl.ds(g * each + offset, slabs, stride=ODD)
-            part = wide[rows, :].astype(BF16)
-            gathered[offset] = part
-            made[rows, :] = lax.dot_general(
-                part, held[g, offset], (((1,), (1,)), ((), ())), preferred_element_type=F32
+            degree = step * each + offset
+            across = pl.ds(degree, slabs, stride=ODD)
+            part = wide[across, :].astype(BF16)
+            rows[degree] = part
+            mixed[across, :] = lax.dot_general(
+                part, held[step, offset], (((1,), (1,)), ((), ())), preferred_element_type=F32
             )
-
+        block = pl.ds(step * each, each)
+        sent.append(send(rows.at[block], gathered.at[block], done.at[step]))
     for step in range(TAIL):
-
-        @pl.when(g == steps + step)
-        def _():
-            for slab in range(slabs // TAIL):
-                first = (step * (slabs // TAIL) + slab) * ODD
-                out_ref[slab * PAD : slab * PAD + PAD, :] = made[first : first + PAD, :].astype(
-                    BF16
-                )
+        first = step * (slabs // TAIL)
+        for slab in range(first, first + slabs // TAIL):
+            made[slab * PAD : slab * PAD + PAD, :] = mixed[
+                slab * ODD : slab * ODD + PAD, :
+            ].astype(BF16)
+        block = pl.ds(first * PAD, slabs // TAIL * PAD)
+        sent.append(send(made.at[block], out_ref.at[block], done.at[steps + step]))
+    finish(sent)
 
 
 def mix(x, weights):
     steps = 5
-    each = DEGREES // steps
     size = LATS * Q * PAD
-    weights = weights.reshape(steps, each, C, C)
+    weights = weights.reshape(steps, DEGREES // steps, C, C)
     return pl.pallas_call(
         mix_kernel,
-        grid=(steps + TAIL,),
         out_shape=(
             pltpu.HBM((DEGREES, LATS * Q, C), BF16),
             pltpu.HBM((size, C), BF16),
         ),
         in_specs=[whole(), whole(pltpu.HBM)],
-        out_specs=(
-            pl.BlockSpec((each, LATS * Q, C), lambda g: (jnp.minimum(g, steps - 1), 0, 0)),
-            pl.BlockSpec((size // TAIL, C), lambda g: (jnp.maximum(g - steps, 0), 0)),
-        ),
-        scratch_shapes=[pltpu.VMEM((LATS * Q * ODD, C), F32)] * 2 + streamed(weights),
-        compiler_params=limit(26),
+        out_specs=(whole(pltpu.HBM), whole(pltpu.HBM)),
+        scratch_shapes=[pltpu.VMEM((LATS * Q * ODD, C), F32)] * 2
+        + [pltpu.VMEM((DEGREES, LATS * Q, C), BF16), pltpu.VMEM((size, C), BF16)]
+        + streamed(weights)
+        + [pltpu.SemaphoreType.DMA((steps + TAIL,))],
+        compiler_params=limit(28),
         name="mix",
     )(near(x), far(weights))
 
@@ -389,74 +381,74 @@
     )(jnp.stack([lon & 1, lon >> 2]), far(stored), far(gathered))
 
 
-def synthesise_kernel(table, x_ref, out_ref, made, held, ready):
-    g = pl.program_id(0)
-    arrive = stream(table, held, ready, ORDERS)
-    arrive()
-
-    @pl.when(g < ORDERS)
-    def _():
+def synthesise_kernel(table, x_ref, out_ref, mixed, made, held, ready, done):
+    copies = fetch(table, held, ready)
+    for k in range(ORDERS):
         right = jnp.concatenate(
-            [x_ref[:, 2 * g + half].reshape(LATS * PAD, C) for half in range(2)], axis=1
+            [x_ref[:, 2 * k + half].reshape(LATS * PAD, C) for half in range(2)], axis=1
         )
-        done = jnp.dot(held[g], right, preferred_element_type=F32)
+        copies[k].wait()
+        part = jnp.dot(held[k], right, preferred_element_type=F32)
         for half in range(2):
             for tt in range(SLOT):
-                made[pl.ds((2 * g + half) * SLOT + tt, DEVICES, stride=CHUNK), :] = done[
+                mixed[pl.ds((2 * k + half) * SLOT + tt, DEVICES, stride=CHUNK), :] = part[
                     tt * DEVICES : tt * DEVICES + DEVICES, half * C : half * C + C
                 ]
-
-    rows = out_ref.shape[0]
+    sent = []
+    rows = DEVICES * CHUNK // TAIL
     for step in range(TAIL):
-
-        @pl.when(g == ORDERS + step)
-        def _():
-            out_ref[...] = made[step * rows : step * rows + rows, :].astype(BF16)
+        block = pl.ds(step * rows, rows)
+        made[block, :] = mixed[block, :].astype(BF16)
+        sent.append(send(made.at[block], out_ref.at[block], done.at[step]))
+    finish(sent)
 
 
 def synthesise(table, x):
     return pl.pallas_call(
         synthesise_kernel,
-        grid=(ORDERS + TAIL,),
         out_shape=pltpu.HBM((DEVICES * CHUNK, C), BF16),
         in_specs=[whole(pltpu.HBM), whole()],
-        out_specs=pl.BlockSpec(
-            (DEVICES * CHUNK // TAIL, C), lambda g: (jnp.maximum(g - ORDERS, 0), 0)
-        ),
-        scratch_shapes=[pltpu.VMEM((DEVICES * CHUNK, C), F32)] + streamed(table),
-        compiler_params=limit(26),
+        out_specs=whole(pltpu.HBM),
+        scratch_shapes=[
+            pltpu.VMEM((DEVICES * CHUNK, C), F32),
+            pltpu.VMEM((DEVICES * CHUNK, C), BF16),
+        ]
+        + streamed(table)
+        + [pltpu.SemaphoreType.DMA((TAIL,))],
+        compiler_params=limit(28),
         name="synthesise",
     )(far(table), near(x))
 
 
-def backward_kernel(table, x_ref, out_ref, wide, right, held, ready):
-    g = pl.program_id(0)
-    arrive = stream(table, held, ready, held.shape[0])
+def backward_kernel(table, x_ref, out_ref, wide, right, made, held, ready, done):
+    copies = fetch(table, held, ready)
     rows = LONS * Q
-
-    @pl.when(g == 0)
-    def _():
-        wide[...] = x_ref[...].astype(F32)
-        for tt in range(SLOT):
-            part = wide[pl.ds(tt, 2 * M, stride=SLOT), :].astype(BF16)
-            for lat in range(LATS):
-                first = lat // 2 * rows
-                right[lat % 2, first : first + rows, tt * C : tt * C + C] = part[
-                    lat * rows : lat * rows + rows
-                ]
-
-    arrive()
-    for pair in range(SLOT // 2):
-        lanes = slice(2 * pair * C, 2 * pair * C + 2 * C)
-        even = jnp.dot(held[g, :, :M], right[0, :, lanes], preferred_element_type=F32)
-        odd = jnp.dot(held[g, :, M:], right[1, :, lanes], preferred_element_type=F32)
-        for side, done in enumerate((even + odd, even - odd)):
-            done = done.astype(BF16)
-            for half in range(2):
-                for j in range(out_ref.shape[1]):
-                    out_ref[side, j, 2 * pair + half] = done[
-                        j * PAD : j * PAD + PAD, half * C : half * C + C
-                    ]
+    wide[...] = x_ref[...].astype(F32)
+    for tt in range(SLOT):
+        part = wide[pl.ds(tt, 2 * M, stride=SLOT), :].astype(BF16)
+        for lat in range(LATS):
+            first = lat // 2 * rows
+            right[lat % 2, first : first + rows, tt * C : tt * C + C] = part[
+                lat * rows : lat * rows + rows
+            ]
+    sent = []
+    each = made.shape[2]
+    for step in range(held.shape[0]):
+        copies[step].wait()
+        for pair in range(SLOT // 2):
+            lanes = slice(2 * pair * C, 2 * pair * C + 2 * C)
+            even = jnp.dot(held[step, :, :M], right[0, :, lanes], preferred_element_type=F32)
+            odd = jnp.dot(held[step, :, M:], right[1, :, lanes], preferred_element_type=F32)
+            for side, whole_part in enumerate((even + odd, even - odd)):
+                whole_part = whole_part.astype(BF16)
+                for half in range(2):
+                    for j in range(each):
+                        made[step, side, j, 2 * pair + half] = whole_part[
+                            j * PAD : j * PAD + PAD, half * C : half * C + C
+                        ]
+        block = pl.ds(step * each, each)
+        sent.append(send(made.at[step], out_ref.at[:, block], done.at[step]))
+    finish(sent)
 
 
 def fourier_backward(table, x):
@@ -465,16 +457,17 @@
     table = table.reshape(steps, each * PAD, 2 * M)
     return pl.pallas_call(
         backward_kernel,
-        grid=(steps,),
         out_shape=pltpu.HBM((2, HALF, SLOT, PAD, C), BF16),
         in_specs=[whole(pltpu.HBM), whole()],
-        out_specs=pl.BlockSpec((2, each, SLOT, PAD, C), lambda g: (0, g, 0, 0, 0)),
+        out_specs=whole(pltpu.HBM),
         scratch_shapes=[
             pltpu.VMEM((DEVICES * CHUNK, C), F32),
             pltpu.VMEM((2, M, SLOT * C), BF16),
+            pltpu.VMEM((steps, 2, each, SLOT, PAD, C), BF16),
         ]
-        + streamed(table),
-        compiler_params=limit(26),
+        + streamed(table)
+        + [pltpu.SemaphoreType.DMA((steps,))],
+        compiler_params=limit(28),
         name="fourier_backward",
     )(far(table), near(x))
 

time: 269 us -> 268 us (level)
  no operation moved by 1% of the time
where the time goes in v8:
time: 268 us; the launch traced here: 267 us
  waiting for transfers between devices  139 us (52%)
  starting transfers between devices  48.1 us (18%)
  Pallas kernels  41.2 us (15%)
  local copies, waits for them, and re-layouts  23 us (9%)
  other arithmetic  14.4 us (5%)
    all_to_all x6, waiting for transfers between devices, exchange(): return lax.all_to_all(x, axis, split_axis=0, concat_axis=0, tiled=True)  72.5 us
    all_to_all x6, starting transfers between devices, exchange(): return lax.all_to_all(x, axis, split_axis=0, concat_axis=0, tiled=True)  39.7 us
    ppermute x3, waiting for transfers between devices, on_device(): got.append(lax.ppermute(sums[step].astype(BF16), 'lon', pairs))  35.4 us
    ppermute x1, waiting for transfers between devices, on_device(): got = lax.ppermute(give, 'lon', [(k, k ^ 2) for k in range(LONS)])  31 us
    pallas_call x1, Pallas kernels, legendre_table(): pl.pallas_call(legendre_kernel, out_shape=jax.ShapeDtypeStruct((ORDERS, L...  9.14 us
    optimization_barrier x1, local copies, waits for them, and re-layouts, on_device(): lax.optimization_barrier((rows, forward, legendre))  9.07 us
    pallas_call x1, Pallas kernels, synthesise(): pl.pallas_call(synthesise_kernel, out_shape=pltpu.HBM((DEVICES * CHUNK, C...  6.16 us
    pallas_call x1, Pallas kernels, weigh(): pl.pallas_call(weigh_kernel, grid=(steps,), out_shape=(pltpu.HBM(shape, B...  5.91 us
  transfers between devices with their start and end apart: 11, of which 7 were waited for; matrix products, arithmetic and copies ran while one was open for 11% of the time, Pallas kernels for 3%

profile of v8, /device:TPU:0, one launch (start us, length us, event | category | flops | bytes accessed | tf_op | source)
XLA Modules:
  0.0 266.5 jit_solution(16804188929138050382)
XLA Ops:
  0.6 3.3 %pad.4 = bf16[96,96,128]{2,1,0:T(8,128)(2,1)} pad(bf16[90,90,128]{2,1,0:T(8,128)(2,1)} %bitcast.57, bf16[]{:T(256)} %constant.277.clone.1), padding=0_6x0_6x0_0 | pad | bytes 4432898 | tf_op jit(solution)/shard_map/jit(_pad)/pad | solution.py:486
  3.9 8.2 %all-to-all-start = ((bf16[16,6,96,128]{3,2,1,0:T(8,128)(2,1)}), bf16[16,6,96,128]{3,2,1,0:T(8,128)(2,1)S(1)}, u32[]{:S(2)}, u32[]{:S(2)}) async-start(bf16[16,6,96,128]{3,2,1,0:T(8,128)(2,1)} %bitcast.50), calls=%async_computation | async-start | bytes 4718592 | tf_op jit(solution)/shard_map/all_to_all | solution.py:476
  12.1 0.1 subtract_multiply_fusion
  12.2 0.1 mul.419
  12.3 0.1 sub.152
  12.3 0.1 fusion.10
  12.4 0.1 gt.23
  12.6 0.1 div.175
  12.6 0.1 mul.421
  12.7 0.1 reshape.688.start
  12.8 0.7 fusion.76.seed
  13.5 0.1 fusion.75.sine_ref
  13.6 0.1 sqrt_select_fusion.2
  13.7 9.1 %legendre.1.table = bf16[5,768,768]{2,1,0:T(8,128)(2,1)S(1)} custom-call(f32[3600]{0:T(1024)S(1)} %get-tuple-element.43.up, f32[3600]{0:T(1024)S(1)} %get-tuple-element.42.back, f32[3600]{0:T(1024)S(1)} %reshape.688.start, f32[5]{0:T(128)S(1)} %fusion.76.seed, f32[5]{0:T(128)S(1)} %get-tuple-element.36.order, f32[8,128]{1,0:T(8,128)S(1)} %get-tuple-element.51.x_ref, ...), custom_call_target="tpu_custom_call" | custom-call | tf_op jit(solution)/shard_map/legendre/pallas_call | solution.py:205
  22.8 0.0 copy-start
  22.8 2.5 copy-done
  25.4 0.1 fusion.48
  25.5 4.3 %multiply_convert_fusion.1.table = bf16[2,640,768]{2,1,0:T(8,128)(2,1)} fusion(f32[768]{0:T(1024)S(1)} %fusion.69, f32[2,640]{1,0:T(2,128)S(1)} %fusion.46, f32[2,640]{1,0:T(2,128)S(1)} %fusion.48, f32[768]{0:T(1024)S(1)} %fusion.54), kind=kLoop, calls=%fused_computation.7 | loop fusion | flops 24576000 | bytes 1982464 | tf_op jit(solution)/shard_map/convert_element_type | solution.py:106
  29.8 14.3 %all-to-all-done.x_ref = bf16[16,6,96,128]{3,2,1,0:T(8,128)(2,1)S(1)} async-done(((bf16[16,6,96,128]{3,2,1,0:T(8,128)(2,1)}), bf16[16,6,96,128]{3,2,1,0:T(8,128)(2,1)S(1)}, u32[]{:S(2)}, u32[]{:S(2)}) %all-to-all-start) | async-done | bytes 2359328 | tf_op jit(solution)/shard_map/all_to_all | solution.py:476
  44.1 4.7 %fourier_forward.1 = bf16[4,2,960,128]{3,2,1,0:T(8,128)(2,1)} custom-call(bf16[2,640,768]{2,1,0:T(8,128)(2,1)} %multiply_convert_fusion.1.table, bf16[16,6,96,128]{3,2,1,0:T(8,128)(2,1)S(1)} %all-to-all-done.x_ref), custom_call_target="tpu_custom_call" | custom-call | tf_op jit(solution)/shard_map/fourier_forward/pallas_call | solution.py:244
  48.8 6.2 %all-to-all-start.1 = ((bf16[128,30,2,128]{3,2,1,0:T(2,128)(2,1)}), bf16[128,30,2,128]{3,2,1,0:T(2,128)(2,1)S(1)}, u32[]{:S(2)}, u32[]{:S(2)}) async-start(bf16[128,30,2,128]{3,2,1,0:T(2,128)(2,1)} %bitcast.54), calls=%async_computation.1 | async-start | bytes 3932160 | tf_op jit(solution)/shard_map/all_to_all | solution.py:476
  55.1 4.0 %copy.7 = bf16[5,8,90,2,128]{4,3,0,1,2:T(2,128)(2,1)} copy(bf16[5,8,90,2,128]{4,3,2,1,0:T(2,128)(2,1)} %bitcast.59) | data formatting | bytes 3686400 | tf_op jit(solution)/shard_map/reshape | solution.py:495
  59.1 9.1 %copy.6 = bf16[5,768,768]{1,2,0:T(8,128)(2,1)} copy(bf16[5,768,768]{2,1,0:T(8,128)(2,1)} %copy-done) | data formatting | bytes 11796480 | tf_op jit(solution)/shard_map/optimization_barrier | solution.py:490
  68.1 14.4 %all-to-all-done.1 = bf16[128,30,2,128]{3,2,1,0:T(2,128)(2,1)S(1)} async-done(((bf16[128,30,2,128]{3,2,1,0:T(2,128)(2,1)}), bf16[128,30,2,128]{3,2,1,0:T(2,128)(2,1)S(1)}, u32[]{:S(2)}, u32[]{:S(2)}) %all-to-all-start.1) | async-done | bytes 1966112 | tf_op jit(solution)/shard_map/all_to_all | solution.py:476
  82.5 5.7 %analyse.1 = bf16[8,10,96,128]{3,2,1,0:T(8,128)(2,1)} custom-call(bf16[5,768,768]{2,1,0:T(8,128)(2,1)} %copy-done, bf16[7680,128]{1,0:T(8,128)(2,1)S(1)} %bitcast.45), custom_call_target="tpu_custom_call" | custom-call | tf_op jit(solution)/shard_map/analyse/pallas_call | solution.py:280
  88.2 3.8 %all-to-all-start.2 = ((bf16[8,10,96,128]{3,2,1,0:T(8,128)(2,1)}), bf16[8,10,96,128]{3,2,1,0:T(8,128)(2,1)S(1)}, u32[]{:S(2)}, u32[]{:S(2)}) async-start(bf16[8,10,96,128]{3,2,1,0:T(8,128)(2,1)} %analyse.1), calls=%async_computation.2 | async-start | bytes 3932160 | tf_op jit(solution)/shard_map/all_to_all | solution.py:476
  92.0 0.1 pad_add_fusion.place
  92.2 4.6 %multiply_convert_fusion = bf16[768,1280]{1,0:T(8,128)(2,1)} fusion(f32[768]{0:T(1024)S(1)} %fusion.69, f32[1280]{0:T(1024)S(1)} %fusion.25, f32[1280]{0:T(1024)S(1)} %fusion.20, f32[768]{0:T(1024)S(1)} %fusion.54), kind=kLoop, calls=%fused_computation | loop fusion | flops 24576000 | bytes 1982464 | tf_op jit(solution)/shard_map/convert_element_type | solution.py:109
  96.7 21.8 %all-to-all-done.2 = bf16[8,10,96,128]{3,2,1,0:T(8,128)(2,1)S(1)} async-done(((bf16[8,10,96,128]{3,2,1,0:T(8,128)(2,1)}), bf16[8,10,96,128]{3,2,1,0:T(8,128)(2,1)S(1)}, u32[]{:S(2)}, u32[]{:S(2)}) %all-to-all-start.2) | async-done | bytes 1966112 | tf_op jit(solution)/shard_map/all_to_all | solution.py:476
  118.5 5.2 %mix.1 = (bf16[90,80,128]{2,1,0:T(8,128)(2,1)}, bf16[7680,128]{1,0:T(8,128)(2,1)}) custom-call(bf16[7680,128]{1,0:T(8,128)(2,1)S(1)} %bitcast.47, bf16[5,18,128,128]{3,2,1,0:T(8,128)(2,1)} %bitcast.56), custom_call_target="tpu_custom_call" | custom-call | tf_op jit(solution)/shard_map/mix/pallas_call | solution.py:333
  123.7 5.9 %weigh.1 = (bf16[4,90,16,128]{3,2,1,0:T(8,128)(2,1)}, bf16[4,90,16,128]{3,2,1,0:T(8,128)(2,1)}) custom-call(s32[2]{0:T(128)S(1)} %pad_add_fusion.place, bf16[90,80,128]{2,1,0:T(8,128)(2,1)} %bitcast.55, bf16[90,80,128]{2,1,0:T(8,128)(2,1)} %get-tuple-element.28.gathered), custom_call_target="tpu_custom_call" | custom-call | tf_op jit(solution)/shard_map/weigh/pallas_call | solution.py:373
  129.6 0.0 collective-permute-start
  129.6 8.5 %all-to-all-start.3 = ((bf16[8,10,96,128]{3,2,1,0:T(8,128)(2,1)}), bf16[8,10,96,128]{3,2,1,0:T(8,128)(2,1)S(1)}, u32[]{:S(2)}, u32[]{:S(2)}) async-start(bf16[8,10,96,128]{3,2,1,0:T(8,128)(2,1)} %bitcast.58), calls=%async_computation.3 | async-start | bytes 3932160 | tf_op jit(solution)/shard_map/all_to_all | solution.py:476
  138.1 0.0 collective-permute-done
  138.1 0.0 copy-start.1
  138.2 1.2 copy-done.1
  139.4 3.0 %fusion.6 = (bf16[90,16,128]{2,1,0:T(8,128)(2,1)}, bf16[90,16,128]{2,1,0:T(8,128)(2,1)}, bf16[90,16,128]{2,1,0:T(8,128)(2,1)}, f32[90,16,128]{2,1,0:T(8,128)S(1)}) fusion(bf16[4,90,16,128]{3,2,1,0:T(8,128)(2,1)} %copy-done.1, bf16[4,90,16,128]{3,2,1,0:T(8,128)(2,1)} %get-tuple-element.29), kind=kLoop, calls=%fused_computation.20 | loop fusion | flops 2764800 | bytes 4792320 | tf_op jit(solution)/shard_map/convert_element_type | solution.py:510
  142.4 22.0 %all-to-all-done.3.x_ref = bf16[8,10,96,128]{3,2,1,0:T(8,128)(2,1)S(1)} async-done(((bf16[8,10,96,128]{3,2,1,0:T(8,128)(2,1)}), bf16[8,10,96,128]{3,2,1,0:T(8,128)(2,1)S(1)}, u32[]{:S(2)}, u32[]{:S(2)}) %all-to-all-start.3) | async-done | bytes 1966112 | tf_op jit(solution)/shard_map/all_to_all | solution.py:476
  164.3 6.2 %synthesise.1 = bf16[7680,128]{1,0:T(8,128)(2,1)} custom-call(bf16[5,768,768]{2,1,0:T(8,128)(2,1)} %bitcast.48, bf16[8,10,96,128]{3,2,1,0:T(8,128)(2,1)S(1)} %all-to-all-done.3.x_ref), custom_call_target="tpu_custom_call" | custom-call | tf_op jit(solution)/shard_map/synthesise/pallas_call | solution.py:407
  170.5 8.4 %all-to-all-start.4 = ((bf16[128,30,2,128]{3,2,1,0:T(2,128)(2,1)}), bf16[128,30,2,128]{3,2,1,0:T(2,128)(2,1)S(1)}, u32[]{:S(2)}, u32[]{:S(2)}) async-start(bf16[128,30,2,128]{3,2,1,0:T(2,128)(2,1)} %bitcast.52), calls=%async_computation.4 | async-start | bytes 3932160 | tf_op jit(solution)/shard_map/all_to_all | solution.py:476
  178.9 1.1 collective-permute-start.1
  180.0 2.2 collective-permute-start.2
  182.2 1.6 collective-permute-start.3
  183.8 27.8 %collective-permute-done.1 = bf16[90,16,128]{2,1,0:T(8,128)(2,1)S(1)} collective-permute-done((bf16[90,16,128]{2,1,0:T(8,128)(2,1)}, bf16[90,16,128]{2,1,0:T(8,128)(2,1)S(1)}, u32[]{:S(2)}, u32[]{:S(2)}) %collective-permute-start.1) | collective-permute-done | bytes 368672 | tf_op jit(solution)/shard_map/ppermute | solution.py:510
  211.6 0.0 collective-permute-done.2
  211.6 7.6 %collective-permute-done.3 = bf16[90,16,128]{2,1,0:T(8,128)(2,1)} collective-permute-done((bf16[90,16,128]{2,1,0:T(8,128)(2,1)}, bf16[90,16,128]{2,1,0:T(8,128)(2,1)}, u32[]{:S(2)}, u32[]{:S(2)}) %collective-permute-start.3) | collective-permute-done | bytes 368672 | tf_op jit(solution)/shard_map/ppermute | solution.py:510
  219.3 1.2 add_bitcast_fusion
  220.5 0.0 all-to-all-done.4
  220.5 4.4 %fourier_backward.1 = bf16[2,8,6,96,128]{4,3,2,1,0:T(8,128)(2,1)} custom-call(bf16[2,384,1280]{2,1,0:T(8,128)(2,1)} %bitcast.53, bf16[7680,128]{1,0:T(8,128)(2,1)S(1)} %bitcast.46), custom_call_target="tpu_custom_call" | custom-call | tf_op jit(solution)/shard_map/fourier_backward/pallas_call | solution.py:458
  225.0 4.7 %all-to-all-start.5 = ((bf16[16,6,96,128]{3,2,1,0:T(8,128)(2,1)}), bf16[16,6,96,128]{3,2,1,0:T(8,128)(2,1)S(1)}, u32[]{:S(2)}, u32[]{:S(2)}) async-start(bf16[16,6,96,128]{3,2,1,0:T(8,128)(2,1)} %bitcast.49), calls=%async_computation.5 | async-start | bytes 4718592 | tf_op jit(solution)/shard_map/all_to_all | solution.py:476
  229.7 3.4 %collective-permute-start.4 = (bf16[90,8,128]{2,1,0:T(8,128)(2,1)S(1)}, bf16[90,8,128]{2,1,0:T(8,128)(2,1)S(1)}, u32[]{:S(2)}, u32[]{:S(2)}) collective-permute-start(bf16[90,8,128]{2,1,0:T(8,128)(2,1)S(1)} %fusion.9), channel_id=1, source_target_pairs={{0,2},{1,3},{2,0},{3,1},{4,6},{5,7},{6,4},{7,5},{8,10},{9,11},{10,... | collective-permute-start | bytes 552968 | tf_op jit(solution)/shard_map/ppermute | solution.py:524
  233.1 31.0 %collective-permute-done.4 = bf16[90,8,128]{2,1,0:T(8,128)(2,1)S(1)} collective-permute-done((bf16[90,8,128]{2,1,0:T(8,128)(2,1)S(1)}, bf16[90,8,128]{2,1,0:T(8,128)(2,1)S(1)}, u32[]{:S(2)}, u32[]{:S(2)}) %collective-permute-start.4) | collective-permute-done | bytes 184352 | tf_op jit(solution)/shard_map/ppermute | solution.py:524
  264.1 0.8 convert_add_fusion
  264.9 0.0 all-to-all-done.5
  264.9 0.1 slice.44
  265.0 1.5 slice_bitcast_fusion
  (16 shorter events, 0.2 us)
Async XLA Ops:
  3.9 40.2 %all-to-all-start = ((bf16[16,6,96,128]{3,2,1,0:T(8,128)(2,1)}), bf16[16,6,96,128]{3,2,1,0:T(8,128)(2,1)S(1)}, u32[]{:S(2)}, u32[]{:S(2)}) async-start(bf16[16,6,96,128]{3,2,1,0:T(8,128)(2,1)} %bitcast.50), calls=%async_computation | async-start | bytes 4718592 | tf_op jit(solution)/shard_map/all_to_all | solution.py:476
  22.8 2.5 copy-start
  48.8 33.7 %all-to-all-start.1 = ((bf16[128,30,2,128]{3,2,1,0:T(2,128)(2,1)}), bf16[128,30,2,128]{3,2,1,0:T(2,128)(2,1)S(1)}, u32[]{:S(2)}, u32[]{:S(2)}) async-start(bf16[128,30,2,128]{3,2,1,0:T(2,128)(2,1)} %bitcast.54), calls=%async_computation.1 | async-start | bytes 3932160 | tf_op jit(solution)/shard_map/all_to_all | solution.py:476
  88.2 30.3 %all-to-all-start.2 = ((bf16[8,10,96,128]{3,2,1,0:T(8,128)(2,1)}), bf16[8,10,96,128]{3,2,1,0:T(8,128)(2,1)S(1)}, u32[]{:S(2)}, u32[]{:S(2)}) async-start(bf16[8,10,96,128]{3,2,1,0:T(8,128)(2,1)} %analyse.1), calls=%async_computation.2 | async-start | bytes 3932160 | tf_op jit(solution)/shard_map/all_to_all | solution.py:476
  129.6 8.5 %collective-permute-start = (bf16[4,90,16,128]{3,2,1,0:T(8,128)(2,1)}, bf16[4,90,16,128]{3,2,1,0:T(8,128)(2,1)S(1)}, u32[]{:S(2)}, u32[]{:S(2)}) collective-permute-start(bf16[4,90,16,128]{3,2,1,0:T(8,128)(2,1)} %get-tuple-element.30), channel_id=1, source_target_pairs={{0,1},{1,0},{2,3},{3,2},{4,5},{5,4},{6,7},{7,6},{8,9},{9,8},{10,11... | collective-permute-start | bytes 4423688 | tf_op jit(solution)/shard_map/ppermute | solution.py:505
  129.6 34.7 %all-to-all-start.3 = ((bf16[8,10,96,128]{3,2,1,0:T(8,128)(2,1)}), bf16[8,10,96,128]{3,2,1,0:T(8,128)(2,1)S(1)}, u32[]{:S(2)}, u32[]{:S(2)}) async-start(bf16[8,10,96,128]{3,2,1,0:T(8,128)(2,1)} %bitcast.58), calls=%async_computation.3 | async-start | bytes 3932160 | tf_op jit(solution)/shard_map/all_to_all | solution.py:476
  138.1 1.2 copy-start.1
  170.5 50.0 %all-to-all-start.4 = ((bf16[128,30,2,128]{3,2,1,0:T(2,128)(2,1)}), bf16[128,30,2,128]{3,2,1,0:T(2,128)(2,1)S(1)}, u32[]{:S(2)}, u32[]{:S(2)}) async-start(bf16[128,30,2,128]{3,2,1,0:T(2,128)(2,1)} %bitcast.52), calls=%async_computation.4 | async-start | bytes 3932160 | tf_op jit(solution)/shard_map/all_to_all | solution.py:476
  178.9 32.8 %collective-permute-start.1 = (bf16[90,16,128]{2,1,0:T(8,128)(2,1)}, bf16[90,16,128]{2,1,0:T(8,128)(2,1)S(1)}, u32[]{:S(2)}, u32[]{:S(2)}) collective-permute-start(bf16[90,16,128]{2,1,0:T(8,128)(2,1)} %get-tuple-element.38), channel_id=1, source_target_pairs={{0,4},{1,5},{2,6},{3,7},{4,8},{5,9},{6,10},{7,11},{8,12},{9,13},{1... | collective-permute-start | bytes 1105928 | tf_op jit(solution)/shard_map/ppermute | solution.py:510
  180.0 31.6 %collective-permute-start.2 = (bf16[90,16,128]{2,1,0:T(8,128)(2,1)}, bf16[90,16,128]{2,1,0:T(8,128)(2,1)S(1)}, u32[]{:S(2)}, u32[]{:S(2)}) collective-permute-start(bf16[90,16,128]{2,1,0:T(8,128)(2,1)} %get-tuple-element.40), channel_id=1, source_target_pairs={{0,12},{1,13},{2,14},{3,15},{4,0},{5,1},{6,2},{7,3},{8,4},{9,5},{1... | collective-permute-start | bytes 1105928 | tf_op jit(solution)/shard_map/ppermute | solution.py:510
  182.2 37.1 %collective-permute-start.3 = (bf16[90,16,128]{2,1,0:T(8,128)(2,1)}, bf16[90,16,128]{2,1,0:T(8,128)(2,1)}, u32[]{:S(2)}, u32[]{:S(2)}) collective-permute-start(bf16[90,16,128]{2,1,0:T(8,128)(2,1)} %get-tuple-element.39), channel_id=1, source_target_pairs={{0,8},{1,9},{2,10},{3,11},{4,12},{5,13},{6,14},{7,15},{8,0},{9,1},... | collective-permute-start | bytes 1105928 | tf_op jit(solution)/shard_map/ppermute | solution.py:510
  225.0 39.9 %all-to-all-start.5 = ((bf16[16,6,96,128]{3,2,1,0:T(8,128)(2,1)}), bf16[16,6,96,128]{3,2,1,0:T(8,128)(2,1)S(1)}, u32[]{:S(2)}, u32[]{:S(2)}) async-start(bf16[16,6,96,128]{3,2,1,0:T(8,128)(2,1)} %bitcast.49), calls=%async_computation.5 | async-start | bytes 4718592 | tf_op jit(solution)/shard_map/all_to_all | solution.py:476
  229.7 34.4 %collective-permute-start.4 = (bf16[90,8,128]{2,1,0:T(8,128)(2,1)S(1)}, bf16[90,8,128]{2,1,0:T(8,128)(2,1)S(1)}, u32[]{:S(2)}, u32[]{:S(2)}) collective-permute-start(bf16[90,8,128]{2,1,0:T(8,128)(2,1)S(1)} %fusion.9), channel_id=1, source_target_pairs={{0,2},{1,3},{2,0},{3,1},{4,6},{5,7},{6,4},{7,5},{8,10},{9,11},{10,... | collective-permute-start | bytes 552968 | tf_op jit(solution)/shard_map/ppermute | solution.py:524
